TPU v7x, 256 devices: a whole 4x4x8 slice. The times are simulated.
256 devices in a mesh: grp: 4 (over x), dev: 64 (over z, y, core).
Axes of the slice: x: 4, y: 4, z: 8, core: 2. Of those that a mesh axis runs over, the one named last changes fastest.
Arguments:
- token_ids: int32 [1024, 128], P(('grp', 'dev')), may hold values from 0 to 128255, as said below
- sensitivity: bfloat16 [1024, 128, 4096], P(('grp', 'dev')), may hold values from -6 to 6
- last_hidden: bfloat16 [1024, 4096], P(('grp', 'dev')), may hold values from -6 to 6
- lengths: int32 [1024], P(('grp', 'dev')), may hold values from 97 to 128
- norm_gain: float32 [4096], replicated, may hold values from 0.25 to 1.75
- reward_head: float32 [4096], replicated, may hold values from -0.09375 to 0.09375
- chosen_index: int32 [512], replicated, may hold values from 0 to 1023, as said below
- rejected_index: int32 [512], replicated, may hold values from 0 to 1023, as said below
- shard_owner: int32 [256], replicated, may hold values from 0 to 255, each once
Outputs:
- owned_grad: bfloat16 [128256, 4096], P(('grp', 'dev'))
- head_grad: float32 [4096], P(('grp', 'dev'))
Inputs may be any that keep to these rules, and one draw needn't show every extreme that they name: `token_ids`: within the token slots of one device, at most 4 ids fall in any one vocabulary shard of 501 rows, and on every device some shard gets exactly 4. chosen_index and rejected_index together name every response exactly once. `rejected_index`: see chosen_index.
All inputs are finite; a program needn't handle non-finite values.
Results may differ from a plain program's by a relative error of at most 0.0042.
Values may be sent and summed in bfloat16 or wider, within the bound.
No kernel may reach another device: no remote copies, remote signals or barrier semaphores. Data moves between devices by JAX's collectives and lax.ppermute only.
A program may use at most 64 MiB of HBM per device.

v0:
```python
import jax
import jax.numpy as jnp
from jax import lax
from jax.sharding import Mesh
from jax.sharding import PartitionSpec as P

VOCAB = 128256
DEV = ("dev_0", "dev_1", "dev_2")
GRP_DEV = ("grp", "dev_0", "dev_1", "dev_2")


def from_everyone(array, axis):
    copies = jnp.broadcast_to(array, (lax.axis_size(axis), *array.shape))
    return lax.all_to_all(copies, axis, split_axis=0, concat_axis=0, tiled=True)


def in_order(parts, dim):
    parts = jnp.moveaxis(parts, 0, dim)
    lengths = parts.shape
    return parts.reshape(*lengths[:dim], lengths[dim] * lengths[dim + 1], *lengths[dim + 2 :])


def gathered_by_axis(array, axes, dim):
    far, near = axes
    first = from_everyone(array, far)
    parts = jnp.swapaxes(from_everyone(first, near), 0, 1)
    return in_order(parts.reshape(-1, *array.shape), dim)


def split_up(array, dim, count):
    lengths = array.shape
    parts = array.reshape(*lengths[:dim], count, lengths[dim] // count, *lengths[dim + 1 :])
    return jnp.moveaxis(parts, dim, 0)


def sent_and_summed(array, axis, dim):
    parts = split_up(array, dim, lax.axis_size(axis))
    arrived = lax.all_to_all(parts, axis, split_axis=0, concat_axis=0, tiled=True)
    return arrived.sum(axis=0)


def sum_by_axis(array, axes, dim):
    far, near = axes
    own = sent_and_summed(split_up(array, dim, lax.axis_size(far)), near, dim + 1)
    return jnp.sum(lax.all_to_all(own, far, 0, 0, tiled=True), axis=0)


def one_exchange(array, axis, axes, splits, concats):
    sizes = [lax.axis_size(a) for a in axes]
    parts = split_up(array, splits[0], sizes[0])
    parts = jnp.moveaxis(split_up(parts, splits[1] + 1, sizes[1]), 0, 1)
    inside = parts.shape[2:]
    parts = parts.reshape(-1, *inside)
    parts = lax.all_to_all(parts, axis, split_axis=0, concat_axis=0, tiled=True)
    parts = in_order(parts.reshape(*sizes, *inside), concats[0] + 1)
    return in_order(parts, concats[1])


def local(
    token_ids,
    sensitivity,
    last_hidden,
    lengths,
    norm_gain,
    reward_head,
    chosen_index,
    rejected_index,
    shard_owner,
):
    resp_local, block_len = token_ids.shape
    width = sensitivity.shape[2]
    tok_local = resp_local * block_len
    n_grp = lax.axis_size("grp")
    n_dev = lax.axis_size(DEV)
    devices = shard_owner.shape[0]
    shard_rows = VOCAB // devices
    capacity = max(2, (2 * tok_local + devices - 1) // devices)
    hidden = last_hidden.astype(jnp.float32)
    normed = (
        hidden / jnp.sqrt(jnp.mean(hidden * hidden, axis=-1, keepdims=True) + 1e-05) * norm_gain
    )
    own_reward = jnp.sum(normed * reward_head, axis=-1)
    reward = gathered_by_axis(own_reward, (("grp", "dev_0"), ("dev_1", "dev_2")), 0)
    margin = reward[chosen_index] - reward[rejected_index]
    push = -jax.nn.sigmoid(-margin)
    mine = lax.axis_index(GRP_DEV) * resp_local + jnp.arange(resp_local, dtype=jnp.int32)
    sign_table = (chosen_index[None, :] == mine[:, None]).astype(jnp.float32) - (
        rejected_index[None, :] == mine[:, None]
    ).astype(jnp.float32)
    reward_grad = jnp.sum(sign_table * push[None, :], axis=1)
    head_grad = sum_by_axis(
        jnp.sum(reward_grad[:, None] * normed, axis=0), (("grp", "dev_0"), ("dev_1", "dev_2")), 0
    )
    positions = jnp.arange(block_len, dtype=jnp.int32)
    scale = jnp.where(positions[None, :] < lengths[:, None], reward_grad[:, None], jnp.float32(0.0))
    grad_rows = (scale[:, :, None] * sensitivity).astype(jnp.bfloat16).reshape(tok_local, width)
    ids = token_ids.reshape(tok_local)
    shard_of = ids // shard_rows
    offset = ids - shard_of * shard_rows
    owner = shard_owner[shard_of]
    owner_hot = (owner[:, None] == jnp.arange(devices, dtype=jnp.int32)[None, :]).astype(
        jnp.bfloat16
    )
    token_pos = jnp.arange(tok_local, dtype=jnp.int32)
    earlier = (token_pos[:, None] > token_pos[None, :]).astype(jnp.bfloat16)
    before = jnp.dot(earlier, owner_hot, preferred_element_type=jnp.float32)
    rank = jnp.sum(before * owner_hot.astype(jnp.float32), axis=1).astype(jnp.int32)
    slot = owner * capacity + rank
    slot_match = slot[None, :] == jnp.arange(devices * capacity, dtype=jnp.int32)[:, None]
    outgoing = jnp.dot(
        slot_match.astype(jnp.bfloat16), grad_rows, preferred_element_type=jnp.float32
    ).astype(jnp.bfloat16)
    outgoing = outgoing.reshape(n_grp, n_dev, capacity, width)
    targets = jnp.sum(jnp.where(slot_match, offset[None, :] + 1, 0), axis=1) - 1
    targets = targets.reshape(n_grp, n_dev, capacity)
    arrived, arrived_rows = (
        one_exchange(outgoing, GRP_DEV, ("grp", DEV), (0, 1), (0, 1)),
        one_exchange(targets, GRP_DEV, ("grp", DEV), (0, 1), (0, 1)),
    )
    arrived = arrived.reshape(devices * capacity, width)
    arrived_rows = arrived_rows.reshape(devices * capacity)
    placing = (arrived_rows[None, :] == jnp.arange(shard_rows, dtype=jnp.int32)[:, None]).astype(
        jnp.bfloat16
    )
    owned = jnp.dot(placing, arrived, preferred_element_type=jnp.float32).astype(jnp.bfloat16)
    return (owned, head_grad)


def solution(mesh):
    torus = Mesh(
        mesh.devices.reshape(mesh.shape["grp"], 8, 4, 2), ("grp", "dev_0", "dev_1", "dev_2")
    )
    placed = (
        P(GRP_DEV, None),
        P(GRP_DEV, None, None),
        P(GRP_DEV, None),
        P(GRP_DEV),
        P(),
        P(),
        P(),
        P(),
        P(),
    )
    return jax.shard_map(
        local,
        mesh=torus,
        in_specs=placed,
        out_specs=(P(GRP_DEV, None), P(GRP_DEV)),
        check_vma=False,
    )
```

profile of v0, /device:TPU:1, one launch (start us, length us, event | category | flops | bytes accessed | tf_op | source)
XLA Modules:
  0.0 324.1 jit_solution(8315797660243638519)
XLA Ops:
  0.6 0.0 copy-start
  0.7 0.9 fusion.6
  1.6 1.0 multiply_reduce_fusion.1
  2.6 0.6 broadcast_in_dim.30
  3.3 11.9 %all-to-all-start.1 = ((f32[32,1,4]{2,1,0:T(1,128)}), f32[32,1,4]{2,1,0:T(1,128)S(1)}, u32[]{:S(2)}, u32[]{:S(2)}) async-start(f32[32,1,4]{2,1,0:T(1,128)} %broadcast_in_dim.30), calls=%async_computation.1 | async-start | bytes 32768 | tf_op jit(solution)/shard_map/all_to_all | solution.py:14
  15.1 0.7 fusion.13
  15.8 0.7 broadcast_divide_fusion
  16.5 0.7 compare_select_fusion.2
  17.2 0.7 compare_select_fusion.1
  17.9 3.5 %gather_fusion = s32[512]{0:T(512)S(1)} fusion(s32[256]{0:T(256)S(1)} %copy-done, s32[1024]{0:T(1024)S(1)} %pad_clamp_fusion.2), kind=kCustom, calls=%fused_computation | custom fusion | bytes 6144 | tf_op jit(solution)/shard_map/gather | solution.py:100
  21.5 0.4 fusion
  21.8 0.7 fusion.9
  22.5 0.3 select_reduce_fusion
  22.9 0.8 all-to-all-done.1
  23.7 0.1 copy.25
  23.8 0.7 reshape.230
  24.5 6.6 %all-to-all-start.2 = ((f32[8,1,128]{2,1,0:T(1,128)}), f32[8,1,128]{2,1,0:T(1,128)S(1)}, u32[]{:S(2)}, u32[]{:S(2)}) async-start(f32[8,1,128]{2,1,0:T(1,128)} %reshape.230), calls=%async_computation.2 | async-start | bytes 8192 | tf_op jit(solution)/shard_map/all_to_all | solution.py:14
  31.0 0.8 sub.35
  31.8 3.8 %all-to-all-done.2 = f32[8,1,128]{2,1,0:T(1,128)S(1)} async-done(((f32[8,1,128]{2,1,0:T(1,128)}), f32[8,1,128]{2,1,0:T(1,128)S(1)}, u32[]{:S(2)}, u32[]{:S(2)}) %all-to-all-start.2) | async-done | bytes 4128 | tf_op jit(solution)/shard_map/all_to_all | solution.py:14
  35.6 0.5 broadcast.207
  36.1 0.7 reduce.1
  36.8 0.1 reshape.231
  36.9 0.1 copy.26
  37.0 0.1 reshape_reshape.9
  37.1 2.3 gather_fusion.2
  39.4 2.3 gather_fusion.1
  41.8 0.2 multiply_reduce_fusion.2
  42.0 0.1 multiply_reduce_fusion
  42.1 0.1 fusion.11
  42.2 0.1 reshape_reshape.11
  42.3 0.1 copy.28
  42.4 0.7 reshape.232
  43.1 3.9 %all-to-all-start.4 = ((f32[8,1,512]{2,1,0:T(1,128)}), f32[8,1,512]{2,1,0:T(1,128)S(1)}, u32[]{:S(2)}, u32[]{:S(2)}) async-start(f32[8,1,512]{2,1,0:T(1,128)} %reshape.232), calls=%async_computation.4 | async-start | bytes 32768 | tf_op jit(solution)/shard_map/all_to_all | solution.py:38
  47.0 5.6 %multiply_convert_fusion = bf16[4,128,4096]{2,1,0:T(8,128)(2,1)} fusion(bf16[4,128,4096]{2,1,0:T(8,128)(2,1)} %param.10, f32[4,128]{1,0:T(4,128)S(1)} %fusion.11), kind=kLoop, calls=%fused_computation.3 | loop fusion | flops 6291456 | bytes 8390656 | tf_op jit(solution)/shard_map/convert_element_type | solution.py:96
  52.5 11.0 %all-to-all-start = ((s32[256,1,1,4]{3,2,1,0:T(1,128)}), s32[256,1,1,4]{3,2,1,0:T(1,128)S(1)}, u32[]{:S(2)}, u32[]{:S(2)}) async-start(s32[256,1,1,4]{3,2,1,0:T(1,128)} %bitcast.3), calls=%async_computation | async-start | bytes 262144 | tf_op jit(solution)/shard_map/all_to_all | solution.py:54
  63.6 0.7 reduce.2
  64.3 0.1 reshape.233
  64.4 0.7 copy.29
  65.0 11.3 %all-to-all-done = s32[256,1,1,4]{3,2,1,0:T(1,128)S(1)} async-done(((s32[256,1,1,4]{3,2,1,0:T(1,128)}), s32[256,1,1,4]{3,2,1,0:T(1,128)S(1)}, u32[]{:S(2)}, u32[]{:S(2)}) %all-to-all-start) | async-done | bytes 4128 | tf_op jit(solution)/shard_map/all_to_all | solution.py:54
  76.3 3.8 %all-to-all-start.5 = ((f32[32,1,16]{2,1,0:T(1,128)}), f32[32,1,16]{2,1,0:T(1,128)S(1)}, u32[]{:S(2)}, u32[]{:S(2)}) async-start(f32[32,1,16]{2,1,0:T(1,128)} %copy.29), calls=%async_computation.5 | async-start | bytes 32768 | tf_op jit(solution)/shard_map/all_to_all | solution.py:45
  80.1 8.9 %convolution_convert_fusion = bf16[1024,4096]{1,0:T(8,128)(2,1)} fusion(bf16[512,4096]{1,0:T(8,128)(2,1)} %bitcast.67, s32[512]{0:T(512)S(1)} %get-tuple-element.5), kind=kOutput, calls=%fused_computation.4 | convolution fusion | flops 4299685888 | bytes 12584960 | tf_op jit(solution)/shard_map/dot_general | solution.py:110
  89.0 13.1 %reshape_transpose_transpose_reshape_reshape_reshape.4 = bf16[256,1,1,4,4096]{4,3,0,2,1:T(4,128)(2,1)} reshape(bf16[1024,4096]{1,0:T(8,128)(2,1)} %convolution_convert_fusion) | data formatting | bytes 16777216 | tf_op jit(solution)/shard_map/reshape;transpose;transpose;reshape;reshape;reshape | solution.py:53
  102.1 12.6 %all-to-all-start.3 = ((bf16[256,1,1,4,4096]{4,3,2,1,0:T(4,128)(2,1)}), bf16[256,1,1,4,4096]{4,3,2,1,0:T(4,128)(2,1)}, u32[]{:S(2)}, u32[]{:S(2)}) async-start(bf16[256,1,1,4,4096]{4,3,2,1,0:T(4,128)(2,1)} %bitcast.66), calls=%async_computation.3 | async-start | bytes 16777216 | tf_op jit(solution)/shard_map/all_to_all | solution.py:54
  114.6 0.1 eq.71
  114.8 0.6 reduce_sum.79
  115.3 186.9 %all-to-all-done.3 = bf16[256,1,1,4,4096]{4,3,2,1,0:T(4,128)(2,1)} async-done(((bf16[256,1,1,4,4096]{4,3,2,1,0:T(4,128)(2,1)}), bf16[256,1,1,4,4096]{4,3,2,1,0:T(4,128)(2,1)}, u32[]{:S(2)}, u32[]{:S(2)}) %all-to-all-start.3) | async-done | bytes 8388640 | tf_op jit(solution)/shard_map/all_to_all | solution.py:54
  302.2 12.5 %reshape_reshape.10 = bf16[1024,4096]{1,0:T(8,128)(2,1)} reshape(bf16[4,64,1,4,4096]{4,3,1,0,2:T(4,128)(2,1)} %bitcast.15) | data formatting | bytes 16777216 | tf_op jit(solution)/shard_map/reshape;reshape | solution.py:120
  314.7 9.4 %convolution_convert_fusion.1 = bf16[501,4096]{1,0:T(8,128)(2,1)} fusion(bf16[1024,4096]{1,0:T(8,128)(2,1)} %reshape_reshape.10, s32[1024]{0:T(1024)S(1)} %eq.71), kind=kOutput, calls=%fused_computation.5 | convolution fusion | flops 4205257728 | bytes 12496896 | tf_op jit(solution)/shard_map/dot_general | solution.py:125
  (20 shorter events, 0.1 us)
Async XLA Ops:
  0.6 17.3 %copy-start = (s32[256]{0:T(256)S(1)}, s32[256]{0:T(256)}, u32[]{:S(2)}) copy-start(s32[256]{0:T(256)} %param.17) | copy-start | bytes 3076
  0.6 41.1 %copy-start.1 = (s32[512]{0:T(512)S(1)}, s32[512]{0:T(512)}, u32[]{:S(2)}) copy-start(s32[512]{0:T(512)} %param.15) | copy-start | bytes 6148
  0.7 41.1 %copy-start.2 = (s32[512]{0:T(512)S(1)}, s32[512]{0:T(512)}, u32[]{:S(2)}) copy-start(s32[512]{0:T(512)} %param.16) | copy-start | bytes 6148
  0.7 41.4 %copy-start.3 = (s32[4]{0:T(128)S(1)}, s32[4]{0:T(128)}, u32[]{:S(2)}) copy-start(s32[4]{0:T(128)} %param.12) | copy-start | bytes 52
  3.3 20.4 %all-to-all-start.1 = ((f32[32,1,4]{2,1,0:T(1,128)}), f32[32,1,4]{2,1,0:T(1,128)S(1)}, u32[]{:S(2)}, u32[]{:S(2)}) async-start(f32[32,1,4]{2,1,0:T(1,128)} %broadcast_in_dim.30), calls=%async_computation.1 | async-start | bytes 32768 | tf_op jit(solution)/shard_map/all_to_all | solution.py:14
  24.5 11.1 %all-to-all-start.2 = ((f32[8,1,128]{2,1,0:T(1,128)}), f32[8,1,128]{2,1,0:T(1,128)S(1)}, u32[]{:S(2)}, u32[]{:S(2)}) async-start(f32[8,1,128]{2,1,0:T(1,128)} %reshape.230), calls=%async_computation.2 | async-start | bytes 8192 | tf_op jit(solution)/shard_map/all_to_all | solution.py:14
  43.1 9.5 %all-to-all-start.4 = ((f32[8,1,512]{2,1,0:T(1,128)}), f32[8,1,512]{2,1,0:T(1,128)S(1)}, u32[]{:S(2)}, u32[]{:S(2)}) async-start(f32[8,1,512]{2,1,0:T(1,128)} %reshape.232), calls=%async_computation.4 | async-start | bytes 32768 | tf_op jit(solution)/shard_map/all_to_all | solution.py:38
  52.5 23.8 %all-to-all-start = ((s32[256,1,1,4]{3,2,1,0:T(1,128)}), s32[256,1,1,4]{3,2,1,0:T(1,128)S(1)}, u32[]{:S(2)}, u32[]{:S(2)}) async-start(s32[256,1,1,4]{3,2,1,0:T(1,128)} %bitcast.3), calls=%async_computation | async-start | bytes 262144 | tf_op jit(solution)/shard_map/all_to_all | solution.py:54
  76.3 25.7 %all-to-all-start.5 = ((f32[32,1,16]{2,1,0:T(1,128)}), f32[32,1,16]{2,1,0:T(1,128)S(1)}, u32[]{:S(2)}, u32[]{:S(2)}) async-start(f32[32,1,16]{2,1,0:T(1,128)} %copy.29), calls=%async_computation.5 | async-start | bytes 32768 | tf_op jit(solution)/shard_map/all_to_all | solution.py:45
  102.1 200.1 %all-to-all-start.3 = ((bf16[256,1,1,4,4096]{4,3,2,1,0:T(4,128)(2,1)}), bf16[256,1,1,4,4096]{4,3,2,1,0:T(4,128)(2,1)}, u32[]{:S(2)}, u32[]{:S(2)}) async-start(bf16[256,1,1,4,4096]{4,3,2,1,0:T(4,128)(2,1)} %bitcast.66), calls=%async_computation.3 | async-start | bytes 16777216 | tf_op jit(solution)/shard_map/all_to_all | solution.py:54
where the time goes:
time: 325 us; the launch traced here: 324 us
  waiting for transfers between devices  203 us (62%)
  starting transfers between devices  49.7 us (15%)
  local copies, waits for them, and re-layouts  38.5 us (12%)
  matrix products  18.6 us (6%)
  other arithmetic  13.6 us (4%)
    all_to_all x2, waiting for transfers between devices, one_exchange(): parts = lax.all_to_all(parts, axis, split_axis=0, concat_axis=0, tiled=True)  198 us
    all_to_all x2, starting transfers between devices, one_exchange(): parts = lax.all_to_all(parts, axis, split_axis=0, concat_axis=0, tiled=True)  23.6 us
    all_to_all x2, starting transfers between devices, from_everyone(): return lax.all_to_all(copies, axis, split_axis=0, concat_axis=0, tiled=True)  18.4 us
    another operation x1, local copies, waits for them, and re-layouts, one_exchange(): parts = parts.reshape(-1, *inside)  13.1 us
    another operation x1, local copies, waits for them, and re-layouts, local(): arrived = arrived.reshape(devices * capacity, width)  12.5 us
    dot_general x1, matrix products, local(): jnp.dot(placing, arrived, preferred_element_type=jnp.float32)  9.36 us
    dot_general x1, matrix products, local(): jnp.dot(slot_match.astype(jnp.bfloat16), grad_rows, preferred_element_typ...  8.86 us
  transfers between devices with their start and end apart: 6, of which 4 were waited for; matrix products, arithmetic and copies ran while one was open for 12% of the time, Pallas kernels for 0%

commit v1 on v0

v1 whole, which is shorter than its diff:
```python
import jax
import jax.numpy as jnp
from jax import lax
from jax.experimental import pallas as pl
from jax.experimental.pallas import tpu as pltpu
from jax.sharding import Mesh
from jax.sharding import PartitionSpec as P

VOCAB = 128256
CAP = 4
GRP_DEV = ("grp", "dev_0", "dev_1", "dev_2")


def pack_kernel(slot_ref, rows_ref, out_ref):
    slots, cap, width = out_ref.shape
    tokens = slot_ref.shape[1]
    hot = jax.lax.broadcasted_iota(jnp.int32, (slots * cap, tokens), 0) == slot_ref[...]
    picked = jnp.dot(
        hot.astype(jnp.bfloat16), rows_ref[...], preferred_element_type=jnp.float32
    )
    out_ref[...] = picked.reshape(slots, cap, width).astype(jnp.bfloat16)


def packed_rows(slot, rows, devices, block):
    tokens, width = rows.shape
    return pl.pallas_call(
        pack_kernel,
        out_shape=jax.ShapeDtypeStruct((devices, CAP, width), jnp.bfloat16),
        grid=(width // block,),
        in_specs=[
            pl.BlockSpec((1, tokens), lambda j: (0, 0)),
            pl.BlockSpec((tokens, block), lambda j: (0, j)),
        ],
        out_specs=pl.BlockSpec((devices, CAP, block), lambda j: (0, 0, j)),
        compiler_params=pltpu.CompilerParams(vmem_limit_bytes=48 << 20),
        cost_estimate=pl.CostEstimate(
            flops=2 * devices * CAP * tokens * width,
            bytes_accessed=2 * (tokens + devices * CAP) * width,
            transcendentals=0,
        ),
    )(slot, rows)


def place_kernel(target_ref, scale_ref, rows_ref, out_ref):
    slots, cap, width = rows_ref.shape
    rows = rows_ref[...].astype(jnp.float32).reshape(slots * cap, width)
    scaled = (scale_ref[...] * rows).astype(jnp.bfloat16)
    hot = jax.lax.broadcasted_iota(jnp.int32, (out_ref.shape[0], slots * cap), 0) == target_ref[...]
    out_ref[...] = jnp.dot(
        hot.astype(jnp.bfloat16), scaled, preferred_element_type=jnp.float32
    ).astype(jnp.bfloat16)


def placed_rows(target, scale, rows, shard_rows, block):
    devices, cap, width = rows.shape
    return pl.pallas_call(
        place_kernel,
        out_shape=jax.ShapeDtypeStruct((shard_rows, width), jnp.bfloat16),
        grid=(width // block,),
        in_specs=[
            pl.BlockSpec((1, devices * cap), lambda j: (0, 0)),
            pl.BlockSpec((devices * cap, 1), lambda j: (0, 0)),
            pl.BlockSpec((devices, cap, block), lambda j: (0, 0, j)),
        ],
        out_specs=pl.BlockSpec((shard_rows, block), lambda j: (0, j)),
        compiler_params=pltpu.CompilerParams(vmem_limit_bytes=48 << 20),
        cost_estimate=pl.CostEstimate(
            flops=2 * shard_rows * devices * cap * width,
            bytes_accessed=2 * (shard_rows + devices * cap) * width,
            transcendentals=0,
        ),
    )(target, scale, rows)


def local(
    token_ids,
    sensitivity,
    last_hidden,
    lengths,
    norm_gain,
    reward_head,
    chosen_index,
    rejected_index,
    shard_owner,
):
    resp_local, block_len = token_ids.shape
    width = sensitivity.shape[2]
    tok_local = resp_local * block_len
    devices = shard_owner.shape[0]
    shard_rows = VOCAB // devices
    responses = devices * resp_local

    own_place = lax.axis_index(GRP_DEV)
    cols = width // devices

    ids = token_ids.reshape(tok_local)
    shard_of = ids // shard_rows
    offset = ids - shard_of * shard_rows
    shard_hot = shard_of[:, None] == jnp.arange(devices, dtype=jnp.int32)[None, :]
    owner = jnp.sum(jnp.where(shard_hot, shard_owner[None, :], 0), axis=1)
    token_pos = jnp.arange(tok_local, dtype=jnp.int32)
    earlier = (token_pos[None, :] < token_pos[:, None]) & (shard_of[None, :] == shard_of[:, None])
    rank = jnp.sum(earlier.astype(jnp.int32), axis=1)
    slot = owner * CAP + rank

    live = (jnp.arange(block_len, dtype=jnp.int32)[None, :] < lengths[:, None]).reshape(tok_local)
    code = jnp.where(live, (offset + 1) * resp_local + token_pos // block_len, 0)
    hidden = last_hidden.astype(jnp.float32)
    norm = jnp.sqrt(jnp.mean(hidden * hidden, axis=-1, keepdims=True) + 1e-05)
    own_reward = jnp.sum(hidden / norm * norm_gain * reward_head, axis=-1)
    slot_match = slot[None, :] == jnp.arange(devices * CAP, dtype=jnp.int32)[:, None]
    codes = jnp.sum(jnp.where(slot_match, code[None, :], 0), axis=1).reshape(devices, CAP)
    own_facts = jnp.concatenate([own_reward, norm[:, 0], jnp.zeros((52,), jnp.float32)])
    message = jnp.concatenate(
        [
            codes.astype(jnp.float32),
            jnp.broadcast_to(own_facts[None, :], (devices, 60)),
            hidden.reshape(resp_local, devices, cols).swapaxes(0, 1).reshape(devices, -1),
        ],
        axis=1,
    )
    heard = lax.all_to_all(message, GRP_DEV, split_axis=0, concat_axis=0, tiled=True)
    outgoing = packed_rows(slot[None, :], sensitivity.reshape(tok_local, width), devices, 512)
    arrived = lax.all_to_all(outgoing, GRP_DEV, split_axis=0, concat_axis=0, tiled=True)

    arrived_code = heard[:, :CAP].astype(jnp.int32)
    reward = heard[:, 4:8].reshape(responses)
    margin = reward[chosen_index] - reward[rejected_index]
    push = -jax.nn.sigmoid(-margin)
    every = jnp.arange(responses, dtype=jnp.int32)
    sign_table = (chosen_index[None, :] == every[:, None]).astype(jnp.float32) - (
        rejected_index[None, :] == every[:, None]
    ).astype(jnp.float32)
    reward_grad = jnp.sum(sign_table * push[None, :], axis=1).reshape(devices, resp_local)
    own_gain = lax.dynamic_slice(norm_gain, (own_place * cols,), (cols,))
    head_grad = jnp.zeros((cols,), jnp.float32)
    for r in range(resp_local):
        normed = heard[:, 64 + r * cols : 64 + (r + 1) * cols] / heard[:, 8 + r : 9 + r] * own_gain
        head_grad += jnp.sum(reward_grad[:, r : r + 1] * normed, axis=0)

    response_in = arrived_code % resp_local
    scale = jnp.zeros(arrived_code.shape, jnp.float32)
    for r in range(resp_local):
        scale = jnp.where(response_in == r, reward_grad[:, r : r + 1], scale)
    target = arrived_code // resp_local - 1
    scale = jnp.where(target >= 0, scale, 0.0)
    owned = placed_rows(
        target.reshape(1, devices * CAP), scale.reshape(devices * CAP, 1), arrived, shard_rows, 512
    )
    return (owned, head_grad)


def solution(mesh):
    torus = Mesh(
        mesh.devices.reshape(mesh.shape["grp"], 8, 4, 2), ("grp", "dev_0", "dev_1", "dev_2")
    )
    placed = (
        P(GRP_DEV, None),
        P(GRP_DEV, None, None),
        P(GRP_DEV, None),
        P(GRP_DEV),
        P(),
        P(),
        P(),
        P(),
        P(),
    )
    return jax.shard_map(
        local,
        mesh=torus,
        in_specs=placed,
        out_specs=(P(GRP_DEV, None), P(GRP_DEV)),
        check_vma=False,
    )
```

time: 325 us -> 247 us (0.76)
  local copies, waits for them, and re-layouts: 38.5 us -> 11 us
  waiting for transfers between devices: 203 us -> 181 us
  starting transfers between devices: 49.7 us -> 28.2 us
  Pallas kernels: 0 us -> 19 us
  matrix products: 18.6 us -> 0 us
  other arithmetic: 13.6 us -> 5.67 us
    another operation x4 -> x0, local copies, waits for them, and re-layouts: 25.8 us -> none  [the longest x1 13.1 us: one_exchange(): parts = parts.reshape(-1, *inside)]
    all_to_all x6 -> x2, starting transfers between devices: 49.7 us -> 28.2 us  [the longest x1 15.7 us: local(): lax.all_to_all(message, GRP_DEV, split_axis=0, concat_axis=0, tiled=True)]
    all_to_all x6 -> x2, waiting for transfers between devices: 203 us -> 181 us  [the longest x1 179 us: local(): lax.all_to_all(outgoing, GRP_DEV, split_axis=0, concat_axis=0, tiled=True)]
    pallas_call x0 -> x2, Pallas kernels: none -> 19 us  [the longest x1 10.6 us: placed_rows(): pl.pallas_call(place_kernel, out_shape=jax.ShapeDtypeStruct((shard_rows,...]
    dot_general x3 -> x0, matrix products: 18.6 us -> none  [the longest x1 9.36 us: local(): jnp.dot(placing, arrived, preferred_element_type=jnp.float32)]
    convert_element_type x1, other arithmetic: 5.57 us -> 0.01 us  [local(): codes.astype(jnp.float32)]
    gather x1 -> x0, local copies, waits for them, and re-layouts: 3.52 us -> none  [local(): owner = shard_owner[shard_of]]
  transfers between devices with their start and end apart: 6 -> 2, of which waited for: 4 -> 2; matrix products, arithmetic and copies ran while one was open for 12% -> 3% of each run, Pallas kernels for 0% -> 3%
where the time goes in v1:
time: 247 us; the launch traced here: 246 us
  waiting for transfers between devices  181 us (73%)
  starting transfers between devices  28.2 us (11%)
  Pallas kernels  19 us (8%)
  local copies, waits for them, and re-layouts  11 us (4%)
  other arithmetic  5.67 us (2%)
    all_to_all x1, waiting for transfers between devices, local(): lax.all_to_all(outgoing, GRP_DEV, split_axis=0, concat_axis=0, tiled=True)  179 us
    all_to_all x1, starting transfers between devices, local(): lax.all_to_all(message, GRP_DEV, split_axis=0, concat_axis=0, tiled=True)  15.7 us
    all_to_all x1, starting transfers between devices, local(): lax.all_to_all(outgoing, GRP_DEV, split_axis=0, concat_axis=0, tiled=True)  12.6 us
    pallas_call x1, Pallas kernels, placed_rows(): pl.pallas_call(place_kernel, out_shape=jax.ShapeDtypeStruct((shard_rows,...  10.6 us
    pallas_call x1, Pallas kernels, packed_rows(): pl.pallas_call(pack_kernel, out_shape=jax.ShapeDtypeStruct((devices, CAP,...  8.43 us
  transfers between devices with their start and end apart: 2, of which 2 were waited for; matrix products, arithmetic and copies ran while one was open for 3% of the time, Pallas kernels for 3%

profile of v1, /device:TPU:1, one launch (start us, length us, event | category | flops | bytes accessed | tf_op | source)
XLA Modules:
  0.0 246.3 jit_solution(14387412218142059966)
XLA Ops:
  0.6 0.9 multiply_reduce_fusion.2
  1.5 1.0 reshape.153
  2.5 0.8 add_select_fusion.3
  3.3 0.2 convert_reduce_fusion
  3.5 0.9 select_reduce_fusion.1
  4.5 0.3 select_reduce_fusion
  4.8 0.1 convert_element_type.23
  4.9 0.1 copy.27
  5.0 0.2 copy.26
  5.1 1.0 multiply_reduce_fusion.1
  6.2 0.1 pad_maximum_fusion
  6.3 0.1 maximum_bitcast_fusion
  6.3 0.8 copy.28
  7.1 15.7 %all-to-all-start = ((f32[256,1,128]{2,1,0:T(1,128)}), f32[256,1,128]{2,1,0:T(1,128)S(1)}, u32[]{:S(2)}, u32[]{:S(2)}) async-start(f32[256,1,128]{2,1,0:T(1,128)} %copy.28), calls=%async_computation | async-start | bytes 262144 | tf_op jit(solution)/shard_map/all_to_all | solution.py:122
  22.8 0.0 copy-start
  22.8 2.2 copy-done
  25.0 8.4 %shard_map.104 = bf16[256,4,4096]{2,1,0:T(4,128)(2,1)} custom-call(s32[1,512]{1,0:T(1,128)S(1)} %bitcast.38, bf16[512,4096]{1,0:T(8,128)(2,1)S(1)} %bitcast.39), custom_call_target="tpu_custom_call" | custom-call | flops 4294967296 | bytes 12582912 | tf_op jit(solution)/shard_map/pallas_call | solution.py:26
  33.4 0.0 copy-start.1
  33.4 0.0 copy-start.2
  33.4 2.2 all-to-all-done
  35.5 12.6 %all-to-all-start.1 = ((bf16[256,4,4096]{2,1,0:T(4,128)(2,1)}), bf16[256,4,4096]{2,1,0:T(4,128)(2,1)}, u32[]{:S(2)}, u32[]{:S(2)}) async-start(bf16[256,4,4096]{2,1,0:T(4,128)(2,1)} %shard_map.104), calls=%async_computation.1 | async-start | bytes 16777216 | tf_op jit(solution)/shard_map/all_to_all | solution.py:124
  48.1 0.8 dynamic_slice.3
  48.9 0.0 copy-done.1
  48.9 0.0 copy-done.2
  49.0 0.1 copy.29
  49.1 0.1 copy.31
  49.2 0.1 reshape.156
  49.3 2.3 gather_fusion.1
  51.6 2.3 gather_fusion
  53.9 0.6 multiply_reduce_fusion
  54.5 0.1 reshape.157
  54.6 0.3 slice_reduce_fusion.3
  55.0 0.1 copy.32
  55.2 0.1 copy.30
  55.3 0.1 reshape.155.target_ref
  55.4 0.2 reshape.178.scale_ref
  55.6 0.2 fusion.10
  55.9 0.5 add_add_fusion
  56.4 179.3 %all-to-all-done.1.rows_ref = bf16[256,4,4096]{2,1,0:T(4,128)(2,1)} async-done(((bf16[256,4,4096]{2,1,0:T(4,128)(2,1)}), bf16[256,4,4096]{2,1,0:T(4,128)(2,1)}, u32[]{:S(2)}, u32[]{:S(2)}) %all-to-all-start.1) | async-done | bytes 8388640 | tf_op jit(solution)/shard_map/all_to_all | solution.py:124
  235.7 10.6 %shard_map.105 = bf16[501,4096]{1,0:T(8,128)(2,1)} custom-call(s32[1,1024]{1,0:T(1,128)S(1)} %reshape.155.target_ref, f32[1024,1]{1,0:T(8,128)S(1)} %reshape.178.scale_ref, bf16[256,4,4096]{2,1,0:T(4,128)(2,1)} %all-to-all-done.1.rows_ref), custom_call_target="tpu_custom_call" | custom-call | flops 4202692608 | bytes 12492800 | tf_op jit(solution)/shard_map/pallas_call | solution.py:56
  (12 shorter events, 0.1 us)
Async XLA Ops:
  7.1 28.4 %all-to-all-start = ((f32[256,1,128]{2,1,0:T(1,128)}), f32[256,1,128]{2,1,0:T(1,128)S(1)}, u32[]{:S(2)}, u32[]{:S(2)}) async-start(f32[256,1,128]{2,1,0:T(1,128)} %copy.28), calls=%async_computation | async-start | bytes 262144 | tf_op jit(solution)/shard_map/all_to_all | solution.py:122
  22.8 2.2 copy-start
  33.4 15.5 %copy-start.1 = (s32[512]{0:T(512)S(1)}, s32[512]{0:T(512)}, u32[]{:S(2)}) copy-start(s32[512]{0:T(512)} %param.15) | copy-start | bytes 6148
  33.4 15.5 %copy-start.2 = (s32[512]{0:T(512)S(1)}, s32[512]{0:T(512)}, u32[]{:S(2)}) copy-start(s32[512]{0:T(512)} %param.16) | copy-start | bytes 6148
  35.5 200.2 %all-to-all-start.1 = ((bf16[256,4,4096]{2,1,0:T(4,128)(2,1)}), bf16[256,4,4096]{2,1,0:T(4,128)(2,1)}, u32[]{:S(2)}, u32[]{:S(2)}) async-start(bf16[256,4,4096]{2,1,0:T(4,128)(2,1)} %shard_map.104), calls=%async_computation.1 | async-start | bytes 16777216 | tf_op jit(solution)/shard_map/all_to_all | solution.py:124

commit v2 on v1

v2 whole, which is shorter than its diff:
```python
import functools

import jax
import jax.numpy as jnp
from jax import lax
from jax.experimental import pallas as pl
from jax.experimental.pallas import tpu as pltpu
from jax.sharding import Mesh
from jax.sharding import PartitionSpec as P

VOCAB = 128256
CAP = 4
GRP_DEV = ("grp", "dev_0", "dev_1", "dev_2")
PLANE = ("grp", "dev_1", "dev_2")
RING = 8
COLUMNS = 32
ROWS = 88
BLOCK = 512
VMEM = pltpu.CompilerParams(vmem_limit_bytes=48 << 20)
NT = (((1,), (1,)), ((), ()))


def cost(contractions, elements):
    return pl.CostEstimate(flops=2 * contractions, bytes_accessed=2 * elements, transcendentals=0)


def rows_of(shape):
    return lax.broadcasted_iota(jnp.int32, shape, 0)


def whole(shape):
    return pl.BlockSpec(shape, lambda j: (0,) * len(shape))


def pack_kernel(slot_ref, rows_ref, out_ref):
    hot = rows_of((out_ref.shape[0], slot_ref.shape[1])) == slot_ref[...]
    out_ref[...] = jnp.dot(
        hot.astype(jnp.bfloat16), rows_ref[...], preferred_element_type=jnp.float32
    ).astype(jnp.bfloat16)


def packed_rows(slot, rows, slots, first, width):
    tokens = rows.shape[0]
    skip = first // BLOCK
    return pl.pallas_call(
        pack_kernel,
        out_shape=jax.ShapeDtypeStruct((slots, width), jnp.bfloat16),
        grid=(width // BLOCK,),
        in_specs=[
            whole((1, tokens)),
            pl.BlockSpec((tokens, BLOCK), lambda j: (0, skip + j)),
        ],
        out_specs=pl.BlockSpec((slots, BLOCK), lambda j: (0, j)),
        compiler_params=VMEM,
        cost_estimate=cost(slots * tokens * width, (slots + tokens) * width),
    )(slot, rows)


def compact_tables(ring, place, code, hot_ref, note_ref):
    count = ring.shape[1]
    row = jnp.where(ring >= 0, ring * ROWS + place, -1)
    hot_ref[...] = (rows_of((RING * ROWS, count)) == row).astype(jnp.bfloat16)
    codes = jnp.broadcast_to(code, (8, count)).astype(jnp.bfloat16)
    for k in range(RING):
        mine = rows_of((128, count)) == jnp.where(ring == k, place, -1)
        note_ref[8 * k : 8 * k + 8, :] = lax.dot_general(
            codes, mine.astype(jnp.bfloat16), NT, preferred_element_type=jnp.float32
        )


def write_compact(rows, hot_ref, note_ref, out_refs):
    picked = jnp.dot(hot_ref[...], rows, preferred_element_type=jnp.float32)
    for k in range(RING):
        out_refs[k][...] = picked[k * ROWS : (k + 1) * ROWS].astype(jnp.bfloat16)

    @pl.when(pl.program_id(0) == 0)
    def _():
        for k in range(RING):
            tail = picked[(k + 1) * ROWS - 8 : (k + 1) * ROWS, :128]
            note = jnp.where(rows_of((8, 128)) == 7, note_ref[8 * k : 8 * k + 8, :], 0.0)
            out_refs[k][ROWS - 8 : ROWS, 0:128] = (tail + note).astype(jnp.bfloat16)


def ring_pack_kernel(ring_ref, place_ref, code_ref, rows_ref, *refs):
    outs, (hot_ref, note_ref) = refs[:RING], refs[RING:]

    @pl.when(pl.program_id(0) == 0)
    def _():
        compact_tables(ring_ref[...], place_ref[...], code_ref[...], hot_ref, note_ref)

    write_compact(rows_ref[...], hot_ref, note_ref, outs)


def ring_packed(ring, place, code, rows, width):
    tokens = rows.shape[0]
    return pl.pallas_call(
        ring_pack_kernel,
        out_shape=[jax.ShapeDtypeStruct((ROWS, width), jnp.bfloat16)] * RING,
        grid=(width // BLOCK,),
        in_specs=[whole((1, tokens))] * 3 + [pl.BlockSpec((tokens, BLOCK), lambda j: (0, j))],
        out_specs=[pl.BlockSpec((ROWS, BLOCK), lambda j: (0, j))] * RING,
        scratch_shapes=[
            pltpu.VMEM((RING * ROWS, tokens), jnp.bfloat16),
            pltpu.VMEM((8 * RING, 128), jnp.float32),
        ],
        compiler_params=VMEM,
        cost_estimate=cost(RING * ROWS * tokens * width, (RING * ROWS + tokens) * width),
    )(ring, place, code, rows)


def ring_repack_kernel(z_ref, rows_ref, *refs):
    outs, flag_ref = refs[:RING], refs[RING]
    hot_ref, note_ref, sum_ref, place_ref = refs[RING + 1 :]
    slots, width = rows_ref.shape
    step = pl.program_id(0)

    @pl.when(step == 0)
    def _():
        for r in range(0, slots, 256):
            total = jnp.zeros((256, 128), jnp.float32)
            for c in range(0, width, 128):
                total += jnp.abs(rows_ref[r : r + 256, c : c + 128].astype(jnp.float32))
            sum_ref[r : r + 256, :] = (total > 0).astype(jnp.bfloat16)
        seen = lax.dot_general(
            jnp.ones((8, 128), jnp.bfloat16), sum_ref[...], NT, preferred_element_type=jnp.float32
        )
        used = seen > 0
        used_bf16 = used.astype(jnp.bfloat16)
        for c in range(0, slots, 256):
            before = rows_of((slots, 256))
            slot = lax.broadcasted_iota(jnp.int32, (slots, 256), 1) + c
            ahead = (before < slot) & (((before ^ slot) & 28) == 0)
            place_ref[:, c : c + 256] = jnp.dot(
                used_bf16, ahead.astype(jnp.bfloat16), preferred_element_type=jnp.float32
            )
        place = place_ref[...].astype(jnp.int32)
        slot = lax.broadcasted_iota(jnp.int32, (8, slots), 1)
        over = jnp.where(used & (place >= ROWS - 1), 1.0, 0.0)
        flag_ref[...] = jnp.broadcast_to(jnp.max(over, axis=1, keepdims=True), (8, 128))
        ring = jnp.where(used & (place < ROWS - 1), (((slot >> 2) & 7) - z_ref[0]) & 7, -1)
        code = (((slot >> 5) << 2) + (slot & 3) + 1).astype(jnp.float32)
        compact_tables(ring[0:1, :], place[0:1, :], code[0:1, :], hot_ref, note_ref)

    start = pl.multiple_of(step * BLOCK, BLOCK)
    write_compact(rows_ref[:, pl.ds(start, BLOCK)], hot_ref, note_ref, outs)


def ring_repacked(z, rows):
    slots, width = rows.shape
    out = pl.pallas_call(
        ring_repack_kernel,
        out_shape=[jax.ShapeDtypeStruct((ROWS, width), jnp.bfloat16)] * RING
        + [jax.ShapeDtypeStruct((8, 128), jnp.float32)],
        grid=(width // BLOCK,),
        in_specs=[pl.BlockSpec(memory_space=pltpu.SMEM), whole((slots, width))],
        out_specs=[pl.BlockSpec((ROWS, BLOCK), lambda j: (0, j))] * RING + [whole((8, 128))],
        scratch_shapes=[
            pltpu.VMEM((RING * ROWS, slots), jnp.bfloat16),
            pltpu.VMEM((8 * RING, 128), jnp.float32),
            pltpu.VMEM((slots, 128), jnp.bfloat16),
            pltpu.VMEM((8, slots), jnp.float32),
        ],
        compiler_params=VMEM,
        cost_estimate=cost(RING * ROWS * slots * width, (RING * ROWS + slots) * width),
    )(z, rows)
    return out[:RING], out[RING]


def spread(z_ref, in_refs, hot_ref, held_ref):
    slots = hot_ref.shape[0]

    @pl.when(pl.program_id(0) == 0)
    def _():
        held_ref[...] = jnp.zeros_like(held_ref)
        for k in range(RING):
            code = in_refs[k][ROWS - 8 : ROWS, 0:128].astype(jnp.float32)[7:8, :].astype(jnp.int32)
            where = code - 1
            plane = (z_ref[0] - k) & 7
            slot = jnp.where(code > 0, ((where >> 2) << 5) + (plane << 2) + (where & 3), -1)
            hot_ref[:, 128 * k : 128 * k + 128] = (rows_of((slots, 128)) == slot).astype(
                jnp.bfloat16
            )

    for k in range(RING):
        held_ref[128 * k : 128 * k + ROWS, :] = in_refs[k][...]
    return jnp.dot(hot_ref[...], held_ref[...], preferred_element_type=jnp.float32)


def ring_spread_kernel(z_ref, *refs):
    ins, (out_ref, hot_ref, held_ref) = refs[:RING], refs[RING:]
    out_ref[...] = spread(z_ref, ins, hot_ref, held_ref).astype(jnp.bfloat16)


def ring_specs():
    return [pl.BlockSpec(memory_space=pltpu.SMEM)] + [
        pl.BlockSpec((ROWS, BLOCK), lambda j: (0, j))
    ] * RING


def ring_spread(z, parts, slots):
    width = parts[0].shape[1]
    return pl.pallas_call(
        ring_spread_kernel,
        out_shape=jax.ShapeDtypeStruct((slots, width), jnp.bfloat16),
        grid=(width // BLOCK,),
        in_specs=ring_specs(),
        out_specs=pl.BlockSpec((slots, BLOCK), lambda j: (0, j)),
        scratch_shapes=[
            pltpu.VMEM((slots, 128 * RING), jnp.bfloat16),
            pltpu.VMEM((128 * RING, BLOCK), jnp.bfloat16),
        ],
        compiler_params=VMEM,
        cost_estimate=cost(slots * 128 * RING * width, (slots + ROWS * RING) * width),
    )(z, *parts)


def placed(target, scale, rows, out_ref):
    scaled = (scale * rows).astype(jnp.bfloat16)
    hot = rows_of((out_ref.shape[0], target.shape[1])) == target
    out_ref[...] = jnp.dot(
        hot.astype(jnp.bfloat16), scaled, preferred_element_type=jnp.float32
    ).astype(jnp.bfloat16)


def place_kernel(target_ref, scale_ref, rows_ref, out_ref):
    placed(target_ref[...], scale_ref[...], rows_ref[...].astype(jnp.float32), out_ref)


def placed_rows(target, scale, rows, shard_rows, out_width):
    slots, width = rows.shape
    return pl.pallas_call(
        place_kernel,
        out_shape=jax.ShapeDtypeStruct((shard_rows, out_width), jnp.bfloat16),
        grid=(width // BLOCK,),
        in_specs=[
            whole((1, slots)),
            whole((slots, 1)),
            pl.BlockSpec((slots, BLOCK), lambda j: (0, j)),
        ],
        out_specs=pl.BlockSpec((shard_rows, BLOCK), lambda j: (0, j)),
        compiler_params=VMEM,
        cost_estimate=cost(shard_rows * slots * width, (shard_rows + slots) * width),
    )(target, scale, rows)


def ring_place_kernel(target_ref, scale_ref, z_ref, *refs):
    ins, (_, out_ref, hot_ref, held_ref) = refs[:RING], refs[RING:]
    placed(target_ref[...], scale_ref[...], spread(z_ref, ins, hot_ref, held_ref), out_ref)


def ring_placed(target, scale, z, parts, half_done):
    shard_rows, out_width = half_done.shape
    slots = target.shape[1]
    width = parts[0].shape[1]
    skip = (out_width - width) // BLOCK
    return pl.pallas_call(
        ring_place_kernel,
        out_shape=jax.ShapeDtypeStruct(half_done.shape, jnp.bfloat16),
        grid=(width // BLOCK,),
        in_specs=[whole((1, slots)), whole((slots, 1))]
        + ring_specs()
        + [pl.BlockSpec(memory_space=pl.ANY)],
        out_specs=pl.BlockSpec((shard_rows, BLOCK), lambda j: (0, skip + j)),
        scratch_shapes=[
            pltpu.VMEM((slots, 128 * RING), jnp.bfloat16),
            pltpu.VMEM((128 * RING, BLOCK), jnp.bfloat16),
        ],
        input_output_aliases={3 + RING: 0},
        compiler_params=VMEM,
        cost_estimate=cost((shard_rows + 1024) * slots * width, (shard_rows + slots) * width),
    )(target, scale, z, *parts, half_done)


def ring_shifted(parts):
    moved = [parts[0]]
    for k in range(1, RING):
        moved.append(lax.ppermute(parts[k], "dev_0", [(i, (i + k) % RING) for i in range(RING)]))
    return moved


def in_plane(rows):
    slots, width = rows.shape
    parts = rows.reshape(COLUMNS, slots // COLUMNS, width)
    return lax.all_to_all(parts, PLANE, split_axis=0, concat_axis=0, tiled=True).reshape(
        slots, width
    )


def slot_order(table):
    return table.reshape(4, RING, 8, CAP).swapaxes(1, 2).reshape(-1)


def count_earlier(key, counts):
    pos = jnp.arange(key.shape[0], dtype=jnp.int32)
    earlier = (pos[None, :] < pos[:, None]) & (key[None, :] == key[:, None]) & counts[None, :]
    return jnp.sum(earlier.astype(jnp.int32), axis=1)


def local(
    token_ids,
    sensitivity,
    last_hidden,
    lengths,
    norm_gain,
    reward_head,
    chosen_index,
    rejected_index,
    shard_owner,
):
    resp_local, block_len = token_ids.shape
    width = sensitivity.shape[2]
    half = width // 2
    tok_local = resp_local * block_len
    devices = shard_owner.shape[0]
    slots = devices * CAP
    shard_rows = VOCAB // devices
    responses = devices * resp_local
    cols = width // devices
    own_place = lax.axis_index(GRP_DEV)
    z = lax.axis_index("dev_0")[None]
    rows = sensitivity.reshape(tok_local, width)

    ids = token_ids.reshape(tok_local)
    shard_of = ids // shard_rows
    offset = ids - shard_of * shard_rows
    shard_hot = shard_of[:, None] == jnp.arange(devices, dtype=jnp.int32)[None, :]
    owner = jnp.sum(jnp.where(shard_hot, shard_owner[None, :], 0), axis=1)
    token_pos = jnp.arange(tok_local, dtype=jnp.int32)
    live = (jnp.arange(block_len, dtype=jnp.int32)[None, :] < lengths[:, None]).reshape(tok_local)
    rank = count_earlier(shard_of, jnp.ones_like(live))
    plane = (owner >> 3) & 7
    column = ((owner >> 6) << 3) + (owner & 7)
    place = count_earlier(plane, live)
    fits = live & (place < ROWS - 1)
    over_here = jnp.any(live & ~fits).astype(jnp.float32)
    ring = jnp.where(fits, (plane - z) & 7, -1)

    first = ring_packed(
        ring[None, :],
        place[None, :],
        (column * CAP + rank + 1).astype(jnp.float32)[None, :],
        rows,
        half,
    )
    first = ring_shifted(first)
    second_slot = jnp.where(live, (column << 5) + (plane << 2) + rank, -1)
    second = in_plane(packed_rows(second_slot[None, :], rows, slots, half, half))
    second, over_there = ring_repacked(z, second)
    second = ring_shifted(second)

    code = jnp.where(live, (offset + 1) * resp_local + token_pos // block_len, 0)
    direct_slot = owner * CAP + rank
    hidden = last_hidden.astype(jnp.float32)
    norm = jnp.sqrt(jnp.mean(hidden * hidden, axis=-1, keepdims=True) + 1e-05)
    own_reward = jnp.sum(hidden / norm * norm_gain * reward_head, axis=-1)
    slot_match = direct_slot[None, :] == jnp.arange(slots, dtype=jnp.int32)[:, None]
    codes = jnp.sum(jnp.where(slot_match, code[None, :], 0), axis=1).reshape(devices, CAP)
    over = jnp.maximum(over_here, over_there[0, 0])
    own_facts = jnp.concatenate(
        [own_reward, norm[:, 0], over[None], jnp.zeros((51,), jnp.float32)]
    )
    message = jnp.concatenate(
        [
            codes.astype(jnp.float32),
            jnp.broadcast_to(own_facts[None, :], (devices, 60)),
            hidden.reshape(resp_local, devices, cols).swapaxes(0, 1).reshape(devices, -1),
        ],
        axis=1,
    )
    heard = lax.all_to_all(message, GRP_DEV, split_axis=0, concat_axis=0, tiled=True)

    first = in_plane(ring_spread(z, first, slots))

    arrived_code = heard[:, :CAP].astype(jnp.int32)
    reward = heard[:, 4:8].reshape(responses)
    any_over = jnp.max(heard[:, 12]) > 0
    margin = reward[chosen_index] - reward[rejected_index]
    push = -jax.nn.sigmoid(-margin)
    every = jnp.arange(responses, dtype=jnp.int32)
    sign_table = (chosen_index[None, :] == every[:, None]).astype(jnp.float32) - (
        rejected_index[None, :] == every[:, None]
    ).astype(jnp.float32)
    reward_grad = jnp.sum(sign_table * push[None, :], axis=1).reshape(devices, resp_local)
    own_gain = lax.dynamic_slice(norm_gain, (own_place * cols,), (cols,))
    head_grad = jnp.zeros((cols,), jnp.float32)
    for r in range(resp_local):
        normed = heard[:, 64 + r * cols : 64 + (r + 1) * cols] / heard[:, 8 + r : 9 + r] * own_gain
        head_grad += jnp.sum(reward_grad[:, r : r + 1] * normed, axis=0)

    response_in = arrived_code % resp_local
    scale = jnp.zeros(arrived_code.shape, jnp.float32)
    for r in range(resp_local):
        scale = jnp.where(response_in == r, reward_grad[:, r : r + 1], scale)
    target = arrived_code // resp_local - 1
    scale = jnp.where(target >= 0, scale, 0.0)
    target_row = slot_order(target)[None, :]
    scale_column = slot_order(scale)[:, None]
    half_done = placed_rows(target_row, scale_column, first, shard_rows, width)

    def by_ring():
        return ring_placed(target_row, scale_column, z, second, half_done)

    def direct():
        sent = packed_rows(
            jnp.where(live, direct_slot, -1)[None, :], rows, slots, 0, width
        ).reshape(devices, CAP, width)
        arrived = lax.all_to_all(sent, GRP_DEV, split_axis=0, concat_axis=0, tiled=True)
        return placed_rows(
            target.reshape(1, slots),
            scale.reshape(slots, 1),
            arrived.reshape(slots, width),
            shard_rows,
            width,
        )

    return (lax.cond(any_over, direct, by_ring), head_grad)


def solution(mesh):
    torus = Mesh(
        mesh.devices.reshape(mesh.shape["grp"], 8, 4, 2), ("grp", "dev_0", "dev_1", "dev_2")
    )
    placed_as = (
        P(GRP_DEV, None),
        P(GRP_DEV, None, None),
        P(GRP_DEV, None),
        P(GRP_DEV),
        P(),
        P(),
        P(),
        P(),
        P(),
    )
    return jax.shard_map(
        local,
        mesh=torus,
        in_specs=placed_as,
        out_specs=(P(GRP_DEV, None), P(GRP_DEV)),
        check_vma=False,
    )
```

time: 247 us -> 203 us (0.82)
  waiting for transfers between devices: 181 us -> 60.7 us
  starting transfers between devices: 28.2 us -> 72.9 us
  Pallas kernels: 19 us -> 43.5 us
  local copies, waits for them, and re-layouts: 11 us -> 14.2 us
    all_to_all x1 -> x2, waiting for transfers between devices: 179 us -> 20.6 us  [in_plane(): lax.all_to_all(parts, PLANE, split_axis=0, concat_axis=0, tiled=True)]
    ppermute x0 -> x14, starting transfers between devices: none -> 47.7 us  [ring_shifted(): lax.ppermute(parts[k], 'dev_0', [(i, (i + k) % RING) for i in range(RING)])]
    ppermute x0 -> x14, waiting for transfers between devices: none -> 37.4 us  [ring_shifted(): lax.ppermute(parts[k], 'dev_0', [(i, (i + k) % RING) for i in range(RING)])]
    pallas_call x1 -> x5, Pallas kernels: 8.43 us -> 37.5 us  [the longest x1 10.1 us: ring_placed(): pl.pallas_call(ring_place_kernel, out_shape=jax.ShapeDtypeStruct(half_don...]
    pallas_call x1, Pallas kernels: 10.6 us -> 6 us  [placed_rows(): pl.pallas_call(place_kernel, out_shape=jax.ShapeDtypeStruct((shard_rows,...]
    all_to_all x1, starting transfers between devices: 15.7 us -> 11.5 us  [local(): lax.all_to_all(message, GRP_DEV, split_axis=0, concat_axis=0, tiled=True)]
    unnamed x6 -> x22, local copies, waits for them, and re-layouts: 2.19 us -> 5.46 us
    all_to_all x1 -> x2, starting transfers between devices: 12.6 us -> 13.7 us  [in_plane(): lax.all_to_all(parts, PLANE, split_axis=0, concat_axis=0, tiled=True)]
  transfers between devices with their start and end apart: 2 -> 17, of which waited for: 2 -> 7; matrix products, arithmetic and copies ran while one was open for 3% -> 6% of each run, Pallas kernels for 3% -> 14%
where the time goes in v2:
time: 203 us; the launch traced here: 201 us
  starting transfers between devices  72.9 us (36%)
  waiting for transfers between devices  60.7 us (30%)
  Pallas kernels  43.5 us (21%)
  local copies, waits for them, and re-layouts  14.2 us (7%)
  other arithmetic  6.44 us (3%)
  between operations  2.97 us (1%)
    ppermute x14, starting transfers between devices, ring_shifted(): lax.ppermute(parts[k], 'dev_0', [(i, (i + k) % RING) for i in range(RING)])  47.7 us
    ppermute x14, waiting for transfers between devices, ring_shifted(): lax.ppermute(parts[k], 'dev_0', [(i, (i + k) % RING) for i in range(RING)])  37.4 us
    all_to_all x2, waiting for transfers between devices, in_plane(): lax.all_to_all(parts, PLANE, split_axis=0, concat_axis=0, tiled=True)  20.6 us
    all_to_all x2, starting transfers between devices, in_plane(): lax.all_to_all(parts, PLANE, split_axis=0, concat_axis=0, tiled=True)  13.7 us
    all_to_all x1, starting transfers between devices, local(): lax.all_to_all(message, GRP_DEV, split_axis=0, concat_axis=0, tiled=True)  11.5 us
    pallas_call x1, Pallas kernels, ring_placed(): pl.pallas_call(ring_place_kernel, out_shape=jax.ShapeDtypeStruct(half_don...  10.1 us
    pallas_call x1, Pallas kernels, ring_repacked(): pl.pallas_call(ring_repack_kernel, out_shape=[jax.ShapeDtypeStruct((ROWS,...  9.41 us
    pallas_call x1, Pallas kernels, ring_spread(): pl.pallas_call(ring_spread_kernel, out_shape=jax.ShapeDtypeStruct((slots,...  8.06 us
  transfers between devices with their start and end apart: 17, of which 7 were waited for; matrix products, arithmetic and copies ran while one was open for 6% of the time, Pallas kernels for 14%

profile of v2, /device:TPU:1, one launch (start us, length us, event | category | flops | bytes accessed | tf_op | source)
XLA Modules:
  0.0 200.7 jit_solution(16716215984074025287)
XLA Ops:
  0.6 0.7 fusion.27
  1.4 0.8 add_select_fusion.4
  2.4 0.9 select_reduce_fusion.1
  3.6 4.5 %shard_map.104 = bf16[1024,2048]{1,0:T(8,128)(2,1)S(1)} custom-call(s32[1,512]{1,0:T(1,128)S(1)} %get-tuple-element.188.slot_ref, bf16[512,4096]{1,0:T(8,128)(2,1)} %bitcast.76), custom_call_target="tpu_custom_call" | custom-call | flops 2147483648 | bytes 6291456 | tf_op jit(solution)/shard_map/pallas_call | solution.py:45
  8.1 2.0 copy-done
  10.1 8.6 %all-to-all-start.1 = ((bf16[32,32,2048]{2,1,0:T(8,128)(2,1)}), bf16[32,32,2048]{2,1,0:T(8,128)(2,1)}, u32[]{:S(2)}, u32[]{:S(2)}) async-start(bf16[32,32,2048]{2,1,0:T(8,128)(2,1)} %bitcast.71), calls=%async_computation.1 | async-start | bytes 8388608 | tf_op jit(solution)/shard_map/all_to_all | solution.py:284
  18.8 5.4 %shard_map.106 = (bf16[88,2048]{1,0:T(8,128)(2,1)S(1)}, bf16[88,2048]{1,0:T(8,128)(2,1)}, bf16[88,2048]{1,0:T(8,128)(2,1)}, bf16[88,2048]{1,0:T(8,128)(2,1)S(1)}...) custom-call(s32[1,512]{1,0:T(1,128)S(1)} %get-tuple-element.187.ring, ...), custom_call_target="tpu_custom_call" | custom-call | flops 1476395008 | bytes 4980736 | tf_op jit(solution)/shard_map/pallas_call | solution.py:96
  24.2 0.7 copy-done.3
  24.9 6.9 %collective-permute-start.10 = (bf16[88,2048]{1,0:T(8,128)(2,1)S(1)}, bf16[88,2048]{1,0:T(8,128)(2,1)S(1)}, u32[]{:S(2)}, u32[]{:S(2)}) collective-permute-start(bf16[88,2048]{1,0:T(8,128)(2,1)S(1)} %get-tuple-element.99), channel_id=1, source_target_pairs={{0,32},{8,40},{16,48},{24,56},{32,0},{40,8},{48,16},{56,24},{1,33}... | collective-permute-start | bytes 1081352 | tf_op jit(solution)/shard_map/ppermute | solution.py:277
  31.8 4.0 %collective-permute-start.12 = (bf16[88,2048]{1,0:T(8,128)(2,1)}, bf16[88,2048]{1,0:T(8,128)(2,1)}, u32[]{:S(2)}, u32[]{:S(2)}) collective-permute-start(bf16[88,2048]{1,0:T(8,128)(2,1)} %get-tuple-element.101), channel_id=1, source_target_pairs={{0,48},{8,56},{16,0},{24,8},{32,16},{40,24},{48,32},{56,40},{1,49}... | collective-permute-start | bytes 1081352 | tf_op jit(solution)/shard_map/ppermute | solution.py:277
  35.9 0.7 collective-permute-start.13
  36.6 0.7 collective-permute-start.7
  37.5 0.3 select_reduce_fusion
  37.8 0.7 and_reduce_fusion
  40.0 1.5 collective-permute-done.10.refs_4_
  41.5 8.0 %collective-permute-start.8 = (bf16[88,2048]{1,0:T(8,128)(2,1)}, bf16[88,2048]{1,0:T(8,128)(2,1)}, u32[]{:S(2)}, u32[]{:S(2)}) collective-permute-start(bf16[88,2048]{1,0:T(8,128)(2,1)} %get-tuple-element.97), channel_id=1, source_target_pairs={{0,16},{8,24},{16,32},{24,40},{32,48},{40,56},{48,0},{56,8},{1,17}... | collective-permute-start | bytes 1081352 | tf_op jit(solution)/shard_map/ppermute | solution.py:277
  49.5 22.7 %collective-permute-done.11.refs_5_ = bf16[88,2048]{1,0:T(8,128)(2,1)S(1)} collective-permute-done((bf16[88,2048]{1,0:T(8,128)(2,1)S(1)}, bf16[88,2048]{1,0:T(8,128)(2,1)S(1)}, u32[]{:S(2)}, u32[]{:S(2)}) %collective-permute-start.11) | collective-permute-done | bytes 360480 | tf_op jit(solution)/shard_map/ppermute | solution.py:277
  72.2 0.7 copy-done.1
  72.9 4.9 %collective-permute-start.9 = (bf16[88,2048]{1,0:T(8,128)(2,1)S(1)}, bf16[88,2048]{1,0:T(8,128)(2,1)}, u32[]{:S(2)}, u32[]{:S(2)}) collective-permute-start(bf16[88,2048]{1,0:T(8,128)(2,1)S(1)} %get-tuple-element.98), channel_id=1, source_target_pairs={{0,24},{8,32},{16,40},{24,48},{32,56},{40,0},{48,8},{56,16},{1,25}... | collective-permute-start | bytes 1081352 | tf_op jit(solution)/shard_map/ppermute | solution.py:277
  77.8 9.4 %shard_map.105 = (bf16[88,2048]{1,0:T(8,128)(2,1)}, bf16[88,2048]{1,0:T(8,128)(2,1)S(1)}, bf16[88,2048]{1,0:T(8,128)(2,1)S(1)}, bf16[88,2048]{1,0:T(8,128)(2,1)S...) custom-call(s32[1]{0:T(128)} %bitcast.4.z_ref, ...), custom_call_target="tpu_custom_call" | custom-call | flops 2952790016 | bytes 7077888 | tf_op jit(solution)/shard_map/pallas_call | solution.py:150
  87.3 0.5 slice.52
  88.6 0.7 copy.44
  89.4 11.5 %all-to-all-start.2 = ((f32[256,1,128]{2,1,0:T(1,128)}), f32[256,1,128]{2,1,0:T(1,128)S(1)}, u32[]{:S(2)}, u32[]{:S(2)}) async-start(f32[256,1,128]{2,1,0:T(1,128)} %copy.44), calls=%async_computation.2 | async-start | bytes 262144 | tf_op jit(solution)/shard_map/all_to_all | solution.py:370
  100.9 1.0 copy-done.2
  101.9 1.0 copy-done.4
  102.8 8.1 %shard_map.107 = bf16[1024,2048]{1,0:T(8,128)(2,1)} custom-call(s32[1]{0:T(128)} %bitcast.4.z_ref, bf16[88,2048]{1,0:T(8,128)(2,1)S(1)} %copy-done.4, bf16[88,2048]{1,0:T(8,128)(2,1)} %collective-permute-done.7.refs_1_, bf16[88,2048]{1,0:T(8,128)(2,1)} %collective-permute-done.8.refs_2_, bf16[88,2048]{1,0:T(8,128)(2,1)} %collective-permute-done.9.refs_3_, ...), custom_call_target="tpu_custom_call" | custom-call | flops 4294967296 | bytes 7077888 | tf_op jit(solution)/shard_map/pallas_call | solution.py:202
  110.9 2.8 %all-to-all-done.2 = f32[256,1,128]{2,1,0:T(1,128)S(1)} async-done(((f32[256,1,128]{2,1,0:T(1,128)}), f32[256,1,128]{2,1,0:T(1,128)S(1)}, u32[]{:S(2)}, u32[]{:S(2)}) %all-to-all-start.2) | async-done | bytes 131104 | tf_op jit(solution)/shard_map/all_to_all | solution.py:370
  113.7 5.1 %all-to-all-start.3 = ((bf16[32,32,2048]{2,1,0:T(8,128)(2,1)}), bf16[32,32,2048]{2,1,0:T(8,128)(2,1)}, u32[]{:S(2)}, u32[]{:S(2)}) async-start(bf16[32,32,2048]{2,1,0:T(8,128)(2,1)} %bitcast.79), calls=%async_computation.3 | async-start | bytes 8388608 | tf_op jit(solution)/shard_map/all_to_all | solution.py:284
  118.9 1.3 collective-permute-start
  120.2 2.6 %collective-permute-start.1 = (bf16[88,2048]{1,0:T(8,128)(2,1)S(1)}, bf16[88,2048]{1,0:T(8,128)(2,1)}, u32[]{:S(2)}, u32[]{:S(2)}) collective-permute-start(bf16[88,2048]{1,0:T(8,128)(2,1)S(1)} %get-tuple-element.89), channel_id=1, source_target_pairs={{0,16},{8,24},{16,32},{24,40},{32,48},{40,56},{48,0},{56,8},{1,17}... | collective-permute-start | bytes 1081352 | tf_op jit(solution)/shard_map/ppermute | solution.py:277
  122.8 3.2 %collective-permute-start.2 = (bf16[88,2048]{1,0:T(8,128)(2,1)S(1)}, bf16[88,2048]{1,0:T(8,128)(2,1)}, u32[]{:S(2)}, u32[]{:S(2)}) collective-permute-start(bf16[88,2048]{1,0:T(8,128)(2,1)S(1)} %get-tuple-element.90), channel_id=1, source_target_pairs={{0,24},{8,32},{16,40},{24,48},{32,56},{40,0},{48,8},{56,16},{1,25}... | collective-permute-start | bytes 1081352 | tf_op jit(solution)/shard_map/ppermute | solution.py:277
  126.0 1.0 collective-permute-start.3
  127.0 3.7 %collective-permute-start.4 = (bf16[88,2048]{1,0:T(8,128)(2,1)S(1)}, bf16[88,2048]{1,0:T(8,128)(2,1)}, u32[]{:S(2)}, u32[]{:S(2)}) collective-permute-start(bf16[88,2048]{1,0:T(8,128)(2,1)S(1)} %get-tuple-element.92), channel_id=1, source_target_pairs={{0,40},{8,48},{16,56},{24,0},{32,8},{40,16},{48,24},{56,32},{1,41}... | collective-permute-start | bytes 1081352 | tf_op jit(solution)/shard_map/ppermute | solution.py:277
  131.1 2.3 %gather_fusion = f32[512]{0:T(512)S(1)} fusion(f32[1024]{0:T(1024)S(1)} %reshape.326, s32[1024]{0:T(1024)S(1)} %pad_clamp_fusion.1), kind=kCustom, calls=%fused_computation | custom fusion | bytes 6144 | tf_op jit(solution)/shard_map/gather | solution.py:377
  133.4 2.3 %gather_fusion.1 = f32[512]{0:T(512)S(1)} fusion(f32[1024]{0:T(1024)S(1)} %reshape.326, s32[1024]{0:T(1024)S(1)} %pad_clamp_fusion), kind=kCustom, calls=%fused_computation.1 | custom fusion | bytes 6144 | tf_op jit(solution)/shard_map/gather | solution.py:377
  135.7 0.6 multiply_reduce_fusion
  136.4 0.3 slice_reduce_fusion.3
  138.1 0.6 fusion.32
  139.6 2.8 %collective-permute-start.5 = (bf16[88,2048]{1,0:T(8,128)(2,1)S(1)}, bf16[88,2048]{1,0:T(8,128)(2,1)S(1)}, u32[]{:S(2)}, u32[]{:S(2)}) collective-permute-start(bf16[88,2048]{1,0:T(8,128)(2,1)S(1)} %get-tuple-element.93), channel_id=1, source_target_pairs={{0,48},{8,56},{16,0},{24,8},{32,16},{40,24},{48,32},{56,40},{1,49}... | collective-permute-start | bytes 1081352 | tf_op jit(solution)/shard_map/ppermute | solution.py:277
  142.4 7.7 %collective-permute-start.6 = (bf16[88,2048]{1,0:T(8,128)(2,1)S(1)}, bf16[88,2048]{1,0:T(8,128)(2,1)S(1)}, u32[]{:S(2)}, u32[]{:S(2)}) collective-permute-start(bf16[88,2048]{1,0:T(8,128)(2,1)S(1)} %get-tuple-element.94), channel_id=1, source_target_pairs={{0,56},{8,0},{16,8},{24,16},{32,24},{40,32},{48,40},{56,48},{1,57}... | collective-permute-start | bytes 1081352 | tf_op jit(solution)/shard_map/ppermute | solution.py:277
  150.2 0.5 add_add_fusion.1
  150.7 20.6 %all-to-all-done.3 = bf16[32,32,2048]{2,1,0:T(8,128)(2,1)} async-done(((bf16[32,32,2048]{2,1,0:T(8,128)(2,1)}), bf16[32,32,2048]{2,1,0:T(8,128)(2,1)}, u32[]{:S(2)}, u32[]{:S(2)}) %all-to-all-start.3) | async-done | bytes 4194336 | tf_op jit(solution)/shard_map/all_to_all | solution.py:284
  171.3 6.0 %shard_map.108 = bf16[501,4096]{1,0:T(8,128)(2,1)} custom-call(s32[1,1024]{1,0:T(1,128)S(1)} %broadcast_in_dim_reshape.7.target_ref, f32[1024,1]{1,0:T(8,128)S(1)} %copy.49.scale_ref, bf16[1024,2048]{1,0:T(8,128)(2,1)} %bitcast.21.rows_ref), custom_call_target="tpu_custom_call" | custom-call | flops 2101346304 | bytes 6246400 | tf_op jit(solution)/shard_map/pallas_call | solution.py:231
  177.3 1.3 collective-permute-done.3
  178.6 6.5 %collective-permute-done.5 = bf16[88,2048]{1,0:T(8,128)(2,1)S(1)} collective-permute-done((bf16[88,2048]{1,0:T(8,128)(2,1)S(1)}, bf16[88,2048]{1,0:T(8,128)(2,1)S(1)}, u32[]{:S(2)}, u32[]{:S(2)}) %collective-permute-start.5) | collective-permute-done | bytes 360480 | tf_op jit(solution)/shard_map/ppermute | solution.py:277
  185.1 5.4 %collective-permute-done.6 = bf16[88,2048]{1,0:T(8,128)(2,1)S(1)} collective-permute-done((bf16[88,2048]{1,0:T(8,128)(2,1)S(1)}, bf16[88,2048]{1,0:T(8,128)(2,1)S(1)}, u32[]{:S(2)}, u32[]{:S(2)}) %collective-permute-start.6) | collective-permute-done | bytes 360480 | tf_op jit(solution)/shard_map/ppermute | solution.py:277
  190.4 10.3 %conditional.1 = (bf16[501,4096]{1,0:T(8,128)(2,1)}) conditional(s32[]{:T(128)} %convert_element_type.46, (s32[1,1024]{1,0:T(1,128)S(1)}, f32[1024,1]{0,1:T(1,128)S(1)}, s32[1]{0:T(128)}, bf16[88,2048]{1,0:T(8,128)(2,1)}, bf16[88,2048]{1,0:T(8,128)(2,1)}, /*index=5*/bf16[88,2048]{1,0:T(8,128)(2,1)}, bf16[88,2048]{1,0:T(8,128)(2,1)}, ...), branch_computations={%region_9.10_spmd, %region_10.11_spmd} | conditional | flops 8497661952 | bytes 83839016 | solution.py:416
  190.7 10.1 %branch_0_fun.1 = bf16[501,4096]{1,0:T(8,128)(2,1)} custom-call(s32[1,1024]{1,0:T(1,128)S(1)} %get-tuple-element.48.target_ref, f32[1024,1]{1,0:T(8,128)S(1)} %copy.50.scale_ref, s32[1]{0:T(128)} %get-tuple-element.50.z_ref, bf16[88,2048]{1,0:T(8,128)(2,1)} %get-tuple-element.51.refs_0_, ...), custom_call_target="tpu_custom_call", output_to_operand_aliasing={{}: (11, {})} | custom-call | flops 6396313600 | bytes 6246400 | tf_op jit(solution)/shard_map/cond/branch_0_fun/pallas_call | solution.py:256
  (66 shorter events, 4.0 us)
Async XLA Ops:
  8.1 2.0 copy-start
  10.1 67.8 %all-to-all-start.1 = ((bf16[32,32,2048]{2,1,0:T(8,128)(2,1)}), bf16[32,32,2048]{2,1,0:T(8,128)(2,1)}, u32[]{:S(2)}, u32[]{:S(2)}) async-start(bf16[32,32,2048]{2,1,0:T(8,128)(2,1)} %bitcast.71), calls=%async_computation.1 | async-start | bytes 8388608 | tf_op jit(solution)/shard_map/all_to_all | solution.py:284
  18.7 18.6 %copy-start.5 = (bf16[4,4096]{1,0:T(4,128)(2,1)S(1)}, bf16[4,4096]{1,0:T(4,128)(2,1)}, u32[]{:S(2)}) copy-start(bf16[4,4096]{1,0:T(4,128)(2,1)} %param.13) | copy-start | bytes 98308
  18.7 19.1 %copy-start.8 = (s32[4]{0:T(128)S(1)}, s32[4]{0:T(128)}, u32[]{:S(2)}) copy-start(s32[4]{0:T(128)} %param.14) | copy-start | bytes 52
  18.7 21.0 %copy-start.6 = (f32[4096]{0:T(1024)S(1)}, f32[4096]{0:T(1024)}, u32[]{:S(2)}) copy-start(f32[4096]{0:T(1024)} %param.16) | copy-start | bytes 49156
  18.8 21.0 %copy-start.7 = (f32[4096]{0:T(1024)S(1)}, f32[4096]{0:T(1024)}, u32[]{:S(2)}) copy-start(f32[4096]{0:T(1024)} %param.15) | copy-start | bytes 49156
  24.2 0.7 copy-start.3
  24.9 16.6 %collective-permute-start.10 = (bf16[88,2048]{1,0:T(8,128)(2,1)S(1)}, bf16[88,2048]{1,0:T(8,128)(2,1)S(1)}, u32[]{:S(2)}, u32[]{:S(2)}) collective-permute-start(bf16[88,2048]{1,0:T(8,128)(2,1)S(1)} %get-tuple-element.99), channel_id=1, source_target_pairs={{0,32},{8,40},{16,48},{24,56},{32,0},{40,8},{48,16},{56,24},{1,33}... | collective-permute-start | bytes 1081352 | tf_op jit(solution)/shard_map/ppermute | solution.py:277
  31.8 40.3 %collective-permute-start.11 = (bf16[88,2048]{1,0:T(8,128)(2,1)S(1)}, bf16[88,2048]{1,0:T(8,128)(2,1)S(1)}, u32[]{:S(2)}, u32[]{:S(2)}) collective-permute-start(bf16[88,2048]{1,0:T(8,128)(2,1)S(1)} %get-tuple-element.100), channel_id=1, source_target_pairs={{0,40},{8,48},{16,56},{24,0},{32,8},{40,16},{48,24},{56,32},{1,41}... | collective-permute-start | bytes 1081352 | tf_op jit(solution)/shard_map/ppermute | solution.py:277
  31.8 69.0 %collective-permute-start.12 = (bf16[88,2048]{1,0:T(8,128)(2,1)}, bf16[88,2048]{1,0:T(8,128)(2,1)}, u32[]{:S(2)}, u32[]{:S(2)}) collective-permute-start(bf16[88,2048]{1,0:T(8,128)(2,1)} %get-tuple-element.101), channel_id=1, source_target_pairs={{0,48},{8,56},{16,0},{24,8},{32,16},{40,24},{48,32},{56,40},{1,49}... | collective-permute-start | bytes 1081352 | tf_op jit(solution)/shard_map/ppermute | solution.py:277
  35.9 64.9 %collective-permute-start.13 = (bf16[88,2048]{1,0:T(8,128)(2,1)}, bf16[88,2048]{1,0:T(8,128)(2,1)}, u32[]{:S(2)}, u32[]{:S(2)}) collective-permute-start(bf16[88,2048]{1,0:T(8,128)(2,1)} %get-tuple-element.102), channel_id=1, source_target_pairs={{0,56},{8,0},{16,8},{24,16},{32,24},{40,32},{48,40},{56,48},{1,57}... | collective-permute-start | bytes 1081352 | tf_op jit(solution)/shard_map/ppermute | solution.py:277
  36.6 64.2 %collective-permute-start.7 = (bf16[88,2048]{1,0:T(8,128)(2,1)}, bf16[88,2048]{1,0:T(8,128)(2,1)}, u32[]{:S(2)}, u32[]{:S(2)}) collective-permute-start(bf16[88,2048]{1,0:T(8,128)(2,1)} %get-tuple-element.96), channel_id=1, source_target_pairs={{0,8},{8,16},{16,24},{24,32},{32,40},{40,48},{48,56},{56,0},{1,9},... | collective-permute-start | bytes 1081352 | tf_op jit(solution)/shard_map/ppermute | solution.py:277
  41.5 59.3 %collective-permute-start.8 = (bf16[88,2048]{1,0:T(8,128)(2,1)}, bf16[88,2048]{1,0:T(8,128)(2,1)}, u32[]{:S(2)}, u32[]{:S(2)}) collective-permute-start(bf16[88,2048]{1,0:T(8,128)(2,1)} %get-tuple-element.97), channel_id=1, source_target_pairs={{0,16},{8,24},{16,32},{24,40},{32,48},{40,56},{48,0},{56,8},{1,17}... | collective-permute-start | bytes 1081352 | tf_op jit(solution)/shard_map/ppermute | solution.py:277
  72.2 0.7 copy-start.1
  72.9 27.9 %collective-permute-start.9 = (bf16[88,2048]{1,0:T(8,128)(2,1)S(1)}, bf16[88,2048]{1,0:T(8,128)(2,1)}, u32[]{:S(2)}, u32[]{:S(2)}) collective-permute-start(bf16[88,2048]{1,0:T(8,128)(2,1)S(1)} %get-tuple-element.98), channel_id=1, source_target_pairs={{0,24},{8,32},{16,40},{24,48},{32,56},{40,0},{48,8},{56,16},{1,25}... | collective-permute-start | bytes 1081352 | tf_op jit(solution)/shard_map/ppermute | solution.py:277
  89.4 24.3 %all-to-all-start.2 = ((f32[256,1,128]{2,1,0:T(1,128)}), f32[256,1,128]{2,1,0:T(1,128)S(1)}, u32[]{:S(2)}, u32[]{:S(2)}) async-start(f32[256,1,128]{2,1,0:T(1,128)} %copy.44), calls=%async_computation.2 | async-start | bytes 262144 | tf_op jit(solution)/shard_map/all_to_all | solution.py:370
  100.9 1.0 copy-start.2
  101.9 1.0 copy-start.4
  113.7 5.2 %copy-start.9 = (s32[512]{0:T(512)S(1)}, s32[512]{0:T(512)}, u32[]{:S(2)}) copy-start(s32[512]{0:T(512)} %param.17) | copy-start | bytes 6148
  113.7 5.2 %copy-start.10 = (s32[512]{0:T(512)S(1)}, s32[512]{0:T(512)}, u32[]{:S(2)}) copy-start(s32[512]{0:T(512)} %param.18) | copy-start | bytes 6148
  113.7 57.6 %all-to-all-start.3 = ((bf16[32,32,2048]{2,1,0:T(8,128)(2,1)}), bf16[32,32,2048]{2,1,0:T(8,128)(2,1)}, u32[]{:S(2)}, u32[]{:S(2)}) async-start(bf16[32,32,2048]{2,1,0:T(8,128)(2,1)} %bitcast.79), calls=%async_computation.3 | async-start | bytes 8388608 | tf_op jit(solution)/shard_map/all_to_all | solution.py:284
  118.9 20.7 %collective-permute-start = (bf16[88,2048]{1,0:T(8,128)(2,1)S(1)}, bf16[88,2048]{1,0:T(8,128)(2,1)}, u32[]{:S(2)}, u32[]{:S(2)}) collective-permute-start(bf16[88,2048]{1,0:T(8,128)(2,1)S(1)} %get-tuple-element.88), channel_id=1, source_target_pairs={{0,8},{8,16},{16,24},{24,32},{32,40},{40,48},{48,56},{56,0},{1,9},... | collective-permute-start | bytes 1081352 | tf_op jit(solution)/shard_map/ppermute | solution.py:277
  120.2 22.3 %collective-permute-start.1 = (bf16[88,2048]{1,0:T(8,128)(2,1)S(1)}, bf16[88,2048]{1,0:T(8,128)(2,1)}, u32[]{:S(2)}, u32[]{:S(2)}) collective-permute-start(bf16[88,2048]{1,0:T(8,128)(2,1)S(1)} %get-tuple-element.89), channel_id=1, source_target_pairs={{0,16},{8,24},{16,32},{24,40},{32,48},{40,56},{48,0},{56,8},{1,17}... | collective-permute-start | bytes 1081352 | tf_op jit(solution)/shard_map/ppermute | solution.py:277
  122.8 54.5 %collective-permute-start.2 = (bf16[88,2048]{1,0:T(8,128)(2,1)S(1)}, bf16[88,2048]{1,0:T(8,128)(2,1)}, u32[]{:S(2)}, u32[]{:S(2)}) collective-permute-start(bf16[88,2048]{1,0:T(8,128)(2,1)S(1)} %get-tuple-element.90), channel_id=1, source_target_pairs={{0,24},{8,32},{16,40},{24,48},{32,56},{40,0},{48,8},{56,16},{1,25}... | collective-permute-start | bytes 1081352 | tf_op jit(solution)/shard_map/ppermute | solution.py:277
  126.0 52.6 %collective-permute-start.3 = (bf16[88,2048]{1,0:T(8,128)(2,1)S(1)}, bf16[88,2048]{1,0:T(8,128)(2,1)}, u32[]{:S(2)}, u32[]{:S(2)}) collective-permute-start(bf16[88,2048]{1,0:T(8,128)(2,1)S(1)} %get-tuple-element.91), channel_id=1, source_target_pairs={{0,32},{8,40},{16,48},{24,56},{32,0},{40,8},{48,16},{56,24},{1,33}... | collective-permute-start | bytes 1081352 | tf_op jit(solution)/shard_map/ppermute | solution.py:277
  127.0 51.6 %collective-permute-start.4 = (bf16[88,2048]{1,0:T(8,128)(2,1)S(1)}, bf16[88,2048]{1,0:T(8,128)(2,1)}, u32[]{:S(2)}, u32[]{:S(2)}) collective-permute-start(bf16[88,2048]{1,0:T(8,128)(2,1)S(1)} %get-tuple-element.92), channel_id=1, source_target_pairs={{0,40},{8,48},{16,56},{24,0},{32,8},{40,16},{48,24},{56,32},{1,41}... | collective-permute-start | bytes 1081352 | tf_op jit(solution)/shard_map/ppermute | solution.py:277
  139.6 45.5 %collective-permute-start.5 = (bf16[88,2048]{1,0:T(8,128)(2,1)S(1)}, bf16[88,2048]{1,0:T(8,128)(2,1)S(1)}, u32[]{:S(2)}, u32[]{:S(2)}) collective-permute-start(bf16[88,2048]{1,0:T(8,128)(2,1)S(1)} %get-tuple-element.93), channel_id=1, source_target_pairs={{0,48},{8,56},{16,0},{24,8},{32,16},{40,24},{48,32},{56,40},{1,49}... | collective-permute-start | bytes 1081352 | tf_op jit(solution)/shard_map/ppermute | solution.py:277
  142.4 48.0 %collective-permute-start.6 = (bf16[88,2048]{1,0:T(8,128)(2,1)S(1)}, bf16[88,2048]{1,0:T(8,128)(2,1)S(1)}, u32[]{:S(2)}, u32[]{:S(2)}) collective-permute-start(bf16[88,2048]{1,0:T(8,128)(2,1)S(1)} %get-tuple-element.94), channel_id=1, source_target_pairs={{0,56},{8,0},{16,8},{24,16},{32,24},{40,32},{48,40},{56,48},{1,57}... | collective-permute-start | bytes 1081352 | tf_op jit(solution)/shard_map/ppermute | solution.py:277

commit v3 on v2

--- a/solution.py
+++ b/solution.py
@@ -345,6 +345,7 @@
     first = ring_shifted(first)
     second_slot = jnp.where(live, (column << 5) + (plane << 2) + rank, -1)
     second = in_plane(packed_rows(second_slot[None, :], rows, slots, half, half))
+    first[1], first[2], second = lax.optimization_barrier((first[1], first[2], second))
     second, over_there = ring_repacked(z, second)
     second = ring_shifted(second)
 
@@ -368,8 +369,6 @@
         axis=1,
     )
     heard = lax.all_to_all(message, GRP_DEV, split_axis=0, concat_axis=0, tiled=True)
-
-    first = in_plane(ring_spread(z, first, slots))
 
     arrived_code = heard[:, :CAP].astype(jnp.int32)
     reward = heard[:, 4:8].reshape(responses)
@@ -395,6 +394,10 @@
     scale = jnp.where(target >= 0, scale, 0.0)
     target_row = slot_order(target)[None, :]
     scale_column = slot_order(scale)[:, None]
+    target_row, scale_column, first = lax.optimization_barrier((target_row, scale_column, first))
+    first = ring_spread(z, first, slots)
+    first, second[1], second[7] = lax.optimization_barrier((first, second[1], second[7]))
+    first = in_plane(first)
     half_done = placed_rows(target_row, scale_column, first, shard_rows, width)
 
     def by_ring():

time: 203 us -> 212 us (1.044)
  waiting for transfers between devices: 60.7 us -> 76.7 us
  starting transfers between devices: 72.9 us -> 63.6 us
  local copies, waits for them, and re-layouts: 14.2 us -> 17.7 us
    all_to_all x2, waiting for transfers between devices: 20.6 us -> 56.6 us  [in_plane(): lax.all_to_all(parts, PLANE, split_axis=0, concat_axis=0, tiled=True)]
    ppermute x14, waiting for transfers between devices: 37.4 us -> 7.25 us  [ring_shifted(): lax.ppermute(parts[k], 'dev_0', [(i, (i + k) % RING) for i in range(RING)])]
    ppermute x14, starting transfers between devices: 47.7 us -> 35.4 us  [ring_shifted(): lax.ppermute(parts[k], 'dev_0', [(i, (i + k) % RING) for i in range(RING)])]
    all_to_all x1, waiting for transfers between devices: 2.77 us -> 12.8 us  [local(): lax.all_to_all(message, GRP_DEV, split_axis=0, concat_axis=0, tiled=True)]
    reshape x4, local copies, waits for them, and re-layouts: 0.72 us -> 3.65 us  [slot_order(): return table.reshape(4, RING, 8, CAP).swapaxes(1, 2).reshape(-1)]
    all_to_all x1, starting transfers between devices: 11.5 us -> 13.9 us  [local(): lax.all_to_all(message, GRP_DEV, split_axis=0, concat_axis=0, tiled=True)]
    unnamed x22 -> x40, local copies, waits for them, and re-layouts: 5.46 us -> 6.01 us
  transfers between devices with their start and end apart: 17 -> 17, of which waited for: 7 -> 5; matrix products, arithmetic and copies ran while one was open for 6% -> 7% of each run, Pallas kernels for 14% -> 14%
where the time goes in v3:
time: 212 us; the launch traced here: 211 us
  waiting for transfers between devices  76.7 us (36%)
  starting transfers between devices  63.6 us (30%)
  Pallas kernels  43.6 us (21%)
  local copies, waits for them, and re-layouts  17.7 us (8%)
  other arithmetic  6.45 us (3%)
  between operations  3 us (1%)
    all_to_all x2, waiting for transfers between devices, in_plane(): lax.all_to_all(parts, PLANE, split_axis=0, concat_axis=0, tiled=True)  56.6 us
    ppermute x14, starting transfers between devices, ring_shifted(): lax.ppermute(parts[k], 'dev_0', [(i, (i + k) % RING) for i in range(RING)])  35.4 us
    all_to_all x2, starting transfers between devices, in_plane(): lax.all_to_all(parts, PLANE, split_axis=0, concat_axis=0, tiled=True)  14.3 us
    all_to_all x1, starting transfers between devices, local(): lax.all_to_all(message, GRP_DEV, split_axis=0, concat_axis=0, tiled=True)  13.9 us
    all_to_all x1, waiting for transfers between devices, local(): lax.all_to_all(message, GRP_DEV, split_axis=0, concat_axis=0, tiled=True)  12.8 us
    pallas_call x1, Pallas kernels, ring_placed(): pl.pallas_call(ring_place_kernel, out_shape=jax.ShapeDtypeStruct(half_don...  10.1 us
    pallas_call x1, Pallas kernels, ring_repacked(): pl.pallas_call(ring_repack_kernel, out_shape=[jax.ShapeDtypeStruct((ROWS,...  9.4 us
    pallas_call x1, Pallas kernels, ring_spread(): pl.pallas_call(ring_spread_kernel, out_shape=jax.ShapeDtypeStruct((slots,...  8.09 us
  transfers between devices with their start and end apart: 17, of which 5 were waited for; matrix products, arithmetic and copies ran while one was open for 7% of the time, Pallas kernels for 14%

profile of v3, /device:TPU:1, one launch (start us, length us, event | category | flops | bytes accessed | tf_op | source)
XLA Modules:
  0.0 211.4 jit_solution(1647057350673227382)
XLA Ops:
  0.6 0.7 fusion.27
  1.4 0.8 add_select_fusion.4
  2.4 0.9 select_reduce_fusion.1
  3.6 4.5 %shard_map.105 = bf16[1024,2048]{1,0:T(8,128)(2,1)S(1)} custom-call(s32[1,512]{1,0:T(1,128)S(1)} %get-tuple-element.219.slot_ref, bf16[512,4096]{1,0:T(8,128)(2,1)} %bitcast.76), custom_call_target="tpu_custom_call" | custom-call | flops 2147483648 | bytes 6291456 | tf_op jit(solution)/shard_map/pallas_call | solution.py:45
  8.1 2.0 copy-done
  10.1 8.6 %all-to-all-start.1 = ((bf16[32,32,2048]{2,1,0:T(8,128)(2,1)}), bf16[32,32,2048]{2,1,0:T(8,128)(2,1)}, u32[]{:S(2)}, u32[]{:S(2)}) async-start(bf16[32,32,2048]{2,1,0:T(8,128)(2,1)} %bitcast.71), calls=%async_computation.1 | async-start | bytes 8388608 | tf_op jit(solution)/shard_map/all_to_all | solution.py:284
  18.8 5.5 %shard_map.104 = (bf16[88,2048]{1,0:T(8,128)(2,1)S(1)}, bf16[88,2048]{1,0:T(8,128)(2,1)S(1)}, bf16[88,2048]{1,0:T(8,128)(2,1)S(1)}, bf16[88,2048]{1,0:T(8,128)(2...) custom-call(s32[1,512]{1,0:T(1,128)S(1)} %get-tuple-element.220.ring, ...), custom_call_target="tpu_custom_call" | custom-call | flops 1476395008 | bytes 4980736 | tf_op jit(solution)/shard_map/pallas_call | solution.py:96
  24.3 1.6 collective-permute-start
  25.9 3.0 %collective-permute-start.1 = (bf16[88,2048]{1,0:T(8,128)(2,1)S(1)}, bf16[88,2048]{1,0:T(8,128)(2,1)S(1)}, u32[]{:S(2)}, u32[]{:S(2)}) collective-permute-start(bf16[88,2048]{1,0:T(8,128)(2,1)S(1)} %get-tuple-element.103), channel_id=1, source_target_pairs={{0,16},{8,24},{16,32},{24,40},{32,48},{40,56},{48,0},{56,8},{1,17}... | collective-permute-start | bytes 1081352 | tf_op jit(solution)/shard_map/ppermute | solution.py:277
  28.9 3.8 %collective-permute-start.2 = (bf16[88,2048]{1,0:T(8,128)(2,1)}, bf16[88,2048]{1,0:T(8,128)(2,1)}, u32[]{:S(2)}, u32[]{:S(2)}) collective-permute-start(bf16[88,2048]{1,0:T(8,128)(2,1)} %get-tuple-element.109), channel_id=1, source_target_pairs={{0,24},{8,32},{16,40},{24,48},{32,56},{40,0},{48,8},{56,16},{1,25}... | collective-permute-start | bytes 1081352 | tf_op jit(solution)/shard_map/ppermute | solution.py:277
  33.1 4.5 %collective-permute-start.4 = (bf16[88,2048]{1,0:T(8,128)(2,1)}, bf16[88,2048]{1,0:T(8,128)(2,1)}, u32[]{:S(2)}, u32[]{:S(2)}) collective-permute-start(bf16[88,2048]{1,0:T(8,128)(2,1)} %get-tuple-element.111), channel_id=1, source_target_pairs={{0,40},{8,48},{16,56},{24,0},{32,8},{40,16},{48,24},{56,32},{1,41}... | collective-permute-start | bytes 1081352 | tf_op jit(solution)/shard_map/ppermute | solution.py:277
  38.0 0.7 and_reduce_fusion
  40.2 2.5 %collective-permute-start.5 = (bf16[88,2048]{1,0:T(8,128)(2,1)S(1)}, bf16[88,2048]{1,0:T(8,128)(2,1)}, u32[]{:S(2)}, u32[]{:S(2)}) collective-permute-start(bf16[88,2048]{1,0:T(8,128)(2,1)S(1)} %get-tuple-element.112), channel_id=1, source_target_pairs={{0,48},{8,56},{16,0},{24,8},{32,16},{40,24},{48,32},{56,40},{1,49}... | collective-permute-start | bytes 1081352 | tf_op jit(solution)/shard_map/ppermute | solution.py:277
  42.7 5.1 %collective-permute-done.1.refs_2_ = bf16[88,2048]{1,0:T(8,128)(2,1)S(1)} collective-permute-done((bf16[88,2048]{1,0:T(8,128)(2,1)S(1)}, bf16[88,2048]{1,0:T(8,128)(2,1)S(1)}, u32[]{:S(2)}, u32[]{:S(2)}) %collective-permute-start.1) | collective-permute-done | bytes 360480 | tf_op jit(solution)/shard_map/ppermute | solution.py:277
  47.8 8.7 %collective-permute-start.6 = (bf16[88,2048]{1,0:T(8,128)(2,1)S(1)}, bf16[88,2048]{1,0:T(8,128)(2,1)}, u32[]{:S(2)}, u32[]{:S(2)}) collective-permute-start(bf16[88,2048]{1,0:T(8,128)(2,1)S(1)} %get-tuple-element.113), channel_id=1, source_target_pairs={{0,56},{8,0},{16,8},{24,16},{32,24},{40,32},{48,40},{56,48},{1,57}... | collective-permute-start | bytes 1081352 | tf_op jit(solution)/shard_map/ppermute | solution.py:277
  56.6 14.6 %all-to-all-done.1 = bf16[32,32,2048]{2,1,0:T(8,128)(2,1)} async-done(((bf16[32,32,2048]{2,1,0:T(8,128)(2,1)}), bf16[32,32,2048]{2,1,0:T(8,128)(2,1)}, u32[]{:S(2)}, u32[]{:S(2)}) %all-to-all-start.1) | async-done | bytes 4194336 | tf_op jit(solution)/shard_map/all_to_all | solution.py:284
  71.2 9.4 %shard_map.106 = (bf16[88,2048]{1,0:T(8,128)(2,1)}, bf16[88,2048]{1,0:T(8,128)(2,1)S(1)}, bf16[88,2048]{1,0:T(8,128)(2,1)S(1)}, bf16[88,2048]{1,0:T(8,128)(2,1)S...) custom-call(s32[1]{0:T(128)} %bitcast.4.z_ref, ...), custom_call_target="tpu_custom_call" | custom-call | flops 2952790016 | bytes 7077888 | tf_op jit(solution)/shard_map/pallas_call | solution.py:150
  80.6 0.7 copy-done.1
  81.3 0.7 copy-done.2
  82.1 0.5 slice.52
  83.4 0.8 copy.44
  84.2 13.9 %all-to-all-start.2 = ((f32[256,1,128]{2,1,0:T(1,128)}), f32[256,1,128]{2,1,0:T(1,128)S(1)}, u32[]{:S(2)}, u32[]{:S(2)}) async-start(f32[256,1,128]{2,1,0:T(1,128)} %copy.44), calls=%async_computation.2 | async-start | bytes 262144 | tf_op jit(solution)/shard_map/all_to_all | solution.py:371
  98.1 12.8 %all-to-all-done.2 = f32[256,1,128]{2,1,0:T(1,128)S(1)} async-done(((f32[256,1,128]{2,1,0:T(1,128)}), f32[256,1,128]{2,1,0:T(1,128)S(1)}, u32[]{:S(2)}, u32[]{:S(2)}) %all-to-all-start.2) | async-done | bytes 131104 | tf_op jit(solution)/shard_map/all_to_all | solution.py:371
  111.3 2.3 %gather_fusion = f32[512]{0:T(512)S(1)} fusion(f32[1024]{0:T(1024)S(1)} %reshape.326, s32[1024]{0:T(1024)S(1)} %pad_clamp_fusion.1), kind=kCustom, calls=%fused_computation | custom fusion | bytes 6144 | tf_op jit(solution)/shard_map/gather | solution.py:376
  113.6 2.3 %gather_fusion.1 = f32[512]{0:T(512)S(1)} fusion(f32[1024]{0:T(1024)S(1)} %reshape.326, s32[1024]{0:T(1024)S(1)} %pad_clamp_fusion), kind=kCustom, calls=%fused_computation.1 | custom fusion | bytes 6144 | tf_op jit(solution)/shard_map/gather | solution.py:376
  115.9 0.6 multiply_reduce_fusion
  117.1 0.7 reshape.325
  117.8 1.1 copy.46
  119.0 0.7 reshape.328
  119.7 1.1 copy.48
  121.0 0.9 collective-permute-start.7
  121.9 1.9 collective-permute-start.8
  123.8 1.0 copy-done.4
  124.7 8.1 %shard_map.107 = bf16[1024,2048]{1,0:T(8,128)(2,1)} custom-call(s32[1]{0:T(128)} %bitcast.4.z_ref, bf16[88,2048]{1,0:T(8,128)(2,1)S(1)} %copy-done.4, bf16[88,2048]{1,0:T(8,128)(2,1)S(1)} %collective-permute-done.refs_1_, bf16[88,2048]{1,0:T(8,128)(2,1)S(1)} %collective-permute-done.1.refs_2_, bf16[88,2048]{1,0:T(8,128)(2,1)} %collective-permute-done.2.refs_3_, ...), custom_call_target="tpu_custom_call" | custom-call | flops 4294967296 | bytes 7077888 | tf_op jit(solution)/shard_map/pallas_call | solution.py:202
  132.8 0.8 copy-done.16
  133.6 0.8 copy-done.18
  134.4 5.6 %all-to-all-start.3 = ((bf16[32,32,2048]{2,1,0:T(8,128)(2,1)}), bf16[32,32,2048]{2,1,0:T(8,128)(2,1)}, u32[]{:S(2)}, u32[]{:S(2)}) async-start(bf16[32,32,2048]{2,1,0:T(8,128)(2,1)} %bitcast.79), calls=%async_computation.3 | async-start | bytes 8388608 | tf_op jit(solution)/shard_map/all_to_all | solution.py:284
  140.2 4.3 %collective-permute-start.11 = (bf16[88,2048]{1,0:T(8,128)(2,1)S(1)}, bf16[88,2048]{1,0:T(8,128)(2,1)}, u32[]{:S(2)}, u32[]{:S(2)}) collective-permute-start(bf16[88,2048]{1,0:T(8,128)(2,1)S(1)} %get-tuple-element.130), channel_id=1, source_target_pairs={{0,32},{8,40},{16,48},{24,56},{32,0},{40,8},{48,16},{56,24},{1,33}... | collective-permute-start | bytes 1081352 | tf_op jit(solution)/shard_map/ppermute | solution.py:277
  144.4 1.5 collective-permute-start.12
  145.9 1.9 collective-permute-start.13
  147.8 0.5 collective-permute-start.9
  148.5 0.6 fusion.32
  150.1 0.5 add_add_fusion.1
  150.6 42.0 %all-to-all-done.3 = bf16[32,32,2048]{2,1,0:T(8,128)(2,1)} async-done(((bf16[32,32,2048]{2,1,0:T(8,128)(2,1)}), bf16[32,32,2048]{2,1,0:T(8,128)(2,1)}, u32[]{:S(2)}, u32[]{:S(2)}) %all-to-all-start.3) | async-done | bytes 4194336 | tf_op jit(solution)/shard_map/all_to_all | solution.py:284
  192.6 6.1 %shard_map.108 = bf16[501,4096]{1,0:T(8,128)(2,1)} custom-call(s32[1,1024]{1,0:T(1,128)S(1)} %broadcast_in_dim_reshape.7.target_ref, f32[1024,1]{1,0:T(8,128)S(1)} %copy.49.scale_ref, bf16[1024,2048]{1,0:T(8,128)(2,1)} %bitcast.21.rows_ref), custom_call_target="tpu_custom_call" | custom-call | flops 2101346304 | bytes 6246400 | tf_op jit(solution)/shard_map/pallas_call | solution.py:231
  198.7 2.1 collective-permute-done.13
  200.8 10.5 %conditional.1 = (bf16[501,4096]{1,0:T(8,128)(2,1)}) conditional(s32[]{:T(128)} %convert_element_type.47, (s32[1,1024]{1,0:T(1,128)S(1)}, f32[1024,1]{0,1:T(1,128)S(1)}, s32[1]{0:T(128)}, bf16[88,2048]{1,0:T(8,128)(2,1)}, bf16[88,2048]{1,0:T(8,128)(2,1)S(1)}, /*index=5*/bf16[88,2048]{1,0:T(8,128)(2,1)}, bf16[88,2048]{1,0:T(8,128)(2,1)}, ...), branch_computations={%region_9.10_spmd, %region_10.11_spmd} | conditional | flops 8497661952 | bytes 83839016 | solution.py:419
  201.3 10.1 %branch_0_fun.1 = bf16[501,4096]{1,0:T(8,128)(2,1)} custom-call(s32[1,1024]{1,0:T(1,128)S(1)} %get-tuple-element.48.target_ref, f32[1024,1]{1,0:T(8,128)S(1)} %copy.50.scale_ref, s32[1]{0:T(128)} %get-tuple-element.50.z_ref, bf16[88,2048]{1,0:T(8,128)(2,1)} %get-tuple-element.51.refs_0_, ...), custom_call_target="tpu_custom_call", output_to_operand_aliasing={{}: (11, {})} | custom-call | flops 6396313600 | bytes 6246400 | tf_op jit(solution)/shard_map/cond/branch_0_fun/pallas_call | solution.py:256
  (84 shorter events, 4.5 us)
Async XLA Ops:
  8.1 2.0 copy-start
  10.1 61.1 %all-to-all-start.1 = ((bf16[32,32,2048]{2,1,0:T(8,128)(2,1)}), bf16[32,32,2048]{2,1,0:T(8,128)(2,1)}, u32[]{:S(2)}, u32[]{:S(2)}) async-start(bf16[32,32,2048]{2,1,0:T(8,128)(2,1)} %bitcast.71), calls=%async_computation.1 | async-start | bytes 8388608 | tf_op jit(solution)/shard_map/all_to_all | solution.py:284
  18.7 18.9 %copy-start.5 = (bf16[4,4096]{1,0:T(4,128)(2,1)S(1)}, bf16[4,4096]{1,0:T(4,128)(2,1)}, u32[]{:S(2)}) copy-start(bf16[4,4096]{1,0:T(4,128)(2,1)} %param.13) | copy-start | bytes 98308
  18.7 19.3 %copy-start.12 = (s32[4]{0:T(128)S(1)}, s32[4]{0:T(128)}, u32[]{:S(2)}) copy-start(s32[4]{0:T(128)} %param.14) | copy-start | bytes 52
  18.7 21.2 %copy-start.6 = (f32[4096]{0:T(1024)S(1)}, f32[4096]{0:T(1024)}, u32[]{:S(2)}) copy-start(f32[4096]{0:T(1024)} %param.16) | copy-start | bytes 49156
  18.7 21.2 %copy-start.7 = (f32[4096]{0:T(1024)S(1)}, f32[4096]{0:T(1024)}, u32[]{:S(2)}) copy-start(f32[4096]{0:T(1024)} %param.15) | copy-start | bytes 49156
  18.8 21.5 %copy-start.14 = (s32[512]{0:T(512)S(1)}, s32[512]{0:T(512)}, u32[]{:S(2)}) copy-start(s32[512]{0:T(512)} %param.17) | copy-start | bytes 6148
  24.2 47.0 %copy-start.3 = (bf16[88,2048]{1,0:T(8,128)(2,1)}, bf16[88,2048]{1,0:T(8,128)(2,1)S(1)}, u32[]{:S(2)}) copy-start(bf16[88,2048]{1,0:T(8,128)(2,1)S(1)} %get-tuple-element.117.refs_0_) | copy-start | bytes 1081348
  24.3 16.0 %collective-permute-start = (bf16[88,2048]{1,0:T(8,128)(2,1)S(1)}, bf16[88,2048]{1,0:T(8,128)(2,1)S(1)}, u32[]{:S(2)}, u32[]{:S(2)}) collective-permute-start(bf16[88,2048]{1,0:T(8,128)(2,1)S(1)} %get-tuple-element.102), channel_id=1, source_target_pairs={{0,8},{8,16},{16,24},{24,32},{32,40},{40,48},{48,56},{56,0},{1,9},... | collective-permute-start | bytes 1081352 | tf_op jit(solution)/shard_map/ppermute | solution.py:277
  25.9 21.9 %collective-permute-start.1 = (bf16[88,2048]{1,0:T(8,128)(2,1)S(1)}, bf16[88,2048]{1,0:T(8,128)(2,1)S(1)}, u32[]{:S(2)}, u32[]{:S(2)}) collective-permute-start(bf16[88,2048]{1,0:T(8,128)(2,1)S(1)} %get-tuple-element.103), channel_id=1, source_target_pairs={{0,16},{8,24},{16,32},{24,40},{32,48},{40,56},{48,0},{56,8},{1,17}... | collective-permute-start | bytes 1081352 | tf_op jit(solution)/shard_map/ppermute | solution.py:277
  28.9 92.1 %collective-permute-start.2 = (bf16[88,2048]{1,0:T(8,128)(2,1)}, bf16[88,2048]{1,0:T(8,128)(2,1)}, u32[]{:S(2)}, u32[]{:S(2)}) collective-permute-start(bf16[88,2048]{1,0:T(8,128)(2,1)} %get-tuple-element.109), channel_id=1, source_target_pairs={{0,24},{8,32},{16,40},{24,48},{32,56},{40,0},{48,8},{56,16},{1,25}... | collective-permute-start | bytes 1081352 | tf_op jit(solution)/shard_map/ppermute | solution.py:277
  32.6 89.2 %collective-permute-start.3 = (bf16[88,2048]{1,0:T(8,128)(2,1)}, bf16[88,2048]{1,0:T(8,128)(2,1)}, u32[]{:S(2)}, u32[]{:S(2)}) collective-permute-start(bf16[88,2048]{1,0:T(8,128)(2,1)} %get-tuple-element.110), channel_id=1, source_target_pairs={{0,32},{8,40},{16,48},{24,56},{32,0},{40,8},{48,16},{56,24},{1,33}... | collective-permute-start | bytes 1081352 | tf_op jit(solution)/shard_map/ppermute | solution.py:277
  33.1 90.6 %collective-permute-start.4 = (bf16[88,2048]{1,0:T(8,128)(2,1)}, bf16[88,2048]{1,0:T(8,128)(2,1)}, u32[]{:S(2)}, u32[]{:S(2)}) collective-permute-start(bf16[88,2048]{1,0:T(8,128)(2,1)} %get-tuple-element.111), channel_id=1, source_target_pairs={{0,40},{8,48},{16,56},{24,0},{32,8},{40,16},{48,24},{56,32},{1,41}... | collective-permute-start | bytes 1081352 | tf_op jit(solution)/shard_map/ppermute | solution.py:277
  40.2 83.5 %collective-permute-start.5 = (bf16[88,2048]{1,0:T(8,128)(2,1)S(1)}, bf16[88,2048]{1,0:T(8,128)(2,1)}, u32[]{:S(2)}, u32[]{:S(2)}) collective-permute-start(bf16[88,2048]{1,0:T(8,128)(2,1)S(1)} %get-tuple-element.112), channel_id=1, source_target_pairs={{0,48},{8,56},{16,0},{24,8},{32,16},{40,24},{48,32},{56,40},{1,49}... | collective-permute-start | bytes 1081352 | tf_op jit(solution)/shard_map/ppermute | solution.py:277
  47.8 75.9 %collective-permute-start.6 = (bf16[88,2048]{1,0:T(8,128)(2,1)S(1)}, bf16[88,2048]{1,0:T(8,128)(2,1)}, u32[]{:S(2)}, u32[]{:S(2)}) collective-permute-start(bf16[88,2048]{1,0:T(8,128)(2,1)S(1)} %get-tuple-element.113), channel_id=1, source_target_pairs={{0,56},{8,0},{16,8},{24,16},{32,24},{40,32},{48,40},{56,48},{1,57}... | collective-permute-start | bytes 1081352 | tf_op jit(solution)/shard_map/ppermute | solution.py:277
  71.2 26.9 %copy-start.15 = (s32[512]{0:T(512)S(1)}, s32[512]{0:T(512)}, u32[]{:S(2)}) copy-start(s32[512]{0:T(512)} %param.18) | copy-start | bytes 6148
  80.6 0.7 copy-start.1
  81.3 0.7 copy-start.2
  84.2 26.8 %all-to-all-start.2 = ((f32[256,1,128]{2,1,0:T(1,128)}), f32[256,1,128]{2,1,0:T(1,128)S(1)}, u32[]{:S(2)}, u32[]{:S(2)}) async-start(f32[256,1,128]{2,1,0:T(1,128)} %copy.44), calls=%async_computation.2 | async-start | bytes 262144 | tf_op jit(solution)/shard_map/all_to_all | solution.py:371
  117.0 1.9 copy-start.10
  117.0 3.8 %copy-start.8 = (f32[256]{0:T(256)}, f32[256]{0:T(256)S(1)}, u32[]{:S(2)}) copy-start(f32[256]{0:T(256)S(1)} %get-tuple-element.203) | copy-start | bytes 3076
  121.0 11.8 %collective-permute-start.7 = (bf16[88,2048]{1,0:T(8,128)(2,1)}, bf16[88,2048]{1,0:T(8,128)(2,1)S(1)}, u32[]{:S(2)}, u32[]{:S(2)}) collective-permute-start(bf16[88,2048]{1,0:T(8,128)(2,1)} %copy-done.2), channel_id=1, source_target_pairs={{0,8},{8,16},{16,24},{24,32},{32,40},{40,48},{48,56},{56,0},{1,9},... | collective-permute-start | bytes 1081352 | tf_op jit(solution)/shard_map/ppermute | solution.py:277
  121.9 11.0 %collective-permute-start.8 = (bf16[88,2048]{1,0:T(8,128)(2,1)}, bf16[88,2048]{1,0:T(8,128)(2,1)S(1)}, u32[]{:S(2)}, u32[]{:S(2)}) collective-permute-start(bf16[88,2048]{1,0:T(8,128)(2,1)} %copy-done.1), channel_id=1, source_target_pairs={{0,56},{8,0},{16,8},{24,16},{32,24},{40,32},{48,40},{56,48},{1,57}... | collective-permute-start | bytes 1081352 | tf_op jit(solution)/shard_map/ppermute | solution.py:277
  123.7 1.0 copy-start.4
  132.8 0.8 copy-start.16
  133.6 0.8 copy-start.18
  134.4 15.4 %copy-start.13 = (s32[4]{0:T(128)S(1)}, s32[4]{0:T(128)}, u32[]{:S(2)}) copy-start(s32[4]{0:T(128)} %param.14) | copy-start | bytes 52
  134.4 15.5 %copy-start.9 = (f32[256]{0:T(256)S(1)}, f32[256]{0:T(256)}, u32[]{:S(2)}) copy-start(f32[256]{0:T(256)} %copy-done.8) | copy-start | bytes 3076
  134.4 15.5 %copy-start.11 = (f32[256]{0:T(256)S(1)}, f32[256]{0:T(256)}, u32[]{:S(2)}) copy-start(f32[256]{0:T(256)} %copy-done.10) | copy-start | bytes 3076
  134.4 58.2 %all-to-all-start.3 = ((bf16[32,32,2048]{2,1,0:T(8,128)(2,1)}), bf16[32,32,2048]{2,1,0:T(8,128)(2,1)}, u32[]{:S(2)}, u32[]{:S(2)}) async-start(bf16[32,32,2048]{2,1,0:T(8,128)(2,1)} %bitcast.79), calls=%async_computation.3 | async-start | bytes 8388608 | tf_op jit(solution)/shard_map/all_to_all | solution.py:284
  140.1 58.6 %collective-permute-start.10 = (bf16[88,2048]{1,0:T(8,128)(2,1)S(1)}, bf16[88,2048]{1,0:T(8,128)(2,1)}, u32[]{:S(2)}, u32[]{:S(2)}) collective-permute-start(bf16[88,2048]{1,0:T(8,128)(2,1)S(1)} %get-tuple-element.129), channel_id=1, source_target_pairs={{0,24},{8,32},{16,40},{24,48},{32,56},{40,0},{48,8},{56,16},{1,25}... | collective-permute-start | bytes 1081352 | tf_op jit(solution)/shard_map/ppermute | solution.py:277
  140.2 58.5 %collective-permute-start.11 = (bf16[88,2048]{1,0:T(8,128)(2,1)S(1)}, bf16[88,2048]{1,0:T(8,128)(2,1)}, u32[]{:S(2)}, u32[]{:S(2)}) collective-permute-start(bf16[88,2048]{1,0:T(8,128)(2,1)S(1)} %get-tuple-element.130), channel_id=1, source_target_pairs={{0,32},{8,40},{16,48},{24,56},{32,0},{40,8},{48,16},{56,24},{1,33}... | collective-permute-start | bytes 1081352 | tf_op jit(solution)/shard_map/ppermute | solution.py:277
  144.4 54.3 %collective-permute-start.12 = (bf16[88,2048]{1,0:T(8,128)(2,1)S(1)}, bf16[88,2048]{1,0:T(8,128)(2,1)}, u32[]{:S(2)}, u32[]{:S(2)}) collective-permute-start(bf16[88,2048]{1,0:T(8,128)(2,1)S(1)} %get-tuple-element.131), channel_id=1, source_target_pairs={{0,40},{8,48},{16,56},{24,0},{32,8},{40,16},{48,24},{56,32},{1,41}... | collective-permute-start | bytes 1081352 | tf_op jit(solution)/shard_map/ppermute | solution.py:277
  145.9 54.9 %collective-permute-start.13 = (bf16[88,2048]{1,0:T(8,128)(2,1)S(1)}, bf16[88,2048]{1,0:T(8,128)(2,1)}, u32[]{:S(2)}, u32[]{:S(2)}) collective-permute-start(bf16[88,2048]{1,0:T(8,128)(2,1)S(1)} %get-tuple-element.132), channel_id=1, source_target_pairs={{0,48},{8,56},{16,0},{24,8},{32,16},{40,24},{48,32},{56,40},{1,49}... | collective-permute-start | bytes 1081352 | tf_op jit(solution)/shard_map/ppermute | solution.py:277
  147.8 53.0 %collective-permute-start.9 = (bf16[88,2048]{1,0:T(8,128)(2,1)S(1)}, bf16[88,2048]{1,0:T(8,128)(2,1)}, u32[]{:S(2)}, u32[]{:S(2)}) collective-permute-start(bf16[88,2048]{1,0:T(8,128)(2,1)S(1)} %get-tuple-element.128), channel_id=1, source_target_pairs={{0,16},{8,24},{16,32},{24,40},{32,48},{40,56},{48,0},{56,8},{1,17}... | collective-permute-start | bytes 1081352 | tf_op jit(solution)/shard_map/ppermute | solution.py:277
  192.6 8.2 %copy-start.17 = (bf16[88,2048]{1,0:T(8,128)(2,1)S(1)}, bf16[88,2048]{1,0:T(8,128)(2,1)}, u32[]{:S(2)}) copy-start(bf16[88,2048]{1,0:T(8,128)(2,1)} %copy-done.16) | copy-start | bytes 1081348
  192.6 8.2 %copy-start.19 = (bf16[88,2048]{1,0:T(8,128)(2,1)S(1)}, bf16[88,2048]{1,0:T(8,128)(2,1)}, u32[]{:S(2)}) copy-start(bf16[88,2048]{1,0:T(8,128)(2,1)} %copy-done.18) | copy-start | bytes 1081348

commit v4 on v2

--- a/solution.py
+++ b/solution.py
@@ -214,16 +214,17 @@
     )(z, *parts)
 
 
-def placed(target, scale, rows, out_ref):
-    scaled = (scale * rows).astype(jnp.bfloat16)
-    hot = rows_of((out_ref.shape[0], target.shape[1])) == target
+def place_kernel(target_ref, scale_ref, rows_ref, out_ref, hot_ref, held_ref):
+    @pl.when(pl.program_id(0) == 0)
+    def _():
+        hot_ref[...] = (rows_of(hot_ref.shape) == target_ref[...]).astype(jnp.bfloat16)
+        held_ref[...] = jnp.broadcast_to(scale_ref[...], held_ref.shape)
+
+    scale = jnp.concatenate([held_ref[...]] * (BLOCK // 128), axis=1)
+    scaled = (scale * rows_ref[...].astype(jnp.float32)).astype(jnp.bfloat16)
     out_ref[...] = jnp.dot(
-        hot.astype(jnp.bfloat16), scaled, preferred_element_type=jnp.float32
+        hot_ref[...], scaled, preferred_element_type=jnp.float32
     ).astype(jnp.bfloat16)
-
-
-def place_kernel(target_ref, scale_ref, rows_ref, out_ref):
-    placed(target_ref[...], scale_ref[...], rows_ref[...].astype(jnp.float32), out_ref)
 
 
 def placed_rows(target, scale, rows, shard_rows, out_width):
@@ -238,37 +239,82 @@
             pl.BlockSpec((slots, BLOCK), lambda j: (0, j)),
         ],
         out_specs=pl.BlockSpec((shard_rows, BLOCK), lambda j: (0, j)),
+        scratch_shapes=[
+            pltpu.VMEM((shard_rows, slots), jnp.bfloat16),
+            pltpu.VMEM((slots, 128), jnp.float32),
+        ],
         compiler_params=VMEM,
         cost_estimate=cost(shard_rows * slots * width, (shard_rows + slots) * width),
     )(target, scale, rows)
 
 
-def ring_place_kernel(target_ref, scale_ref, z_ref, *refs):
-    ins, (_, out_ref, hot_ref, held_ref) = refs[:RING], refs[RING:]
-    placed(target_ref[...], scale_ref[...], spread(z_ref, ins, hot_ref, held_ref), out_ref)
-
-
-def ring_placed(target, scale, z, parts, half_done):
+def rounded(x):
+    return x.astype(jnp.bfloat16).astype(jnp.float32)
+
+
+def ring_place_kernel(z_ref, target_ref, scale_ref, *refs):
+    ins, (_, out_ref, hot_ref, held_ref, scaled_ref) = refs[:RING], refs[RING:]
+
+    @pl.when(pl.program_id(0) == 0)
+    def _():
+        scaled_ref[...] = jnp.zeros_like(scaled_ref)
+        row = rows_of((8, 128))
+        for k in range(RING):
+            code = ins[k][ROWS - 8 : ROWS, 0:128].astype(jnp.float32)[7:8, :].astype(jnp.int32)
+            plane = (z_ref[0] - k) & 7
+            listed = (rows_of((128, 128)) == code - 1).astype(jnp.bfloat16)
+            target = target_ref[pl.ds(plane, 1), :] + 1
+            scale = scale_ref[pl.ds(plane, 1), :]
+            high = rounded(scale)
+            middle = rounded(scale - high)
+            low = scale - high - middle
+            parts = [(target >> 4).astype(jnp.float32), (target & 15).astype(jnp.float32)]
+            parts += [high, middle, low]
+            table = jnp.zeros((8, 128), jnp.float32)
+            for r, part in enumerate(parts):
+                table = jnp.where(row == r, part, table)
+            found = jnp.dot(
+                table.astype(jnp.bfloat16), listed, preferred_element_type=jnp.float32
+            )
+            place = (found[0:1, :] * 16 + found[1:2, :]).astype(jnp.int32) - 1
+            hot_ref[:, 128 * k : 128 * k + 128] = (
+                rows_of((out_ref.shape[0], 128)) == place
+            ).astype(jnp.bfloat16)
+            weight = found[2:3, :] + found[3:4, :] + found[4:5, :]
+            held_ref[128 * k : 128 * k + 128, :] = jnp.broadcast_to(weight, (128, 128)).T
+
+    for k in range(RING):
+        scale = held_ref[128 * k : 128 * k + ROWS, :]
+        for c in range(0, BLOCK, 128):
+            rows = ins[k][:, c : c + 128].astype(jnp.float32)
+            scaled_ref[128 * k : 128 * k + ROWS, c : c + 128] = (scale * rows).astype(jnp.bfloat16)
+    out_ref[...] = jnp.dot(
+        hot_ref[...], scaled_ref[...], preferred_element_type=jnp.float32
+    ).astype(jnp.bfloat16)
+
+
+def ring_placed(z, target, scale, parts, half_done):
     shard_rows, out_width = half_done.shape
-    slots = target.shape[1]
     width = parts[0].shape[1]
     skip = (out_width - width) // BLOCK
     return pl.pallas_call(
         ring_place_kernel,
         out_shape=jax.ShapeDtypeStruct(half_done.shape, jnp.bfloat16),
         grid=(width // BLOCK,),
-        in_specs=[whole((1, slots)), whole((slots, 1))]
-        + ring_specs()
+        in_specs=[pl.BlockSpec(memory_space=pltpu.SMEM)]
+        + [whole((RING, 128))] * 2
+        + [pl.BlockSpec((ROWS, BLOCK), lambda j: (0, j))] * RING
         + [pl.BlockSpec(memory_space=pl.ANY)],
         out_specs=pl.BlockSpec((shard_rows, BLOCK), lambda j: (0, skip + j)),
         scratch_shapes=[
-            pltpu.VMEM((slots, 128 * RING), jnp.bfloat16),
+            pltpu.VMEM((shard_rows, 128 * RING), jnp.bfloat16),
+            pltpu.VMEM((128 * RING, 128), jnp.float32),
             pltpu.VMEM((128 * RING, BLOCK), jnp.bfloat16),
         ],
         input_output_aliases={3 + RING: 0},
         compiler_params=VMEM,
-        cost_estimate=cost((shard_rows + 1024) * slots * width, (shard_rows + slots) * width),
-    )(target, scale, z, *parts, half_done)
+        cost_estimate=cost(shard_rows * 1024 * width, (shard_rows + 704) * width),
+    )(z, target, scale, *parts, half_done)
 
 
 def ring_shifted(parts):
@@ -288,6 +334,10 @@
 
 def slot_order(table):
     return table.reshape(4, RING, 8, CAP).swapaxes(1, 2).reshape(-1)
+
+
+def ring_order(table):
+    return table.reshape(4, RING, 8, CAP).swapaxes(0, 1).reshape(RING, -1)
 
 
 def count_earlier(key, counts):
@@ -345,6 +395,7 @@
     first = ring_shifted(first)
     second_slot = jnp.where(live, (column << 5) + (plane << 2) + rank, -1)
     second = in_plane(packed_rows(second_slot[None, :], rows, slots, half, half))
+    first[1], first[2], second = lax.optimization_barrier((first[1], first[2], second))
     second, over_there = ring_repacked(z, second)
     second = ring_shifted(second)
 
@@ -369,7 +420,9 @@
     )
     heard = lax.all_to_all(message, GRP_DEV, split_axis=0, concat_axis=0, tiled=True)
 
-    first = in_plane(ring_spread(z, first, slots))
+    first = ring_spread(z, first, slots)
+    first, second[1], second[7] = lax.optimization_barrier((first, second[1], second[7]))
+    first = in_plane(first)
 
     arrived_code = heard[:, :CAP].astype(jnp.int32)
     reward = heard[:, 4:8].reshape(responses)
@@ -398,7 +451,7 @@
     half_done = placed_rows(target_row, scale_column, first, shard_rows, width)
 
     def by_ring():
-        return ring_placed(target_row, scale_column, z, second, half_done)
+        return ring_placed(z, ring_order(target), ring_order(scale), second, half_done)
 
     def direct():
         sent = packed_rows(

time: 203 us -> 192 us (0.946)
  waiting for transfers between devices: 60.7 us -> 56.4 us
  Pallas kernels: 43.5 us -> 40.3 us
  starting transfers between devices: 72.9 us -> 69.9 us
    ppermute x14, waiting for transfers between devices: 37.4 us -> 9.5 us  [ring_shifted(): lax.ppermute(parts[k], 'dev_0', [(i, (i + k) % RING) for i in range(RING)])]
    all_to_all x2, waiting for transfers between devices: 20.6 us -> 46.9 us  [in_plane(): lax.all_to_all(parts, PLANE, split_axis=0, concat_axis=0, tiled=True)]
    ppermute x14, starting transfers between devices: 47.7 us -> 39.7 us  [ring_shifted(): lax.ppermute(parts[k], 'dev_0', [(i, (i + k) % RING) for i in range(RING)])]
    pallas_call x1, Pallas kernels: 10.1 us -> 6.5 us  [ring_placed(): pl.pallas_call(ring_place_kernel, out_shape=jax.ShapeDtypeStruct(half_don...]
    all_to_all x1, waiting for transfers between devices: 2.77 us -> 0.01 us  [local(): lax.all_to_all(message, GRP_DEV, split_axis=0, concat_axis=0, tiled=True)]
    all_to_all x2, starting transfers between devices: 13.7 us -> 16.4 us  [in_plane(): lax.all_to_all(parts, PLANE, split_axis=0, concat_axis=0, tiled=True)]
    all_to_all x1, starting transfers between devices: 11.5 us -> 13.9 us  [local(): lax.all_to_all(message, GRP_DEV, split_axis=0, concat_axis=0, tiled=True)]
    unnamed x22 -> x28, local copies, waits for them, and re-layouts: 5.46 us -> 5.22 us
  transfers between devices with their start and end apart: 17 -> 17, of which waited for: 7 -> 5; matrix products, arithmetic and copies ran while one was open for 6% -> 6% of each run, Pallas kernels for 14% -> 15%
where the time goes in v4:
time: 192 us; the launch traced here: 191 us
  starting transfers between devices  69.9 us (36%)
  waiting for transfers between devices  56.4 us (29%)
  Pallas kernels  40.3 us (21%)
  local copies, waits for them, and re-layouts  14.5 us (8%)
  other arithmetic  6.44 us (3%)
  between operations  2.96 us (2%)
    all_to_all x2, waiting for transfers between devices, in_plane(): lax.all_to_all(parts, PLANE, split_axis=0, concat_axis=0, tiled=True)  46.9 us
    ppermute x14, starting transfers between devices, ring_shifted(): lax.ppermute(parts[k], 'dev_0', [(i, (i + k) % RING) for i in range(RING)])  39.7 us
    all_to_all x2, starting transfers between devices, in_plane(): lax.all_to_all(parts, PLANE, split_axis=0, concat_axis=0, tiled=True)  16.4 us
    all_to_all x1, starting transfers between devices, local(): lax.all_to_all(message, GRP_DEV, split_axis=0, concat_axis=0, tiled=True)  13.9 us
    ppermute x14, waiting for transfers between devices, ring_shifted(): lax.ppermute(parts[k], 'dev_0', [(i, (i + k) % RING) for i in range(RING)])  9.5 us
    pallas_call x1, Pallas kernels, ring_repacked(): pl.pallas_call(ring_repack_kernel, out_shape=[jax.ShapeDtypeStruct((ROWS,...  9.41 us
    pallas_call x1, Pallas kernels, ring_spread(): pl.pallas_call(ring_spread_kernel, out_shape=jax.ShapeDtypeStruct((slots,...  8.08 us
    pallas_call x1, Pallas kernels, ring_placed(): pl.pallas_call(ring_place_kernel, out_shape=jax.ShapeDtypeStruct(half_don...  6.5 us
  transfers between devices with their start and end apart: 17, of which 5 were waited for; matrix products, arithmetic and copies ran while one was open for 6% of the time, Pallas kernels for 15%

profile of v4, /device:TPU:1, one launch (start us, length us, event | category | flops | bytes accessed | tf_op | source)
XLA Modules:
  0.0 190.9 jit_solution(18048091722281077984)
XLA Ops:
  0.6 0.7 fusion.27
  1.4 0.8 add_select_fusion.4
  2.4 0.9 select_reduce_fusion.1
  3.3 0.3 convert_reduce_fusion
  3.6 4.5 %shard_map.105 = bf16[1024,2048]{1,0:T(8,128)(2,1)S(1)} custom-call(s32[1,512]{1,0:T(1,128)S(1)} %get-tuple-element.206.slot_ref, bf16[512,4096]{1,0:T(8,128)(2,1)} %bitcast.84), custom_call_target="tpu_custom_call" | custom-call | flops 2147483648 | bytes 6291456 | tf_op jit(solution)/shard_map/pallas_call | solution.py:45
  8.1 2.0 %copy-done = bf16[1024,2048]{1,0:T(8,128)(2,1)} copy-done((bf16[1024,2048]{1,0:T(8,128)(2,1)}, bf16[1024,2048]{1,0:T(8,128)(2,1)S(1)}, u32[]{:S(2)}) %copy-start) | copy-done | bytes 4194328
  10.1 8.6 %all-to-all-start.1 = ((bf16[32,32,2048]{2,1,0:T(8,128)(2,1)}), bf16[32,32,2048]{2,1,0:T(8,128)(2,1)}, u32[]{:S(2)}, u32[]{:S(2)}) async-start(bf16[32,32,2048]{2,1,0:T(8,128)(2,1)} %bitcast.79), calls=%async_computation.1 | async-start | bytes 8388608 | tf_op jit(solution)/shard_map/all_to_all | solution.py:330
  18.8 5.5 %shard_map.104 = (bf16[88,2048]{1,0:T(8,128)(2,1)S(1)}, bf16[88,2048]{1,0:T(8,128)(2,1)S(1)}, bf16[88,2048]{1,0:T(8,128)(2,1)S(1)}, bf16[88,2048]{1,0:T(8,128)(2...) custom-call(s32[1,512]{1,0:T(1,128)S(1)} %get-tuple-element.207.ring, ...), custom_call_target="tpu_custom_call" | custom-call | flops 1476395008 | bytes 4980736 | tf_op jit(solution)/shard_map/pallas_call | solution.py:96
  24.2 1.6 collective-permute-start
  25.9 3.0 %collective-permute-start.1 = (bf16[88,2048]{1,0:T(8,128)(2,1)S(1)}, bf16[88,2048]{1,0:T(8,128)(2,1)S(1)}, u32[]{:S(2)}, u32[]{:S(2)}) collective-permute-start(bf16[88,2048]{1,0:T(8,128)(2,1)S(1)} %get-tuple-element.93), channel_id=1, source_target_pairs={{0,16},{8,24},{16,32},{24,40},{32,48},{40,56},{48,0},{56,8},{1,17}... | collective-permute-start | bytes 1081352 | tf_op jit(solution)/shard_map/ppermute | solution.py:323
  28.8 3.8 %collective-permute-start.2 = (bf16[88,2048]{1,0:T(8,128)(2,1)}, bf16[88,2048]{1,0:T(8,128)(2,1)}, u32[]{:S(2)}, u32[]{:S(2)}) collective-permute-start(bf16[88,2048]{1,0:T(8,128)(2,1)} %get-tuple-element.100), channel_id=1, source_target_pairs={{0,24},{8,32},{16,40},{24,48},{32,56},{40,0},{48,8},{56,16},{1,25}... | collective-permute-start | bytes 1081352 | tf_op jit(solution)/shard_map/ppermute | solution.py:323
  32.6 0.5 collective-permute-start.3
  33.1 4.5 %collective-permute-start.4 = (bf16[88,2048]{1,0:T(8,128)(2,1)}, bf16[88,2048]{1,0:T(8,128)(2,1)}, u32[]{:S(2)}, u32[]{:S(2)}) collective-permute-start(bf16[88,2048]{1,0:T(8,128)(2,1)} %get-tuple-element.102), channel_id=1, source_target_pairs={{0,40},{8,48},{16,56},{24,0},{32,8},{40,16},{48,24},{56,32},{1,41}... | collective-permute-start | bytes 1081352 | tf_op jit(solution)/shard_map/ppermute | solution.py:323
  37.7 0.3 select_reduce_fusion
  38.0 0.7 and_reduce_fusion
  40.2 2.5 %collective-permute-start.5 = (bf16[88,2048]{1,0:T(8,128)(2,1)S(1)}, bf16[88,2048]{1,0:T(8,128)(2,1)}, u32[]{:S(2)}, u32[]{:S(2)}) collective-permute-start(bf16[88,2048]{1,0:T(8,128)(2,1)S(1)} %get-tuple-element.103), channel_id=1, source_target_pairs={{0,48},{8,56},{16,0},{24,8},{32,16},{40,24},{48,32},{56,40},{1,49}... | collective-permute-start | bytes 1081352 | tf_op jit(solution)/shard_map/ppermute | solution.py:323
  42.6 5.1 %collective-permute-done.1.refs_2_ = bf16[88,2048]{1,0:T(8,128)(2,1)S(1)} collective-permute-done((bf16[88,2048]{1,0:T(8,128)(2,1)S(1)}, bf16[88,2048]{1,0:T(8,128)(2,1)S(1)}, u32[]{:S(2)}, u32[]{:S(2)}) %collective-permute-start.1) | collective-permute-done | bytes 360480 | tf_op jit(solution)/shard_map/ppermute | solution.py:323
  47.8 8.7 %collective-permute-start.6 = (bf16[88,2048]{1,0:T(8,128)(2,1)S(1)}, bf16[88,2048]{1,0:T(8,128)(2,1)}, u32[]{:S(2)}, u32[]{:S(2)}) collective-permute-start(bf16[88,2048]{1,0:T(8,128)(2,1)S(1)} %get-tuple-element.104), channel_id=1, source_target_pairs={{0,56},{8,0},{16,8},{24,16},{32,24},{40,32},{48,40},{56,48},{1,57}... | collective-permute-start | bytes 1081352 | tf_op jit(solution)/shard_map/ppermute | solution.py:323
  56.5 14.7 %all-to-all-done.1 = bf16[32,32,2048]{2,1,0:T(8,128)(2,1)} async-done(((bf16[32,32,2048]{2,1,0:T(8,128)(2,1)}), bf16[32,32,2048]{2,1,0:T(8,128)(2,1)}, u32[]{:S(2)}, u32[]{:S(2)}) %all-to-all-start.1) | async-done | bytes 4194336 | tf_op jit(solution)/shard_map/all_to_all | solution.py:330
  71.2 9.4 %shard_map.106 = (bf16[88,2048]{1,0:T(8,128)(2,1)}, bf16[88,2048]{1,0:T(8,128)(2,1)S(1)}, bf16[88,2048]{1,0:T(8,128)(2,1)S(1)}, bf16[88,2048]{1,0:T(8,128)(2,1)S...) custom-call(s32[1]{0:T(128)} %bitcast.12.z_ref, ...), custom_call_target="tpu_custom_call" | custom-call | flops 2952790016 | bytes 7077888 | tf_op jit(solution)/shard_map/pallas_call | solution.py:150
  80.6 0.7 copy-done.1
  81.4 0.7 copy-done.2
  82.1 0.5 slice.52
  83.4 0.7 copy.80
  84.2 13.9 %all-to-all-start.2 = ((f32[256,1,128]{2,1,0:T(1,128)}), f32[256,1,128]{2,1,0:T(1,128)S(1)}, u32[]{:S(2)}, u32[]{:S(2)}) async-start(f32[256,1,128]{2,1,0:T(1,128)} %copy.80), calls=%async_computation.2 | async-start | bytes 262144 | tf_op jit(solution)/shard_map/all_to_all | solution.py:421
  98.1 1.6 collective-permute-start.7
  99.7 2.9 %collective-permute-start.8 = (bf16[88,2048]{1,0:T(8,128)(2,1)}, bf16[88,2048]{1,0:T(8,128)(2,1)}, u32[]{:S(2)}, u32[]{:S(2)}) collective-permute-start(bf16[88,2048]{1,0:T(8,128)(2,1)} %copy-done.1), channel_id=1, source_target_pairs={{0,56},{8,0},{16,8},{24,16},{32,24},{40,32},{48,40},{56,48},{1,57}... | collective-permute-start | bytes 1081352 | tf_op jit(solution)/shard_map/ppermute | solution.py:323
  102.6 1.0 copy-done.4
  103.6 8.1 %shard_map.107 = bf16[1024,2048]{1,0:T(8,128)(2,1)} custom-call(s32[1]{0:T(128)} %bitcast.12.z_ref, bf16[88,2048]{1,0:T(8,128)(2,1)S(1)} %copy-done.4, bf16[88,2048]{1,0:T(8,128)(2,1)S(1)} %collective-permute-done.refs_1_, bf16[88,2048]{1,0:T(8,128)(2,1)S(1)} %collective-permute-done.1.refs_2_, bf16[88,2048]{1,0:T(8,128)(2,1)} %collective-permute-done.2.refs_3_, ...), custom_call_target="tpu_custom_call" | custom-call | flops 4294967296 | bytes 7077888 | tf_op jit(solution)/shard_map/pallas_call | solution.py:202
  111.7 1.1 collective-permute-done.7
  112.8 0.8 copy-done.6
  113.6 7.7 %all-to-all-start.3 = ((bf16[32,32,2048]{2,1,0:T(8,128)(2,1)}), bf16[32,32,2048]{2,1,0:T(8,128)(2,1)}, u32[]{:S(2)}, u32[]{:S(2)}) async-start(bf16[32,32,2048]{2,1,0:T(8,128)(2,1)} %bitcast.87), calls=%async_computation.3 | async-start | bytes 8388608 | tf_op jit(solution)/shard_map/all_to_all | solution.py:330
  121.4 3.0 %collective-permute-start.10 = (bf16[88,2048]{1,0:T(8,128)(2,1)S(1)}, bf16[88,2048]{1,0:T(8,128)(2,1)}, u32[]{:S(2)}, u32[]{:S(2)}) collective-permute-start(bf16[88,2048]{1,0:T(8,128)(2,1)S(1)} %get-tuple-element.109), channel_id=1, source_target_pairs={{0,24},{8,32},{16,40},{24,48},{32,56},{40,0},{48,8},{56,16},{1,25}... | collective-permute-start | bytes 1081352 | tf_op jit(solution)/shard_map/ppermute | solution.py:323
  124.4 0.9 collective-permute-start.11
  125.4 4.4 %collective-permute-start.12 = (bf16[88,2048]{1,0:T(8,128)(2,1)S(1)}, bf16[88,2048]{1,0:T(8,128)(2,1)}, u32[]{:S(2)}, u32[]{:S(2)}) collective-permute-start(bf16[88,2048]{1,0:T(8,128)(2,1)S(1)} %get-tuple-element.111), channel_id=1, source_target_pairs={{0,40},{8,48},{16,56},{24,0},{32,8},{40,16},{48,24},{56,32},{1,41}... | collective-permute-start | bytes 1081352 | tf_op jit(solution)/shard_map/ppermute | solution.py:323
  129.7 0.4 collective-permute-start.13
  130.1 2.0 %collective-permute-start.9 = (bf16[88,2048]{1,0:T(8,128)(2,1)S(1)}, bf16[88,2048]{1,0:T(8,128)(2,1)}, u32[]{:S(2)}, u32[]{:S(2)}) collective-permute-start(bf16[88,2048]{1,0:T(8,128)(2,1)S(1)} %get-tuple-element.108), channel_id=1, source_target_pairs={{0,16},{8,24},{16,32},{24,40},{32,48},{40,56},{48,0},{56,8},{1,17}... | collective-permute-start | bytes 1081352 | tf_op jit(solution)/shard_map/ppermute | solution.py:323
  132.5 2.3 %gather_fusion = f32[512]{0:T(512)S(1)} fusion(f32[1024]{0:T(1024)S(1)} %reshape.337, s32[1024]{0:T(1024)S(1)} %pad_clamp_fusion.1), kind=kCustom, calls=%fused_computation | custom fusion | bytes 6144 | tf_op jit(solution)/shard_map/gather | solution.py:430
  134.8 2.3 %gather_fusion.1 = f32[512]{0:T(512)S(1)} fusion(f32[1024]{0:T(1024)S(1)} %reshape.337, s32[1024]{0:T(1024)S(1)} %pad_clamp_fusion), kind=kCustom, calls=%fused_computation.1 | custom fusion | bytes 6144 | tf_op jit(solution)/shard_map/gather | solution.py:430
  137.1 0.6 multiply_reduce_fusion
  137.8 0.3 slice_reduce_fusion.3
  139.2 0.6 fusion.32
  140.8 0.5 add_add_fusion.1
  141.3 32.2 %all-to-all-done.3 = bf16[32,32,2048]{2,1,0:T(8,128)(2,1)} async-done(((bf16[32,32,2048]{2,1,0:T(8,128)(2,1)}), bf16[32,32,2048]{2,1,0:T(8,128)(2,1)}, u32[]{:S(2)}, u32[]{:S(2)}) %all-to-all-start.3) | async-done | bytes 4194336 | tf_op jit(solution)/shard_map/all_to_all | solution.py:330
  173.5 6.4 %shard_map.108 = bf16[501,4096]{1,0:T(8,128)(2,1)} custom-call(s32[1,1024]{1,0:T(1,128)S(1)} %broadcast_in_dim_reshape.7.target_ref, f32[1024,1]{1,0:T(8,128)S(1)} %broadcast_in_dim_reshape.9.scale_ref, bf16[1024,2048]{1,0:T(8,128)(2,1)} %bitcast.29.rows_ref), custom_call_target="tpu_custom_call" | custom-call | flops 2101346304 | bytes 6246400 | tf_op jit(solution)/shard_map/pallas_call | solution.py:232
  179.9 3.2 %collective-permute-done.13 = bf16[88,2048]{1,0:T(8,128)(2,1)} collective-permute-done((bf16[88,2048]{1,0:T(8,128)(2,1)S(1)}, bf16[88,2048]{1,0:T(8,128)(2,1)}, u32[]{:S(2)}, u32[]{:S(2)}) %collective-permute-start.13) | collective-permute-done | bytes 360480 | tf_op jit(solution)/shard_map/ppermute | solution.py:323
  183.2 7.7 %conditional.1 = (bf16[501,4096]{1,0:T(8,128)(2,1)}) conditional(s32[]{:T(128)} %convert_element_type.47, (s32[256,4]{0,1:T(4,128)S(1)}, f32[256,4]{0,1:T(4,128)S(1)}, s32[1]{0:T(128)}, bf16[88,2048]{1,0:T(8,128)(2,1)S(1)}, bf16[88,2048]{1,0:T(8,128)(2,1)S(1)}, /*index=5*/bf16[88,2048]{1,0:T(8,128)(2,1)}, bf16[88,2048]{1,0:T(8,128)(2,1)}, ...), branch_computations={%region_9.10_spmd, %region_10.11_spmd} | conditional | flops 8497661952 | bytes 83839016 | solution.py:469
  184.4 6.5 %branch_0_fun.1 = bf16[501,4096]{1,0:T(8,128)(2,1)} custom-call(s32[1]{0:T(128)} %get-tuple-element.48.z_ref, s32[8,128]{1,0:T(8,128)S(1)} %copy.75.target_ref, f32[8,128]{1,0:T(8,128)S(1)} %copy.76.scale_ref, bf16[88,2048]{1,0:T(8,128)(2,1)S(1)} %get-tuple-element.51.refs_0_, ...), custom_call_target="tpu_custom_call", output_to_operand_aliasing={{}: (11, {})} | custom-call | flops 2101346304 | bytes 4935680 | tf_op jit(solution)/shard_map/cond/branch_0_fun/pallas_call | solution.py:300
  (76 shorter events, 4.3 us)
Async XLA Ops:
  8.1 2.0 %copy-start = (bf16[1024,2048]{1,0:T(8,128)(2,1)}, bf16[1024,2048]{1,0:T(8,128)(2,1)S(1)}, u32[]{:S(2)}) copy-start(bf16[1024,2048]{1,0:T(8,128)(2,1)S(1)} %shard_map.105) | copy-start | bytes 12582916
  10.1 61.1 %all-to-all-start.1 = ((bf16[32,32,2048]{2,1,0:T(8,128)(2,1)}), bf16[32,32,2048]{2,1,0:T(8,128)(2,1)}, u32[]{:S(2)}, u32[]{:S(2)}) async-start(bf16[32,32,2048]{2,1,0:T(8,128)(2,1)} %bitcast.79), calls=%async_computation.1 | async-start | bytes 8388608 | tf_op jit(solution)/shard_map/all_to_all | solution.py:330
  18.7 18.8 %copy-start.8 = (bf16[4,4096]{1,0:T(4,128)(2,1)S(1)}, bf16[4,4096]{1,0:T(4,128)(2,1)}, u32[]{:S(2)}) copy-start(bf16[4,4096]{1,0:T(4,128)(2,1)} %param.13) | copy-start | bytes 98308
  18.7 19.2 %copy-start.11 = (s32[4]{0:T(128)S(1)}, s32[4]{0:T(128)}, u32[]{:S(2)}) copy-start(s32[4]{0:T(128)} %param.14) | copy-start | bytes 52
  18.7 21.2 %copy-start.9 = (f32[4096]{0:T(1024)S(1)}, f32[4096]{0:T(1024)}, u32[]{:S(2)}) copy-start(f32[4096]{0:T(1024)} %param.16) | copy-start | bytes 49156
  18.8 21.2 %copy-start.10 = (f32[4096]{0:T(1024)S(1)}, f32[4096]{0:T(1024)}, u32[]{:S(2)}) copy-start(f32[4096]{0:T(1024)} %param.15) | copy-start | bytes 49156
  24.2 47.0 %copy-start.3 = (bf16[88,2048]{1,0:T(8,128)(2,1)}, bf16[88,2048]{1,0:T(8,128)(2,1)S(1)}, u32[]{:S(2)}) copy-start(bf16[88,2048]{1,0:T(8,128)(2,1)S(1)} %get-tuple-element.97.refs_0_) | copy-start | bytes 1081348
  24.2 16.0 %collective-permute-start = (bf16[88,2048]{1,0:T(8,128)(2,1)S(1)}, bf16[88,2048]{1,0:T(8,128)(2,1)S(1)}, u32[]{:S(2)}, u32[]{:S(2)}) collective-permute-start(bf16[88,2048]{1,0:T(8,128)(2,1)S(1)} %get-tuple-element.92), channel_id=1, source_target_pairs={{0,8},{8,16},{16,24},{24,32},{32,40},{40,48},{48,56},{56,0},{1,9},... | collective-permute-start | bytes 1081352 | tf_op jit(solution)/shard_map/ppermute | solution.py:323
  25.9 21.9 %collective-permute-start.1 = (bf16[88,2048]{1,0:T(8,128)(2,1)S(1)}, bf16[88,2048]{1,0:T(8,128)(2,1)S(1)}, u32[]{:S(2)}, u32[]{:S(2)}) collective-permute-start(bf16[88,2048]{1,0:T(8,128)(2,1)S(1)} %get-tuple-element.93), channel_id=1, source_target_pairs={{0,16},{8,24},{16,32},{24,40},{32,48},{40,56},{48,0},{56,8},{1,17}... | collective-permute-start | bytes 1081352 | tf_op jit(solution)/shard_map/ppermute | solution.py:323
  28.8 69.3 %collective-permute-start.2 = (bf16[88,2048]{1,0:T(8,128)(2,1)}, bf16[88,2048]{1,0:T(8,128)(2,1)}, u32[]{:S(2)}, u32[]{:S(2)}) collective-permute-start(bf16[88,2048]{1,0:T(8,128)(2,1)} %get-tuple-element.100), channel_id=1, source_target_pairs={{0,24},{8,32},{16,40},{24,48},{32,56},{40,0},{48,8},{56,16},{1,25}... | collective-permute-start | bytes 1081352 | tf_op jit(solution)/shard_map/ppermute | solution.py:323
  32.6 67.1 %collective-permute-start.3 = (bf16[88,2048]{1,0:T(8,128)(2,1)}, bf16[88,2048]{1,0:T(8,128)(2,1)}, u32[]{:S(2)}, u32[]{:S(2)}) collective-permute-start(bf16[88,2048]{1,0:T(8,128)(2,1)} %get-tuple-element.101), channel_id=1, source_target_pairs={{0,32},{8,40},{16,48},{24,56},{32,0},{40,8},{48,16},{56,24},{1,33}... | collective-permute-start | bytes 1081352 | tf_op jit(solution)/shard_map/ppermute | solution.py:323
  33.1 69.6 %collective-permute-start.4 = (bf16[88,2048]{1,0:T(8,128)(2,1)}, bf16[88,2048]{1,0:T(8,128)(2,1)}, u32[]{:S(2)}, u32[]{:S(2)}) collective-permute-start(bf16[88,2048]{1,0:T(8,128)(2,1)} %get-tuple-element.102), channel_id=1, source_target_pairs={{0,40},{8,48},{16,56},{24,0},{32,8},{40,16},{48,24},{56,32},{1,41}... | collective-permute-start | bytes 1081352 | tf_op jit(solution)/shard_map/ppermute | solution.py:323
  40.2 62.4 %collective-permute-start.5 = (bf16[88,2048]{1,0:T(8,128)(2,1)S(1)}, bf16[88,2048]{1,0:T(8,128)(2,1)}, u32[]{:S(2)}, u32[]{:S(2)}) collective-permute-start(bf16[88,2048]{1,0:T(8,128)(2,1)S(1)} %get-tuple-element.103), channel_id=1, source_target_pairs={{0,48},{8,56},{16,0},{24,8},{32,16},{40,24},{48,32},{56,40},{1,49}... | collective-permute-start | bytes 1081352 | tf_op jit(solution)/shard_map/ppermute | solution.py:323
  47.8 54.8 %collective-permute-start.6 = (bf16[88,2048]{1,0:T(8,128)(2,1)S(1)}, bf16[88,2048]{1,0:T(8,128)(2,1)}, u32[]{:S(2)}, u32[]{:S(2)}) collective-permute-start(bf16[88,2048]{1,0:T(8,128)(2,1)S(1)} %get-tuple-element.104), channel_id=1, source_target_pairs={{0,56},{8,0},{16,8},{24,16},{32,24},{40,32},{48,40},{56,48},{1,57}... | collective-permute-start | bytes 1081352 | tf_op jit(solution)/shard_map/ppermute | solution.py:323
  80.6 0.7 copy-start.1
  81.4 0.7 copy-start.2
  84.2 29.4 %all-to-all-start.2 = ((f32[256,1,128]{2,1,0:T(1,128)}), f32[256,1,128]{2,1,0:T(1,128)S(1)}, u32[]{:S(2)}, u32[]{:S(2)}) async-start(f32[256,1,128]{2,1,0:T(1,128)} %copy.80), calls=%async_computation.2 | async-start | bytes 262144 | tf_op jit(solution)/shard_map/all_to_all | solution.py:421
  98.1 14.7 %collective-permute-start.7 = (bf16[88,2048]{1,0:T(8,128)(2,1)}, bf16[88,2048]{1,0:T(8,128)(2,1)S(1)}, u32[]{:S(2)}, u32[]{:S(2)}) collective-permute-start(bf16[88,2048]{1,0:T(8,128)(2,1)} %copy-done.2), channel_id=1, source_target_pairs={{0,8},{8,16},{16,24},{24,32},{32,40},{40,48},{48,56},{56,0},{1,9},... | collective-permute-start | bytes 1081352 | tf_op jit(solution)/shard_map/ppermute | solution.py:323
  99.7 13.9 %collective-permute-start.8 = (bf16[88,2048]{1,0:T(8,128)(2,1)}, bf16[88,2048]{1,0:T(8,128)(2,1)}, u32[]{:S(2)}, u32[]{:S(2)}) collective-permute-start(bf16[88,2048]{1,0:T(8,128)(2,1)} %copy-done.1), channel_id=1, source_target_pairs={{0,56},{8,0},{16,8},{24,16},{32,24},{40,32},{48,40},{56,48},{1,57}... | collective-permute-start | bytes 1081352 | tf_op jit(solution)/shard_map/ppermute | solution.py:323
  102.6 1.0 copy-start.4
  112.8 0.8 copy-start.6
  113.6 7.8 %copy-start.12 = (s32[512]{0:T(512)S(1)}, s32[512]{0:T(512)}, u32[]{:S(2)}) copy-start(s32[512]{0:T(512)} %param.17) | copy-start | bytes 6148
  113.6 7.8 %copy-start.13 = (s32[512]{0:T(512)S(1)}, s32[512]{0:T(512)}, u32[]{:S(2)}) copy-start(s32[512]{0:T(512)} %param.18) | copy-start | bytes 6148
  113.6 59.9 %all-to-all-start.3 = ((bf16[32,32,2048]{2,1,0:T(8,128)(2,1)}), bf16[32,32,2048]{2,1,0:T(8,128)(2,1)}, u32[]{:S(2)}, u32[]{:S(2)}) async-start(bf16[32,32,2048]{2,1,0:T(8,128)(2,1)} %bitcast.87), calls=%async_computation.3 | async-start | bytes 8388608 | tf_op jit(solution)/shard_map/all_to_all | solution.py:330
  121.4 58.5 %collective-permute-start.10 = (bf16[88,2048]{1,0:T(8,128)(2,1)S(1)}, bf16[88,2048]{1,0:T(8,128)(2,1)}, u32[]{:S(2)}, u32[]{:S(2)}) collective-permute-start(bf16[88,2048]{1,0:T(8,128)(2,1)S(1)} %get-tuple-element.109), channel_id=1, source_target_pairs={{0,24},{8,32},{16,40},{24,48},{32,56},{40,0},{48,8},{56,16},{1,25}... | collective-permute-start | bytes 1081352 | tf_op jit(solution)/shard_map/ppermute | solution.py:323
  124.4 55.5 %collective-permute-start.11 = (bf16[88,2048]{1,0:T(8,128)(2,1)S(1)}, bf16[88,2048]{1,0:T(8,128)(2,1)}, u32[]{:S(2)}, u32[]{:S(2)}) collective-permute-start(bf16[88,2048]{1,0:T(8,128)(2,1)S(1)} %get-tuple-element.110), channel_id=1, source_target_pairs={{0,32},{8,40},{16,48},{24,56},{32,0},{40,8},{48,16},{56,24},{1,33}... | collective-permute-start | bytes 1081352 | tf_op jit(solution)/shard_map/ppermute | solution.py:323
  125.4 54.6 %collective-permute-start.12 = (bf16[88,2048]{1,0:T(8,128)(2,1)S(1)}, bf16[88,2048]{1,0:T(8,128)(2,1)}, u32[]{:S(2)}, u32[]{:S(2)}) collective-permute-start(bf16[88,2048]{1,0:T(8,128)(2,1)S(1)} %get-tuple-element.111), channel_id=1, source_target_pairs={{0,40},{8,48},{16,56},{24,0},{32,8},{40,16},{48,24},{56,32},{1,41}... | collective-permute-start | bytes 1081352 | tf_op jit(solution)/shard_map/ppermute | solution.py:323
  129.7 53.4 %collective-permute-start.13 = (bf16[88,2048]{1,0:T(8,128)(2,1)S(1)}, bf16[88,2048]{1,0:T(8,128)(2,1)}, u32[]{:S(2)}, u32[]{:S(2)}) collective-permute-start(bf16[88,2048]{1,0:T(8,128)(2,1)S(1)} %get-tuple-element.112), channel_id=1, source_target_pairs={{0,48},{8,56},{16,0},{24,8},{32,16},{40,24},{48,32},{56,40},{1,49}... | collective-permute-start | bytes 1081352 | tf_op jit(solution)/shard_map/ppermute | solution.py:323
  130.1 53.0 %collective-permute-start.9 = (bf16[88,2048]{1,0:T(8,128)(2,1)S(1)}, bf16[88,2048]{1,0:T(8,128)(2,1)}, u32[]{:S(2)}, u32[]{:S(2)}) collective-permute-start(bf16[88,2048]{1,0:T(8,128)(2,1)S(1)} %get-tuple-element.108), channel_id=1, source_target_pairs={{0,16},{8,24},{16,32},{24,40},{32,48},{40,56},{48,0},{56,8},{1,17}... | collective-permute-start | bytes 1081352 | tf_op jit(solution)/shard_map/ppermute | solution.py:323
  173.5 9.7 %copy-start.5 = (bf16[88,2048]{1,0:T(8,128)(2,1)S(1)}, bf16[88,2048]{1,0:T(8,128)(2,1)}, u32[]{:S(2)}) copy-start(bf16[88,2048]{1,0:T(8,128)(2,1)} %get-tuple-element.96) | copy-start | bytes 1081348
  173.5 9.7 %copy-start.7 = (bf16[88,2048]{1,0:T(8,128)(2,1)S(1)}, bf16[88,2048]{1,0:T(8,128)(2,1)}, u32[]{:S(2)}) copy-start(bf16[88,2048]{1,0:T(8,128)(2,1)} %copy-done.6) | copy-start | bytes 1081348

commit v5 on v4

--- a/solution.py
+++ b/solution.py
@@ -32,10 +32,13 @@
     return pl.BlockSpec(shape, lambda j: (0,) * len(shape))
 
 
-def pack_kernel(slot_ref, rows_ref, out_ref):
-    hot = rows_of((out_ref.shape[0], slot_ref.shape[1])) == slot_ref[...]
+def pack_kernel(slot_ref, rows_ref, out_ref, hot_ref):
+    @pl.when(pl.program_id(0) == 0)
+    def _():
+        hot_ref[...] = (rows_of(hot_ref.shape) == slot_ref[...]).astype(jnp.bfloat16)
+
     out_ref[...] = jnp.dot(
-        hot.astype(jnp.bfloat16), rows_ref[...], preferred_element_type=jnp.float32
+        hot_ref[...], rows_ref[...], preferred_element_type=jnp.float32
     ).astype(jnp.bfloat16)
 
 
@@ -51,6 +54,7 @@
             pl.BlockSpec((tokens, BLOCK), lambda j: (0, skip + j)),
         ],
         out_specs=pl.BlockSpec((slots, BLOCK), lambda j: (0, j)),
+        scratch_shapes=[pltpu.VMEM((slots, tokens), jnp.bfloat16)],
         compiler_params=VMEM,
         cost_estimate=cost(slots * tokens * width, (slots + tokens) * width),
     )(slot, rows)
@@ -110,107 +114,131 @@
 
 def ring_repack_kernel(z_ref, rows_ref, *refs):
     outs, flag_ref = refs[:RING], refs[RING]
-    hot_ref, note_ref, sum_ref, place_ref = refs[RING + 1 :]
-    slots, width = rows_ref.shape
+    hot_ref, note_ref, place_ref, held_ref = refs[RING + 1 :]
+    width = rows_ref.shape[2]
     step = pl.program_id(0)
 
     @pl.when(step == 0)
     def _():
-        for r in range(0, slots, 256):
-            total = jnp.zeros((256, 128), jnp.float32)
+        lane = lax.broadcasted_iota(jnp.int32, (8, 256), 1)
+        before = rows_of((256, 256))
+        slot = lax.broadcasted_iota(jnp.int32, (256, 256), 1)
+        ahead = ((before < slot) & (((before ^ slot) & 4) == 0)).astype(jnp.bfloat16)
+        over = jnp.zeros((8, 256), jnp.float32)
+        for q in range(RING // 2):
+            total = jnp.zeros((COLUMNS, 8, 128), jnp.float32)
             for c in range(0, width, 128):
-                total += jnp.abs(rows_ref[r : r + 256, c : c + 128].astype(jnp.float32))
-            sum_ref[r : r + 256, :] = (total > 0).astype(jnp.bfloat16)
-        seen = lax.dot_general(
-            jnp.ones((8, 128), jnp.bfloat16), sum_ref[...], NT, preferred_element_type=jnp.float32
+                total += jnp.abs(
+                    rows_ref[:, 8 * q : 8 * q + 8, c : c + 128].astype(jnp.float32)
+                )
+            filled = (total.reshape(256, 128) > 0).astype(jnp.bfloat16)
+            seen = lax.dot_general(
+                jnp.ones((8, 128), jnp.bfloat16), filled, NT, preferred_element_type=jnp.float32
+            )
+            used = seen > 0
+            place = jnp.dot(
+                used.astype(jnp.bfloat16), ahead, preferred_element_type=jnp.float32
+            )
+            over = jnp.maximum(over, jnp.where(used & (place >= ROWS - 1), 1.0, 0.0))
+            place_ref[8 * q : 8 * q + 8, :] = jnp.where(
+                used & (place < ROWS - 1), place, -1.0
+            ).astype(jnp.int32)
+        flag_ref[...] = jnp.broadcast_to(jnp.max(over, axis=1, keepdims=True), (8, 128))
+        codes = (((lane >> 3) << 2) + (lane & 3) + 1).astype(jnp.float32).astype(jnp.bfloat16)
+        for k in range(RING):
+            plane = (z_ref[0] + k) & 7
+            start = pl.multiple_of((plane >> 1) * 8, 8)
+            mine = ((lane >> 2) & 1) == (plane & 1)
+            place = jnp.where(mine, place_ref[pl.ds(start, 8), :], -1)[0:1, :]
+            hot_ref[k] = (rows_of((ROWS, 256)) == place).astype(jnp.bfloat16)
+            note_ref[8 * k : 8 * k + 8, :] = lax.dot_general(
+                codes,
+                (rows_of((128, 256)) == place).astype(jnp.bfloat16),
+                NT,
+                preferred_element_type=jnp.float32,
+            )
+
+    first = pl.multiple_of(step * BLOCK, BLOCK)
+    for q in range(RING // 2):
+        rows = rows_ref[:, 8 * q : 8 * q + 8, pl.ds(first, BLOCK)].astype(jnp.float32)
+        held_ref[256 * q : 256 * q + 256, :] = rows.reshape(256, BLOCK).astype(jnp.bfloat16)
+    for k in range(RING):
+        start = pl.multiple_of((((z_ref[0] + k) & 7) >> 1) * 256, 256)
+        picked = jnp.dot(
+            hot_ref[k], held_ref[pl.ds(start, 256), :], preferred_element_type=jnp.float32
         )
-        used = seen > 0
-        used_bf16 = used.astype(jnp.bfloat16)
-        for c in range(0, slots, 256):
-            before = rows_of((slots, 256))
-            slot = lax.broadcasted_iota(jnp.int32, (slots, 256), 1) + c
-            ahead = (before < slot) & (((before ^ slot) & 28) == 0)
-            place_ref[:, c : c + 256] = jnp.dot(
-                used_bf16, ahead.astype(jnp.bfloat16), preferred_element_type=jnp.float32
+        outs[k][...] = picked.astype(jnp.bfloat16)
+
+        @pl.when(step == 0)
+        def _():
+            note = jnp.where(rows_of((8, 128)) == 7, note_ref[8 * k : 8 * k + 8, :], 0.0)
+            outs[k][ROWS - 8 : ROWS, 0:128] = (picked[ROWS - 8 :, :128] + note).astype(
+                jnp.bfloat16
             )
-        place = place_ref[...].astype(jnp.int32)
-        slot = lax.broadcasted_iota(jnp.int32, (8, slots), 1)
-        over = jnp.where(used & (place >= ROWS - 1), 1.0, 0.0)
-        flag_ref[...] = jnp.broadcast_to(jnp.max(over, axis=1, keepdims=True), (8, 128))
-        ring = jnp.where(used & (place < ROWS - 1), (((slot >> 2) & 7) - z_ref[0]) & 7, -1)
-        code = (((slot >> 5) << 2) + (slot & 3) + 1).astype(jnp.float32)
-        compact_tables(ring[0:1, :], place[0:1, :], code[0:1, :], hot_ref, note_ref)
-
-    start = pl.multiple_of(step * BLOCK, BLOCK)
-    write_compact(rows_ref[:, pl.ds(start, BLOCK)], hot_ref, note_ref, outs)
 
 
 def ring_repacked(z, rows):
-    slots, width = rows.shape
+    width = rows.shape[2]
     out = pl.pallas_call(
         ring_repack_kernel,
         out_shape=[jax.ShapeDtypeStruct((ROWS, width), jnp.bfloat16)] * RING
         + [jax.ShapeDtypeStruct((8, 128), jnp.float32)],
         grid=(width // BLOCK,),
-        in_specs=[pl.BlockSpec(memory_space=pltpu.SMEM), whole((slots, width))],
+        in_specs=[pl.BlockSpec(memory_space=pltpu.SMEM), whole(rows.shape)],
         out_specs=[pl.BlockSpec((ROWS, BLOCK), lambda j: (0, j))] * RING + [whole((8, 128))],
         scratch_shapes=[
-            pltpu.VMEM((RING * ROWS, slots), jnp.bfloat16),
+            pltpu.VMEM((RING, ROWS, 256), jnp.bfloat16),
             pltpu.VMEM((8 * RING, 128), jnp.float32),
-            pltpu.VMEM((slots, 128), jnp.bfloat16),
-            pltpu.VMEM((8, slots), jnp.float32),
+            pltpu.VMEM((4 * RING, 256), jnp.int32),
+            pltpu.VMEM((128 * RING, BLOCK), jnp.bfloat16),
         ],
         compiler_params=VMEM,
-        cost_estimate=cost(RING * ROWS * slots * width, (RING * ROWS + slots) * width),
+        cost_estimate=cost(RING * ROWS * 256 * width, (RING * ROWS + 1024) * width),
     )(z, rows)
     return out[:RING], out[RING]
 
 
-def spread(z_ref, in_refs, hot_ref, held_ref):
-    slots = hot_ref.shape[0]
+def ring_spread_kernel(z_ref, *refs):
+    ins, (out_ref, hot_ref, held_ref) = refs[:RING], refs[RING:]
 
     @pl.when(pl.program_id(0) == 0)
     def _():
         held_ref[...] = jnp.zeros_like(held_ref)
         for k in range(RING):
-            code = in_refs[k][ROWS - 8 : ROWS, 0:128].astype(jnp.float32)[7:8, :].astype(jnp.int32)
+            code = ins[k][ROWS - 8 : ROWS, 0:128].astype(jnp.float32)[7:8, :].astype(jnp.int32)
             where = code - 1
             plane = (z_ref[0] - k) & 7
-            slot = jnp.where(code > 0, ((where >> 2) << 5) + (plane << 2) + (where & 3), -1)
-            hot_ref[:, 128 * k : 128 * k + 128] = (rows_of((slots, 128)) == slot).astype(
+            slot = ((where >> 2) << 3) + ((plane & 1) << 2) + (where & 3)
+            hot_ref[plane] = (rows_of((256, 128)) == jnp.where(code > 0, slot, -1)).astype(
                 jnp.bfloat16
             )
 
     for k in range(RING):
-        held_ref[128 * k : 128 * k + ROWS, :] = in_refs[k][...]
-    return jnp.dot(hot_ref[...], held_ref[...], preferred_element_type=jnp.float32)
-
-
-def ring_spread_kernel(z_ref, *refs):
-    ins, (out_ref, hot_ref, held_ref) = refs[:RING], refs[RING:]
-    out_ref[...] = spread(z_ref, ins, hot_ref, held_ref).astype(jnp.bfloat16)
-
-
-def ring_specs():
-    return [pl.BlockSpec(memory_space=pltpu.SMEM)] + [
-        pl.BlockSpec((ROWS, BLOCK), lambda j: (0, j))
-    ] * RING
-
-
-def ring_spread(z, parts, slots):
+        start = pl.multiple_of(((z_ref[0] - k) & 7) * 128, 128)
+        held_ref[pl.ds(start, ROWS), :] = ins[k][...]
+    for q in range(RING // 2):
+        hot = jnp.concatenate([hot_ref[2 * q], hot_ref[2 * q + 1]], axis=1)
+        picked = jnp.dot(
+            hot, held_ref[256 * q : 256 * q + 256, :], preferred_element_type=jnp.float32
+        )
+        out_ref[:, 8 * q : 8 * q + 8, :] = picked.reshape(COLUMNS, 8, BLOCK).astype(jnp.bfloat16)
+
+
+def ring_spread(z, parts):
     width = parts[0].shape[1]
     return pl.pallas_call(
         ring_spread_kernel,
-        out_shape=jax.ShapeDtypeStruct((slots, width), jnp.bfloat16),
+        out_shape=jax.ShapeDtypeStruct((COLUMNS, CAP * RING, width), jnp.bfloat16),
         grid=(width // BLOCK,),
-        in_specs=ring_specs(),
-        out_specs=pl.BlockSpec((slots, BLOCK), lambda j: (0, j)),
+        in_specs=[pl.BlockSpec(memory_space=pltpu.SMEM)]
+        + [pl.BlockSpec((ROWS, BLOCK), lambda j: (0, j))] * RING,
+        out_specs=pl.BlockSpec((COLUMNS, CAP * RING, BLOCK), lambda j: (0, 0, j)),
         scratch_shapes=[
-            pltpu.VMEM((slots, 128 * RING), jnp.bfloat16),
+            pltpu.VMEM((RING, 256, 128), jnp.bfloat16),
             pltpu.VMEM((128 * RING, BLOCK), jnp.bfloat16),
         ],
         compiler_params=VMEM,
-        cost_estimate=cost(slots * 128 * RING * width, (slots + ROWS * RING) * width),
+        cost_estimate=cost(1024 * 256 * width, (1024 + ROWS * RING) * width),
     )(z, *parts)
 
 
@@ -324,20 +352,18 @@
     return moved
 
 
-def in_plane(rows):
-    slots, width = rows.shape
-    parts = rows.reshape(COLUMNS, slots // COLUMNS, width)
-    return lax.all_to_all(parts, PLANE, split_axis=0, concat_axis=0, tiled=True).reshape(
-        slots, width
-    )
-
-
-def slot_order(table):
-    return table.reshape(4, RING, 8, CAP).swapaxes(1, 2).reshape(-1)
-
-
-def ring_order(table):
-    return table.reshape(4, RING, 8, CAP).swapaxes(0, 1).reshape(RING, -1)
+def in_plane(parts):
+    return lax.all_to_all(parts, PLANE, split_axis=0, concat_axis=0, tiled=True)
+
+
+def by_device(table):
+    rest = table.shape[1:]
+    return table.reshape(4, 8, RING, *rest).swapaxes(1, 2).reshape(-1, *rest)
+
+
+def by_column(table):
+    rest = table.shape[1:]
+    return table.reshape(4, RING, 8, *rest).swapaxes(1, 2).reshape(-1, *rest)
 
 
 def count_earlier(key, counts):
@@ -394,39 +420,43 @@
     )
     first = ring_shifted(first)
     second_slot = jnp.where(live, (column << 5) + (plane << 2) + rank, -1)
-    second = in_plane(packed_rows(second_slot[None, :], rows, slots, half, half))
+    second = packed_rows(second_slot[None, :], rows, slots, half, half)
+    second = in_plane(second.reshape(COLUMNS, CAP * RING, half))
     first[1], first[2], second = lax.optimization_barrier((first[1], first[2], second))
     second, over_there = ring_repacked(z, second)
     second = ring_shifted(second)
 
     code = jnp.where(live, (offset + 1) * resp_local + token_pos // block_len, 0)
-    direct_slot = owner * CAP + rank
+    note_slot = (plane * COLUMNS + column) * CAP + rank
     hidden = last_hidden.astype(jnp.float32)
     norm = jnp.sqrt(jnp.mean(hidden * hidden, axis=-1, keepdims=True) + 1e-05)
     own_reward = jnp.sum(hidden / norm * norm_gain * reward_head, axis=-1)
-    slot_match = direct_slot[None, :] == jnp.arange(slots, dtype=jnp.int32)[:, None]
+    slot_match = note_slot[None, :] == jnp.arange(slots, dtype=jnp.int32)[:, None]
     codes = jnp.sum(jnp.where(slot_match, code[None, :], 0), axis=1).reshape(devices, CAP)
-    over = jnp.maximum(over_here, over_there[0, 0])
-    own_facts = jnp.concatenate(
-        [own_reward, norm[:, 0], over[None], jnp.zeros((51,), jnp.float32)]
-    )
-    message = jnp.concatenate(
+    hidden_cols = hidden.reshape(resp_local, 4, RING, 8, cols).transpose(2, 1, 3, 0, 4)
+    own_facts = jnp.concatenate([own_reward, norm[:, 0], over_here[None]])
+    ready = jnp.concatenate(
         [
             codes.astype(jnp.float32),
-            jnp.broadcast_to(own_facts[None, :], (devices, 60)),
-            hidden.reshape(resp_local, devices, cols).swapaxes(0, 1).reshape(devices, -1),
+            jnp.broadcast_to(own_facts[None, :], (devices, 9)),
+            jnp.zeros((devices, 51), jnp.float32),
+            hidden_cols.reshape(devices, resp_local * cols),
         ],
         axis=1,
     )
-    heard = lax.all_to_all(message, GRP_DEV, split_axis=0, concat_axis=0, tiled=True)
-
-    first = ring_spread(z, first, slots)
+    lane = jnp.arange(128, dtype=jnp.int32)
+    message = jnp.where(lane[None, :] == 13, over_there[0, 0], ready)
+    message = message.reshape(RING, COLUMNS, 128)
+    message = lax.all_to_all(message, "dev_0", split_axis=0, concat_axis=0, tiled=True)
+    heard = in_plane(message.swapaxes(0, 1)).reshape(devices, 128)
+
+    first = ring_spread(z, first)
     first, second[1], second[7] = lax.optimization_barrier((first, second[1], second[7]))
     first = in_plane(first)
 
     arrived_code = heard[:, :CAP].astype(jnp.int32)
-    reward = heard[:, 4:8].reshape(responses)
-    any_over = jnp.max(heard[:, 12]) > 0
+    reward = by_device(heard[:, 4:8]).reshape(responses)
+    any_over = jnp.max(heard[:, 12:14]) > 0
     margin = reward[chosen_index] - reward[rejected_index]
     push = -jax.nn.sigmoid(-margin)
     every = jnp.arange(responses, dtype=jnp.int32)
@@ -434,6 +464,7 @@
         rejected_index[None, :] == every[:, None]
     ).astype(jnp.float32)
     reward_grad = jnp.sum(sign_table * push[None, :], axis=1).reshape(devices, resp_local)
+    reward_grad = by_column(reward_grad)
     own_gain = lax.dynamic_slice(norm_gain, (own_place * cols,), (cols,))
     head_grad = jnp.zeros((cols,), jnp.float32)
     for r in range(resp_local):
@@ -446,21 +477,28 @@
         scale = jnp.where(response_in == r, reward_grad[:, r : r + 1], scale)
     target = arrived_code // resp_local - 1
     scale = jnp.where(target >= 0, scale, 0.0)
-    target_row = slot_order(target)[None, :]
-    scale_column = slot_order(scale)[:, None]
-    half_done = placed_rows(target_row, scale_column, first, shard_rows, width)
+    half_done = placed_rows(
+        target.reshape(1, slots),
+        scale.reshape(slots, 1),
+        first.reshape(slots, half),
+        shard_rows,
+        width,
+    )
+
+    def by_plane(table):
+        return table.reshape(COLUMNS, RING, CAP).swapaxes(0, 1).reshape(RING, -1)
 
     def by_ring():
-        return ring_placed(z, ring_order(target), ring_order(scale), second, half_done)
+        return ring_placed(z, by_plane(target), by_plane(scale), second, half_done)
 
     def direct():
         sent = packed_rows(
-            jnp.where(live, direct_slot, -1)[None, :], rows, slots, 0, width
+            jnp.where(live, owner * CAP + rank, -1)[None, :], rows, slots, 0, width
         ).reshape(devices, CAP, width)
         arrived = lax.all_to_all(sent, GRP_DEV, split_axis=0, concat_axis=0, tiled=True)
         return placed_rows(
-            target.reshape(1, slots),
-            scale.reshape(slots, 1),
+            by_device(target).reshape(1, slots),
+            by_device(scale).reshape(slots, 1),
             arrived.reshape(slots, width),
             shard_rows,
             width,

time: 192 us -> 203 us (1.057)
  blocking collectives: 0 us -> 18.3 us
  starting transfers between devices: 69.9 us -> 61 us
  local copies, waits for them, and re-layouts: 14.5 us -> 18.3 us
  Pallas kernels: 40.3 us -> 38 us
    all_to_all x0 -> x1, blocking collectives: none -> 18.3 us  [local(): lax.all_to_all(message, 'dev_0', split_axis=0, concat_axis=0, tiled=True)]
    all_to_all x3, starting transfers between devices: 30.3 us -> 21.3 us  [in_plane(): return lax.all_to_all(parts, PLANE, split_axis=0, concat_axis=0, tiled=True)]
    pallas_call x1, Pallas kernels: 8.08 us -> 4.09 us  [ring_spread(): pl.pallas_call(ring_spread_kernel, out_shape=jax.ShapeDtypeStruct((COLUMN...]
    all_to_all x3, waiting for transfers between devices: 46.9 us -> 50.5 us  [in_plane(): return lax.all_to_all(parts, PLANE, split_axis=0, concat_axis=0, tiled=True)]
    ppermute x14, waiting for transfers between devices: 9.5 us -> 6.03 us  [ring_shifted(): lax.ppermute(parts[k], 'dev_0', [(i, (i + k) % RING) for i in range(RING)])]
    unnamed x28 -> x42, local copies, waits for them, and re-layouts: 5.22 us -> 5.28 us
  transfers between devices with their start and end apart: 17 -> 17, of which waited for: 5 -> 5; matrix products, arithmetic and copies ran while one was open for 6% -> 9% of each run, Pallas kernels for 15% -> 13%
where the time goes in v5:
time: 203 us; the launch traced here: 202 us
  starting transfers between devices  61 us (30%)
  waiting for transfers between devices  56.5 us (28%)
  Pallas kernels  38 us (19%)
  local copies, waits for them, and re-layouts  18.3 us (9%)
  blocking collectives  18.3 us (9%)
  other arithmetic  7.5 us (4%)
  between operations  2.29 us (1%)
    all_to_all x3, waiting for transfers between devices, in_plane(): return lax.all_to_all(parts, PLANE, split_axis=0, concat_axis=0, tiled=True)  50.5 us
    ppermute x14, starting transfers between devices, ring_shifted(): lax.ppermute(parts[k], 'dev_0', [(i, (i + k) % RING) for i in range(RING)])  39.7 us
    all_to_all x3, starting transfers between devices, in_plane(): return lax.all_to_all(parts, PLANE, split_axis=0, concat_axis=0, tiled=True)  21.3 us
    all_to_all x1, blocking collectives, local(): lax.all_to_all(message, 'dev_0', split_axis=0, concat_axis=0, tiled=True)  18.3 us
    pallas_call x1, Pallas kernels, ring_repacked(): pl.pallas_call(ring_repack_kernel, out_shape=[jax.ShapeDtypeStruct((ROWS,...  10.8 us
    pallas_call x1, Pallas kernels, ring_placed(): pl.pallas_call(ring_place_kernel, out_shape=jax.ShapeDtypeStruct(half_don...  6.49 us
    pallas_call x1, Pallas kernels, placed_rows(): pl.pallas_call(place_kernel, out_shape=jax.ShapeDtypeStruct((shard_rows,...  6.39 us
    ppermute x14, waiting for transfers between devices, ring_shifted(): lax.ppermute(parts[k], 'dev_0', [(i, (i + k) % RING) for i in range(RING)])  6.03 us
  transfers between devices with their start and end apart: 17, of which 5 were waited for; matrix products, arithmetic and copies ran while one was open for 9% of the time, Pallas kernels for 13%

profile of v5, /device:TPU:1, one launch (start us, length us, event | category | flops | bytes accessed | tf_op | source)
XLA Modules:
  0.0 202.0 jit_solution(6413893745390257417)
XLA Ops:
  0.6 0.7 fusion.17
  1.4 0.8 add_select_fusion.4
  2.4 0.9 select_reduce_fusion.1
  3.6 4.7 %shard_map.105 = bf16[1024,2048]{1,0:T(8,128)(2,1)S(1)} custom-call(s32[1,512]{1,0:T(1,128)S(1)} %get-tuple-element.232.slot_ref, bf16[512,4096]{1,0:T(8,128)(2,1)} %bitcast.105), custom_call_target="tpu_custom_call" | custom-call | flops 2147483648 | bytes 6291456 | tf_op jit(solution)/shard_map/pallas_call | solution.py:48
  8.3 2.0 copy-done
  10.3 8.6 %all-to-all-start.1 = ((bf16[32,32,2048]{2,1,0:T(8,128)(2,1)}), bf16[32,32,2048]{2,1,0:T(8,128)(2,1)}, u32[]{:S(2)}, u32[]{:S(2)}) async-start(bf16[32,32,2048]{2,1,0:T(8,128)(2,1)} %bitcast.94), calls=%async_computation.1 | async-start | bytes 8388608 | tf_op jit(solution)/shard_map/all_to_all | solution.py:356
  18.9 5.6 %shard_map.104 = (bf16[88,2048]{1,0:T(8,128)(2,1)S(1)}, bf16[88,2048]{1,0:T(8,128)(2,1)S(1)}, bf16[88,2048]{1,0:T(8,128)(2,1)S(1)}, bf16[88,2048]{1,0:T(8,128)(2...) custom-call(s32[1,512]{1,0:T(1,128)S(1)} %get-tuple-element.233.ring, ...), custom_call_target="tpu_custom_call" | custom-call | flops 1476395008 | bytes 4980736 | tf_op jit(solution)/shard_map/pallas_call | solution.py:100
  24.5 1.7 collective-permute-start
  26.2 3.0 %collective-permute-start.1 = (bf16[88,2048]{1,0:T(8,128)(2,1)S(1)}, bf16[88,2048]{1,0:T(8,128)(2,1)S(1)}, u32[]{:S(2)}, u32[]{:S(2)}) collective-permute-start(bf16[88,2048]{1,0:T(8,128)(2,1)S(1)} %get-tuple-element.90), channel_id=1, source_target_pairs={{0,16},{8,24},{16,32},{24,40},{32,48},{40,56},{48,0},{56,8},{1,17}... | collective-permute-start | bytes 1081352 | tf_op jit(solution)/shard_map/ppermute | solution.py:351
  29.2 3.8 %collective-permute-start.2 = (bf16[88,2048]{1,0:T(8,128)(2,1)}, bf16[88,2048]{1,0:T(8,128)(2,1)S(1)}, u32[]{:S(2)}, u32[]{:S(2)}) collective-permute-start(bf16[88,2048]{1,0:T(8,128)(2,1)} %get-tuple-element.97), channel_id=1, source_target_pairs={{0,24},{8,32},{16,40},{24,48},{32,56},{40,0},{48,8},{56,16},{1,25}... | collective-permute-start | bytes 1081352 | tf_op jit(solution)/shard_map/ppermute | solution.py:351
  33.4 4.5 %collective-permute-start.4 = (bf16[88,2048]{1,0:T(8,128)(2,1)}, bf16[88,2048]{1,0:T(8,128)(2,1)S(1)}, u32[]{:S(2)}, u32[]{:S(2)}) collective-permute-start(bf16[88,2048]{1,0:T(8,128)(2,1)} %get-tuple-element.99), channel_id=1, source_target_pairs={{0,40},{8,48},{16,56},{24,0},{32,8},{40,16},{48,24},{56,32},{1,41}... | collective-permute-start | bytes 1081352 | tf_op jit(solution)/shard_map/ppermute | solution.py:351
  38.4 0.7 and_reduce_fusion
  39.1 1.0 reshape.355
  40.7 0.8 convert_element_type.43
  41.5 1.4 copy.125
  42.9 0.9 concatenate.10
  44.2 2.4 %collective-permute-start.5 = (bf16[88,2048]{1,0:T(8,128)(2,1)}, bf16[88,2048]{1,0:T(8,128)(2,1)S(1)}, u32[]{:S(2)}, u32[]{:S(2)}) collective-permute-start(bf16[88,2048]{1,0:T(8,128)(2,1)} %get-tuple-element.100), channel_id=1, source_target_pairs={{0,48},{8,56},{16,0},{24,8},{32,16},{40,24},{48,32},{56,40},{1,49}... | collective-permute-start | bytes 1081352 | tf_op jit(solution)/shard_map/ppermute | solution.py:351
  46.6 1.6 collective-permute-done.1.refs_2_
  48.2 8.7 %collective-permute-start.6 = (bf16[88,2048]{1,0:T(8,128)(2,1)}, bf16[88,2048]{1,0:T(8,128)(2,1)S(1)}, u32[]{:S(2)}, u32[]{:S(2)}) collective-permute-start(bf16[88,2048]{1,0:T(8,128)(2,1)} %get-tuple-element.101), channel_id=1, source_target_pairs={{0,56},{8,0},{16,8},{24,16},{32,24},{40,32},{48,40},{56,48},{1,57}... | collective-permute-start | bytes 1081352 | tf_op jit(solution)/shard_map/ppermute | solution.py:351
  56.9 14.4 %all-to-all-done.1.rows_ref = bf16[32,32,2048]{2,1,0:T(8,128)(2,1)} async-done(((bf16[32,32,2048]{2,1,0:T(8,128)(2,1)}), bf16[32,32,2048]{2,1,0:T(8,128)(2,1)}, u32[]{:S(2)}, u32[]{:S(2)}) %all-to-all-start.1) | async-done | bytes 4194336 | tf_op jit(solution)/shard_map/all_to_all | solution.py:356
  71.3 10.8 %shard_map.106 = (bf16[88,2048]{1,0:T(8,128)(2,1)}, bf16[88,2048]{1,0:T(8,128)(2,1)}, bf16[88,2048]{1,0:T(8,128)(2,1)S(1)}, bf16[88,2048]{1,0:T(8,128)(2,1)S(1)}...) custom-call(s32[1]{0:T(128)} %bitcast.16.z_ref, ...), custom_call_target="tpu_custom_call" | custom-call | flops 738197504 | bytes 7077888 | tf_op jit(solution)/shard_map/pallas_call | solution.py:182
  82.1 0.8 copy-done.1
  82.9 0.7 copy-done.3
  83.6 0.7 copy-done.5
  84.4 0.7 copy-done.7
  85.6 1.6 collective-permute-start.7
  87.3 4.2 %collective-permute-start.8 = (bf16[88,2048]{1,0:T(8,128)(2,1)}, bf16[88,2048]{1,0:T(8,128)(2,1)}, u32[]{:S(2)}, u32[]{:S(2)}) collective-permute-start(bf16[88,2048]{1,0:T(8,128)(2,1)} %get-tuple-element.103), channel_id=1, source_target_pairs={{0,56},{8,0},{16,8},{24,16},{32,24},{40,32},{48,40},{56,48},{1,57}... | collective-permute-start | bytes 1081352 | tf_op jit(solution)/shard_map/ppermute | solution.py:351
  91.5 0.7 maximum_select_fusion
  92.3 18.3 %all_to_all.24 = f32[8,32,128]{2,1,0:T(8,128)S(1)} all-to-all(f32[8,32,128]{2,1,0:T(8,128)S(1)} %maximum_select_fusion), channel_id=1, replica_groups=mesh['grp'=4,'dev_0'=8,'dev_1'=4,'dev_2'=2] {'dev_0'}, dimensions={0} | all-to-all | bytes 262144 | tf_op jit(solution)/shard_map/all_to_all | solution.py:450
  110.6 0.7 copy.127
  111.3 7.8 %all-to-all-start.3 = ((f32[32,8,128]{2,1,0:T(8,128)}), f32[32,8,128]{2,1,0:T(8,128)S(1)}, u32[]{:S(2)}, u32[]{:S(2)}) async-start(f32[32,8,128]{2,1,0:T(8,128)} %bitcast.93), calls=%async_computation.3 | async-start | bytes 262144 | tf_op jit(solution)/shard_map/all_to_all | solution.py:356
  119.2 4.1 %shard_map.107 = bf16[32,32,2048]{2,1,0:T(8,128)(2,1)} custom-call(s32[1]{0:T(128)} %bitcast.16.z_ref, bf16[88,2048]{1,0:T(8,128)(2,1)S(1)} %get-tuple-element.94.refs_0_, bf16[88,2048]{1,0:T(8,128)(2,1)S(1)} %collective-permute-done.refs_1_, bf16[88,2048]{1,0:T(8,128)(2,1)S(1)} %collective-permute-done.1.refs_2_, ...), custom_call_target="tpu_custom_call" | custom-call | flops 1073741824 | bytes 7077888 | tf_op jit(solution)/shard_map/pallas_call | solution.py:229
  123.3 3.5 %all-to-all-done.3 = f32[32,8,128]{2,1,0:T(8,128)S(1)} async-done(((f32[32,8,128]{2,1,0:T(8,128)}), f32[32,8,128]{2,1,0:T(8,128)S(1)}, u32[]{:S(2)}, u32[]{:S(2)}) %all-to-all-start.3) | async-done | bytes 131104 | tf_op jit(solution)/shard_map/all_to_all | solution.py:356
  126.9 4.8 %all-to-all-start.4 = ((bf16[32,32,2048]{2,1,0:T(8,128)(2,1)}), bf16[32,32,2048]{2,1,0:T(8,128)(2,1)}, u32[]{:S(2)}, u32[]{:S(2)}) async-start(bf16[32,32,2048]{2,1,0:T(8,128)(2,1)} %shard_map.107), calls=%async_computation.4 | async-start | bytes 8388608 | tf_op jit(solution)/shard_map/all_to_all | solution.py:356
  131.7 0.8 dynamic_slice.3
  132.5 1.4 collective-permute-start.10
  133.9 4.7 %collective-permute-start.11 = (bf16[88,2048]{1,0:T(8,128)(2,1)S(1)}, bf16[88,2048]{1,0:T(8,128)(2,1)}, u32[]{:S(2)}, u32[]{:S(2)}) collective-permute-start(bf16[88,2048]{1,0:T(8,128)(2,1)S(1)} %copy-done.6), channel_id=1, source_target_pairs={{0,32},{8,40},{16,48},{24,56},{32,0},{40,8},{48,16},{56,24},{1,33}... | collective-permute-start | bytes 1081352 | tf_op jit(solution)/shard_map/ppermute | solution.py:351
  138.6 3.2 %collective-permute-start.13 = (bf16[88,2048]{1,0:T(8,128)(2,1)S(1)}, bf16[88,2048]{1,0:T(8,128)(2,1)}, u32[]{:S(2)}, u32[]{:S(2)}) collective-permute-start(bf16[88,2048]{1,0:T(8,128)(2,1)S(1)} %copy-done.2), channel_id=1, source_target_pairs={{0,48},{8,56},{16,0},{24,8},{32,16},{40,24},{48,32},{56,40},{1,49}... | collective-permute-start | bytes 1081352 | tf_op jit(solution)/shard_map/ppermute | solution.py:351
  142.6 2.3 %gather_fusion = f32[512]{0:T(512)S(1)} fusion(f32[1024]{0:T(1024)S(1)} %reshape_reshape.6, s32[1024]{0:T(1024)S(1)} %pad_clamp_fusion.1), kind=kCustom, calls=%fused_computation | custom fusion | bytes 6144 | tf_op jit(solution)/shard_map/gather | solution.py:460
  144.9 2.3 %gather_fusion.1 = f32[512]{0:T(512)S(1)} fusion(f32[1024]{0:T(1024)S(1)} %reshape_reshape.6, s32[1024]{0:T(1024)S(1)} %pad_clamp_fusion), kind=kCustom, calls=%fused_computation.1 | custom fusion | bytes 6144 | tf_op jit(solution)/shard_map/gather | solution.py:460
  147.2 0.6 multiply_reduce_fusion
  149.0 0.7 slice_reduce_fusion.4
  150.9 0.5 add_add_fusion.1
  151.4 32.5 %all-to-all-done.4 = bf16[32,32,2048]{2,1,0:T(8,128)(2,1)} async-done(((bf16[32,32,2048]{2,1,0:T(8,128)(2,1)}), bf16[32,32,2048]{2,1,0:T(8,128)(2,1)}, u32[]{:S(2)}, u32[]{:S(2)}) %all-to-all-start.4) | async-done | bytes 4194336 | tf_op jit(solution)/shard_map/all_to_all | solution.py:356
  184.0 6.4 %shard_map.108 = bf16[501,4096]{1,0:T(8,128)(2,1)} custom-call(s32[1,1024]{1,0:T(1,128)S(1)} %reshape.359.target_ref, f32[1024,1]{1,0:T(8,128)S(1)} %reshape.388.scale_ref, bf16[1024,2048]{1,0:T(8,128)(2,1)} %bitcast.37.rows_ref), custom_call_target="tpu_custom_call" | custom-call | flops 2101346304 | bytes 6246400 | tf_op jit(solution)/shard_map/pallas_call | solution.py:260
  190.4 4.4 %collective-permute-done.13 = bf16[88,2048]{1,0:T(8,128)(2,1)} collective-permute-done((bf16[88,2048]{1,0:T(8,128)(2,1)S(1)}, bf16[88,2048]{1,0:T(8,128)(2,1)}, u32[]{:S(2)}, u32[]{:S(2)}) %collective-permute-start.13) | collective-permute-done | bytes 360480 | tf_op jit(solution)/shard_map/ppermute | solution.py:351
  194.8 7.1 %conditional.1 = (bf16[501,4096]{1,0:T(8,128)(2,1)}) conditional(s32[]{:T(128)} %convert_element_type.45, (s32[256,4]{1,0:T(8,128)S(1)}, f32[256,4]{1,0:T(8,128)S(1)}, s32[1]{0:T(128)}, bf16[88,2048]{1,0:T(8,128)(2,1)S(1)}, bf16[88,2048]{1,0:T(8,128)(2,1)}, /*index=5*/bf16[88,2048]{1,0:T(8,128)(2,1)}, bf16[88,2048]{1,0:T(8,128)(2,1)S(1)}, ...), branch_computations={%region_9.10_spmd, %region_10.11_spmd} | conditional | flops 8497661952 | bytes 83836984 | solution.py:507
  195.5 6.5 %branch_0_fun.1 = bf16[501,4096]{1,0:T(8,128)(2,1)} custom-call(s32[1]{0:T(128)} %get-tuple-element.45.z_ref, s32[8,128]{1,0:T(8,128)S(1)} %copy.85.target_ref, f32[8,128]{1,0:T(8,128)S(1)} %copy.86.scale_ref, bf16[88,2048]{1,0:T(8,128)(2,1)S(1)} %get-tuple-element.48.refs_0_, ...), custom_call_target="tpu_custom_call", output_to_operand_aliasing={{}: (11, {})} | custom-call | flops 2101346304 | bytes 4935680 | tf_op jit(solution)/shard_map/cond/branch_0_fun/pallas_call | solution.py:328
  (90 shorter events, 5.6 us)
Async XLA Ops:
  8.3 2.0 copy-start
  10.3 61.0 %all-to-all-start.1 = ((bf16[32,32,2048]{2,1,0:T(8,128)(2,1)}), bf16[32,32,2048]{2,1,0:T(8,128)(2,1)}, u32[]{:S(2)}, u32[]{:S(2)}) async-start(bf16[32,32,2048]{2,1,0:T(8,128)(2,1)} %bitcast.94), calls=%async_computation.1 | async-start | bytes 8388608 | tf_op jit(solution)/shard_map/all_to_all | solution.py:356
  18.9 19.0 %copy-start.12 = (bf16[4,4096]{1,0:T(4,128)(2,1)S(1)}, bf16[4,4096]{1,0:T(4,128)(2,1)}, u32[]{:S(2)}) copy-start(bf16[4,4096]{1,0:T(4,128)(2,1)} %param.13) | copy-start | bytes 98308
  18.9 19.4 %copy-start.16 = (s32[4]{0:T(128)S(1)}, s32[4]{0:T(128)}, u32[]{:S(2)}) copy-start(s32[4]{0:T(128)} %param.14) | copy-start | bytes 52
  24.5 19.4 %copy-start.13 = (bf16[4,4096]{1,0:T(4,128)(2,1)S(1)}, bf16[4,4096]{1,0:T(4,128)(2,1)}, u32[]{:S(2)}) copy-start(bf16[4,4096]{1,0:T(4,128)(2,1)} %param.13) | copy-start | bytes 98308
  24.5 19.4 %copy-start.14 = (f32[4096]{0:T(1024)S(1)}, f32[4096]{0:T(1024)}, u32[]{:S(2)}) copy-start(f32[4096]{0:T(1024)} %param.16) | copy-start | bytes 49156
  24.5 19.4 %copy-start.15 = (f32[4096]{0:T(1024)S(1)}, f32[4096]{0:T(1024)}, u32[]{:S(2)}) copy-start(f32[4096]{0:T(1024)} %param.15) | copy-start | bytes 49156
  24.5 19.7 %collective-permute-start = (bf16[88,2048]{1,0:T(8,128)(2,1)S(1)}, bf16[88,2048]{1,0:T(8,128)(2,1)S(1)}, u32[]{:S(2)}, u32[]{:S(2)}) collective-permute-start(bf16[88,2048]{1,0:T(8,128)(2,1)S(1)} %get-tuple-element.89), channel_id=1, source_target_pairs={{0,8},{8,16},{16,24},{24,32},{32,40},{40,48},{48,56},{56,0},{1,9},... | collective-permute-start | bytes 1081352 | tf_op jit(solution)/shard_map/ppermute | solution.py:351
  26.2 21.9 %collective-permute-start.1 = (bf16[88,2048]{1,0:T(8,128)(2,1)S(1)}, bf16[88,2048]{1,0:T(8,128)(2,1)S(1)}, u32[]{:S(2)}, u32[]{:S(2)}) collective-permute-start(bf16[88,2048]{1,0:T(8,128)(2,1)S(1)} %get-tuple-element.90), channel_id=1, source_target_pairs={{0,16},{8,24},{16,32},{24,40},{32,48},{40,56},{48,0},{56,8},{1,17}... | collective-permute-start | bytes 1081352 | tf_op jit(solution)/shard_map/ppermute | solution.py:351
  29.2 56.4 %collective-permute-start.2 = (bf16[88,2048]{1,0:T(8,128)(2,1)}, bf16[88,2048]{1,0:T(8,128)(2,1)S(1)}, u32[]{:S(2)}, u32[]{:S(2)}) collective-permute-start(bf16[88,2048]{1,0:T(8,128)(2,1)} %get-tuple-element.97), channel_id=1, source_target_pairs={{0,24},{8,32},{16,40},{24,48},{32,56},{40,0},{48,8},{56,16},{1,25}... | collective-permute-start | bytes 1081352 | tf_op jit(solution)/shard_map/ppermute | solution.py:351
  33.0 54.3 %collective-permute-start.3 = (bf16[88,2048]{1,0:T(8,128)(2,1)}, bf16[88,2048]{1,0:T(8,128)(2,1)S(1)}, u32[]{:S(2)}, u32[]{:S(2)}) collective-permute-start(bf16[88,2048]{1,0:T(8,128)(2,1)} %get-tuple-element.98), channel_id=1, source_target_pairs={{0,32},{8,40},{16,48},{24,56},{32,0},{40,8},{48,16},{56,24},{1,33}... | collective-permute-start | bytes 1081352 | tf_op jit(solution)/shard_map/ppermute | solution.py:351
  33.4 85.7 %collective-permute-start.4 = (bf16[88,2048]{1,0:T(8,128)(2,1)}, bf16[88,2048]{1,0:T(8,128)(2,1)S(1)}, u32[]{:S(2)}, u32[]{:S(2)}) collective-permute-start(bf16[88,2048]{1,0:T(8,128)(2,1)} %get-tuple-element.99), channel_id=1, source_target_pairs={{0,40},{8,48},{16,56},{24,0},{32,8},{40,16},{48,24},{56,32},{1,41}... | collective-permute-start | bytes 1081352 | tf_op jit(solution)/shard_map/ppermute | solution.py:351
  44.2 75.0 %collective-permute-start.5 = (bf16[88,2048]{1,0:T(8,128)(2,1)}, bf16[88,2048]{1,0:T(8,128)(2,1)S(1)}, u32[]{:S(2)}, u32[]{:S(2)}) collective-permute-start(bf16[88,2048]{1,0:T(8,128)(2,1)} %get-tuple-element.100), channel_id=1, source_target_pairs={{0,48},{8,56},{16,0},{24,8},{32,16},{40,24},{48,32},{56,40},{1,49}... | collective-permute-start | bytes 1081352 | tf_op jit(solution)/shard_map/ppermute | solution.py:351
  48.2 71.0 %collective-permute-start.6 = (bf16[88,2048]{1,0:T(8,128)(2,1)}, bf16[88,2048]{1,0:T(8,128)(2,1)S(1)}, u32[]{:S(2)}, u32[]{:S(2)}) collective-permute-start(bf16[88,2048]{1,0:T(8,128)(2,1)} %get-tuple-element.101), channel_id=1, source_target_pairs={{0,56},{8,0},{16,8},{24,16},{32,24},{40,32},{48,40},{56,48},{1,57}... | collective-permute-start | bytes 1081352 | tf_op jit(solution)/shard_map/ppermute | solution.py:351
  71.3 20.2 %copy-start.9 = (f32[8,32,64]{2,1,0:T(8,128)S(1)}, f32[8,32,64]{2,1,0:T(8,128)}, u32[]{:S(2)}) copy-start(f32[8,32,64]{2,1,0:T(8,128)} %concatenate.10) | copy-start | bytes 196612
  71.3 20.2 %copy-start.10 = (f32[8,32,4]{2,1,0:T(8,128)S(1)}, f32[8,32,4]{2,1,0:T(8,128)}, u32[]{:S(2)}) copy-start(f32[8,32,4]{2,1,0:T(8,128)} %convert_element_type.43) | copy-start | bytes 12292
  82.1 0.8 copy-start.1
  82.9 0.7 copy-start.3
  83.6 0.7 copy-start.5
  84.4 0.7 copy-start.7
  85.6 37.7 %collective-permute-start.7 = (bf16[88,2048]{1,0:T(8,128)(2,1)}, bf16[88,2048]{1,0:T(8,128)(2,1)}, u32[]{:S(2)}, u32[]{:S(2)}) collective-permute-start(bf16[88,2048]{1,0:T(8,128)(2,1)} %get-tuple-element.102), channel_id=1, source_target_pairs={{0,8},{8,16},{16,24},{24,32},{32,40},{40,48},{48,56},{56,0},{1,9},... | collective-permute-start | bytes 1081352 | tf_op jit(solution)/shard_map/ppermute | solution.py:351
  87.3 36.0 %collective-permute-start.8 = (bf16[88,2048]{1,0:T(8,128)(2,1)}, bf16[88,2048]{1,0:T(8,128)(2,1)}, u32[]{:S(2)}, u32[]{:S(2)}) collective-permute-start(bf16[88,2048]{1,0:T(8,128)(2,1)} %get-tuple-element.103), channel_id=1, source_target_pairs={{0,56},{8,0},{16,8},{24,16},{32,24},{40,32},{48,40},{56,48},{1,57}... | collective-permute-start | bytes 1081352 | tf_op jit(solution)/shard_map/ppermute | solution.py:351
  111.3 15.5 %all-to-all-start.3 = ((f32[32,8,128]{2,1,0:T(8,128)}), f32[32,8,128]{2,1,0:T(8,128)S(1)}, u32[]{:S(2)}, u32[]{:S(2)}) async-start(f32[32,8,128]{2,1,0:T(8,128)} %bitcast.93), calls=%async_computation.3 | async-start | bytes 262144 | tf_op jit(solution)/shard_map/all_to_all | solution.py:356
  123.3 9.2 %copy-start.17 = (s32[512]{0:T(512)S(1)}, s32[512]{0:T(512)}, u32[]{:S(2)}) copy-start(s32[512]{0:T(512)} %param.17) | copy-start | bytes 6148
  123.3 9.2 %copy-start.18 = (s32[512]{0:T(512)S(1)}, s32[512]{0:T(512)}, u32[]{:S(2)}) copy-start(s32[512]{0:T(512)} %param.18) | copy-start | bytes 6148
  123.3 9.2 %copy-start.8 = (bf16[88,2048]{1,0:T(8,128)(2,1)S(1)}, bf16[88,2048]{1,0:T(8,128)(2,1)}, u32[]{:S(2)}) copy-start(bf16[88,2048]{1,0:T(8,128)(2,1)} %copy-done.7) | copy-start | bytes 1081348
  123.3 10.6 %copy-start.6 = (bf16[88,2048]{1,0:T(8,128)(2,1)S(1)}, bf16[88,2048]{1,0:T(8,128)(2,1)}, u32[]{:S(2)}) copy-start(bf16[88,2048]{1,0:T(8,128)(2,1)} %copy-done.5) | copy-start | bytes 1081348
  123.3 15.3 %copy-start.4 = (bf16[88,2048]{1,0:T(8,128)(2,1)S(1)}, bf16[88,2048]{1,0:T(8,128)(2,1)}, u32[]{:S(2)}) copy-start(bf16[88,2048]{1,0:T(8,128)(2,1)} %copy-done.3) | copy-start | bytes 1081348
  123.3 15.3 %copy-start.2 = (bf16[88,2048]{1,0:T(8,128)(2,1)S(1)}, bf16[88,2048]{1,0:T(8,128)(2,1)}, u32[]{:S(2)}) copy-start(bf16[88,2048]{1,0:T(8,128)(2,1)} %copy-done.1) | copy-start | bytes 1081348
  126.9 57.1 %all-to-all-start.4 = ((bf16[32,32,2048]{2,1,0:T(8,128)(2,1)}), bf16[32,32,2048]{2,1,0:T(8,128)(2,1)}, u32[]{:S(2)}, u32[]{:S(2)}) async-start(bf16[32,32,2048]{2,1,0:T(8,128)(2,1)} %shard_map.107), calls=%async_computation.4 | async-start | bytes 8388608 | tf_op jit(solution)/shard_map/all_to_all | solution.py:356
  132.5 57.8 %collective-permute-start.10 = (bf16[88,2048]{1,0:T(8,128)(2,1)S(1)}, bf16[88,2048]{1,0:T(8,128)(2,1)S(1)}, u32[]{:S(2)}, u32[]{:S(2)}) collective-permute-start(bf16[88,2048]{1,0:T(8,128)(2,1)S(1)} %copy-done.8), channel_id=1, source_target_pairs={{0,24},{8,32},{16,40},{24,48},{32,56},{40,0},{48,8},{56,16},{1,25}... | collective-permute-start | bytes 1081352 | tf_op jit(solution)/shard_map/ppermute | solution.py:351
  133.9 56.5 %collective-permute-start.11 = (bf16[88,2048]{1,0:T(8,128)(2,1)S(1)}, bf16[88,2048]{1,0:T(8,128)(2,1)}, u32[]{:S(2)}, u32[]{:S(2)}) collective-permute-start(bf16[88,2048]{1,0:T(8,128)(2,1)S(1)} %copy-done.6), channel_id=1, source_target_pairs={{0,32},{8,40},{16,48},{24,56},{32,0},{40,8},{48,16},{56,24},{1,33}... | collective-permute-start | bytes 1081352 | tf_op jit(solution)/shard_map/ppermute | solution.py:351
  138.6 51.8 %collective-permute-start.12 = (bf16[88,2048]{1,0:T(8,128)(2,1)S(1)}, bf16[88,2048]{1,0:T(8,128)(2,1)}, u32[]{:S(2)}, u32[]{:S(2)}) collective-permute-start(bf16[88,2048]{1,0:T(8,128)(2,1)S(1)} %copy-done.4), channel_id=1, source_target_pairs={{0,40},{8,48},{16,56},{24,0},{32,8},{40,16},{48,24},{56,32},{1,41}... | collective-permute-start | bytes 1081352 | tf_op jit(solution)/shard_map/ppermute | solution.py:351
  138.6 56.2 %collective-permute-start.13 = (bf16[88,2048]{1,0:T(8,128)(2,1)S(1)}, bf16[88,2048]{1,0:T(8,128)(2,1)}, u32[]{:S(2)}, u32[]{:S(2)}) collective-permute-start(bf16[88,2048]{1,0:T(8,128)(2,1)S(1)} %copy-done.2), channel_id=1, source_target_pairs={{0,48},{8,56},{16,0},{24,8},{32,16},{40,24},{48,32},{56,40},{1,49}... | collective-permute-start | bytes 1081352 | tf_op jit(solution)/shard_map/ppermute | solution.py:351
  141.8 53.0 %collective-permute-start.9 = (bf16[88,2048]{1,0:T(8,128)(2,1)S(1)}, bf16[88,2048]{1,0:T(8,128)(2,1)}, u32[]{:S(2)}, u32[]{:S(2)}) collective-permute-start(bf16[88,2048]{1,0:T(8,128)(2,1)S(1)} %get-tuple-element.105), channel_id=1, source_target_pairs={{0,16},{8,24},{16,32},{24,40},{32,48},{40,56},{48,0},{56,8},{1,17}... | collective-permute-start | bytes 1081352 | tf_op jit(solution)/shard_map/ppermute | solution.py:351
  184.0 10.8 %copy-start.11 = (bf16[88,2048]{1,0:T(8,128)(2,1)S(1)}, bf16[88,2048]{1,0:T(8,128)(2,1)}, u32[]{:S(2)}) copy-start(bf16[88,2048]{1,0:T(8,128)(2,1)} %get-tuple-element.93) | copy-start | bytes 1081348

commit v6 on v5

--- a/solution.py
+++ b/solution.py
@@ -85,36 +85,51 @@
             out_refs[k][ROWS - 8 : ROWS, 0:128] = (tail + note).astype(jnp.bfloat16)
 
 
-def ring_pack_kernel(ring_ref, place_ref, code_ref, rows_ref, *refs):
-    outs, (hot_ref, note_ref) = refs[:RING], refs[RING:]
+def both_pack_kernel(ring_ref, place_ref, code_ref, slot_ref, first_ref, second_ref, *refs):
+    outs, (second_out_ref, hot_ref, note_ref, slot_hot_ref) = refs[:RING], refs[RING:]
 
     @pl.when(pl.program_id(0) == 0)
     def _():
         compact_tables(ring_ref[...], place_ref[...], code_ref[...], hot_ref, note_ref)
-
-    write_compact(rows_ref[...], hot_ref, note_ref, outs)
-
-
-def ring_packed(ring, place, code, rows, width):
+        slot_hot_ref[...] = (rows_of(slot_hot_ref.shape) == slot_ref[...]).astype(jnp.bfloat16)
+
+    write_compact(first_ref[...], hot_ref, note_ref, outs)
+    second_out_ref[...] = jnp.dot(
+        slot_hot_ref[...], second_ref[...], preferred_element_type=jnp.float32
+    ).astype(jnp.bfloat16)
+
+
+def both_packed(ring, place, code, slot, rows, slots, half):
     tokens = rows.shape[0]
-    return pl.pallas_call(
-        ring_pack_kernel,
-        out_shape=[jax.ShapeDtypeStruct((ROWS, width), jnp.bfloat16)] * RING,
-        grid=(width // BLOCK,),
-        in_specs=[whole((1, tokens))] * 3 + [pl.BlockSpec((tokens, BLOCK), lambda j: (0, j))],
-        out_specs=[pl.BlockSpec((ROWS, BLOCK), lambda j: (0, j))] * RING,
+    steps = half // BLOCK
+    out = pl.pallas_call(
+        both_pack_kernel,
+        out_shape=[jax.ShapeDtypeStruct((ROWS, half), jnp.bfloat16)] * RING
+        + [jax.ShapeDtypeStruct((slots, half), jnp.bfloat16)],
+        grid=(steps,),
+        in_specs=[whole((1, tokens))] * 4
+        + [
+            pl.BlockSpec((tokens, BLOCK), lambda j: (0, j)),
+            pl.BlockSpec((tokens, BLOCK), lambda j: (0, steps + j)),
+        ],
+        out_specs=[pl.BlockSpec((ROWS, BLOCK), lambda j: (0, j))] * RING
+        + [pl.BlockSpec((slots, BLOCK), lambda j: (0, j))],
         scratch_shapes=[
             pltpu.VMEM((RING * ROWS, tokens), jnp.bfloat16),
             pltpu.VMEM((8 * RING, 128), jnp.float32),
+            pltpu.VMEM((slots, tokens), jnp.bfloat16),
         ],
         compiler_params=VMEM,
-        cost_estimate=cost(RING * ROWS * tokens * width, (RING * ROWS + tokens) * width),
-    )(ring, place, code, rows)
+        cost_estimate=cost(
+            (RING * ROWS + slots) * tokens * half, (RING * ROWS + slots + 2 * tokens) * half
+        ),
+    )(ring, place, code, slot, rows, rows)
+    return out[:RING], out[RING]
 
 
 def ring_repack_kernel(z_ref, rows_ref, *refs):
     outs, flag_ref = refs[:RING], refs[RING]
-    hot_ref, note_ref, place_ref, held_ref = refs[RING + 1 :]
+    hot_ref, note_ref, place_ref, held_ref, sent_ref = refs[RING + 1 :]
     width = rows_ref.shape[2]
     step = pl.program_id(0)
 
@@ -150,7 +165,7 @@
             start = pl.multiple_of((plane >> 1) * 8, 8)
             mine = ((lane >> 2) & 1) == (plane & 1)
             place = jnp.where(mine, place_ref[pl.ds(start, 8), :], -1)[0:1, :]
-            hot_ref[k] = (rows_of((ROWS, 256)) == place).astype(jnp.bfloat16)
+            hot_ref[plane] = (rows_of((ROWS, 256)) == place).astype(jnp.bfloat16)
             note_ref[8 * k : 8 * k + 8, :] = lax.dot_general(
                 codes,
                 (rows_of((128, 256)) == place).astype(jnp.bfloat16),
@@ -162,19 +177,23 @@
     for q in range(RING // 2):
         rows = rows_ref[:, 8 * q : 8 * q + 8, pl.ds(first, BLOCK)].astype(jnp.float32)
         held_ref[256 * q : 256 * q + 256, :] = rows.reshape(256, BLOCK).astype(jnp.bfloat16)
+    for q in range(RING // 2):
+        hot = jnp.concatenate([hot_ref[2 * q], hot_ref[2 * q + 1]], axis=0)
+        picked = jnp.dot(
+            hot, held_ref[256 * q : 256 * q + 256, :], preferred_element_type=jnp.float32
+        )
+        for half in (0, 1):
+            k = (2 * q + half - z_ref[0]) & 7
+            sent_ref[k] = picked[half * ROWS : (half + 1) * ROWS].astype(jnp.bfloat16)
     for k in range(RING):
-        start = pl.multiple_of((((z_ref[0] + k) & 7) >> 1) * 256, 256)
-        picked = jnp.dot(
-            hot_ref[k], held_ref[pl.ds(start, 256), :], preferred_element_type=jnp.float32
-        )
-        outs[k][...] = picked.astype(jnp.bfloat16)
-
-        @pl.when(step == 0)
-        def _():
+        outs[k][...] = sent_ref[k]
+
+    @pl.when(step == 0)
+    def _():
+        for k in range(RING):
+            tail = sent_ref[k, ROWS - 8 : ROWS, 0:128].astype(jnp.float32)
             note = jnp.where(rows_of((8, 128)) == 7, note_ref[8 * k : 8 * k + 8, :], 0.0)
-            outs[k][ROWS - 8 : ROWS, 0:128] = (picked[ROWS - 8 :, :128] + note).astype(
-                jnp.bfloat16
-            )
+            outs[k][ROWS - 8 : ROWS, 0:128] = (tail + note).astype(jnp.bfloat16)
 
 
 def ring_repacked(z, rows):
@@ -191,6 +210,7 @@
             pltpu.VMEM((8 * RING, 128), jnp.float32),
             pltpu.VMEM((4 * RING, 256), jnp.int32),
             pltpu.VMEM((128 * RING, BLOCK), jnp.bfloat16),
+            pltpu.VMEM((RING, ROWS, BLOCK), jnp.bfloat16),
         ],
         compiler_params=VMEM,
         cost_estimate=cost(RING * ROWS * 256 * width, (RING * ROWS + 1024) * width),
@@ -411,29 +431,30 @@
     over_here = jnp.any(live & ~fits).astype(jnp.float32)
     ring = jnp.where(fits, (plane - z) & 7, -1)
 
-    first = ring_packed(
+    second_slot = jnp.where(live, (column << 5) + (plane << 2) + rank, -1)
+    first, second = both_packed(
         ring[None, :],
         place[None, :],
         (column * CAP + rank + 1).astype(jnp.float32)[None, :],
+        second_slot[None, :],
         rows,
+        slots,
         half,
     )
     first = ring_shifted(first)
-    second_slot = jnp.where(live, (column << 5) + (plane << 2) + rank, -1)
-    second = packed_rows(second_slot[None, :], rows, slots, half, half)
     second = in_plane(second.reshape(COLUMNS, CAP * RING, half))
     first[1], first[2], second = lax.optimization_barrier((first[1], first[2], second))
     second, over_there = ring_repacked(z, second)
     second = ring_shifted(second)
 
     code = jnp.where(live, (offset + 1) * resp_local + token_pos // block_len, 0)
-    note_slot = (plane * COLUMNS + column) * CAP + rank
+    note_slot = owner * CAP + rank
     hidden = last_hidden.astype(jnp.float32)
     norm = jnp.sqrt(jnp.mean(hidden * hidden, axis=-1, keepdims=True) + 1e-05)
     own_reward = jnp.sum(hidden / norm * norm_gain * reward_head, axis=-1)
     slot_match = note_slot[None, :] == jnp.arange(slots, dtype=jnp.int32)[:, None]
     codes = jnp.sum(jnp.where(slot_match, code[None, :], 0), axis=1).reshape(devices, CAP)
-    hidden_cols = hidden.reshape(resp_local, 4, RING, 8, cols).transpose(2, 1, 3, 0, 4)
+    hidden_cols = hidden.reshape(resp_local, devices, cols).swapaxes(0, 1)
     own_facts = jnp.concatenate([own_reward, norm[:, 0], over_here[None]])
     ready = jnp.concatenate(
         [
@@ -446,9 +467,8 @@
     )
     lane = jnp.arange(128, dtype=jnp.int32)
     message = jnp.where(lane[None, :] == 13, over_there[0, 0], ready)
-    message = message.reshape(RING, COLUMNS, 128)
-    message = lax.all_to_all(message, "dev_0", split_axis=0, concat_axis=0, tiled=True)
-    heard = in_plane(message.swapaxes(0, 1)).reshape(devices, 128)
+    heard = lax.all_to_all(message, GRP_DEV, split_axis=0, concat_axis=0, tiled=True)
+    heard = by_column(heard)
 
     first = ring_spread(z, first)
     first, second[1], second[7] = lax.optimization_barrier((first, second[1], second[7]))

time: 203 us -> 194 us (0.956)
  blocking collectives: 18.3 us -> 0 us
  waiting for transfers between devices: 56.5 us -> 68.2 us
  starting transfers between devices: 61 us -> 67.3 us
  local copies, waits for them, and re-layouts: 18.3 us -> 12.9 us
  Pallas kernels: 38 us -> 32.7 us
  other arithmetic: 7.5 us -> 9.9 us
    all_to_all x1 -> x0, blocking collectives: 18.3 us -> none  [local(): lax.all_to_all(message, 'dev_0', split_axis=0, concat_axis=0, tiled=True)]
    all_to_all x0 -> x1, starting transfers between devices: none -> 14.3 us  [local(): lax.all_to_all(message, GRP_DEV, split_axis=0, concat_axis=0, tiled=True)]
    all_to_all x0 -> x1, waiting for transfers between devices: none -> 8.6 us  [local(): lax.all_to_all(message, GRP_DEV, split_axis=0, concat_axis=0, tiled=True)]
    all_to_all x3 -> x2, starting transfers between devices: 21.3 us -> 13.7 us  [in_plane(): return lax.all_to_all(parts, PLANE, split_axis=0, concat_axis=0, tiled=True)]
    pallas_call x1, Pallas kernels: 10.8 us -> 6.52 us  [ring_repacked(): pl.pallas_call(ring_repack_kernel, out_shape=[jax.ShapeDtypeStruct((ROWS,...]
    all_to_all x3 -> x2, waiting for transfers between devices: 50.5 us -> 52.7 us  [in_plane(): return lax.all_to_all(parts, PLANE, split_axis=0, concat_axis=0, tiled=True)]
    reshape x2 -> x1, local copies, waits for them, and re-layouts: 2.36 us -> 0.17 us  [local(): hidden_cols = hidden.reshape(resp_local, devices, cols).swapaxes(0, 1)]
    unnamed x42 -> x32, local copies, waits for them, and re-layouts: 5.28 us -> 3.29 us
  transfers between devices with their start and end apart: 17 -> 17, of which waited for: 5 -> 5; matrix products, arithmetic and copies ran while one was open for 9% -> 8% of each run, Pallas kernels for 13% -> 9%
where the time goes in v6:
time: 194 us; the launch traced here: 193 us
  waiting for transfers between devices  68.2 us (35%)
  starting transfers between devices  67.3 us (35%)
  Pallas kernels  32.7 us (17%)
  local copies, waits for them, and re-layouts  12.9 us (7%)
  other arithmetic  9.9 us (5%)
  between operations  2.26 us (1%)
    all_to_all x2, waiting for transfers between devices, in_plane(): return lax.all_to_all(parts, PLANE, split_axis=0, concat_axis=0, tiled=True)  52.7 us
    ppermute x14, starting transfers between devices, ring_shifted(): lax.ppermute(parts[k], 'dev_0', [(i, (i + k) % RING) for i in range(RING)])  39.3 us
    all_to_all x1, starting transfers between devices, local(): lax.all_to_all(message, GRP_DEV, split_axis=0, concat_axis=0, tiled=True)  14.3 us
    all_to_all x2, starting transfers between devices, in_plane(): return lax.all_to_all(parts, PLANE, split_axis=0, concat_axis=0, tiled=True)  13.7 us
    pallas_call x1, Pallas kernels, both_packed(): pl.pallas_call(both_pack_kernel, out_shape=[jax.ShapeDtypeStruct((ROWS, h...  9.14 us
    all_to_all x1, waiting for transfers between devices, local(): lax.all_to_all(message, GRP_DEV, split_axis=0, concat_axis=0, tiled=True)  8.6 us
    ppermute x14, waiting for transfers between devices, ring_shifted(): lax.ppermute(parts[k], 'dev_0', [(i, (i + k) % RING) for i in range(RING)])  6.86 us
    pallas_call x1, Pallas kernels, ring_placed(): pl.pallas_call(ring_place_kernel, out_shape=jax.ShapeDtypeStruct(half_don...  6.57 us
  transfers between devices with their start and end apart: 17, of which 5 were waited for; matrix products, arithmetic and copies ran while one was open for 8% of the time, Pallas kernels for 9%

profile of v6, /device:TPU:1, one launch (start us, length us, event | category | flops | bytes accessed | tf_op | source)
XLA Modules:
  0.0 193.2 jit_solution(15763640749649384941)
XLA Ops:
  0.6 0.7 fusion.17
  1.4 0.8 add_select_fusion.4
  2.4 0.9 select_reduce_fusion.1
  3.6 9.1 %shard_map.104 = (bf16[88,2048]{1,0:T(8,128)(2,1)S(1)}, bf16[88,2048]{1,0:T(8,128)(2,1)S(1)}, bf16[88,2048]{1,0:T(8,128)(2,1)S(1)}, bf16[88,2048]{1,0:T(8,128)(2...) custom-call(s32[1,512]{1,0:T(1,128)S(1)} %get-tuple-element.235.ring, ...), custom_call_target="tpu_custom_call" | custom-call | flops 3623878656 | bytes 11272192 | tf_op jit(solution)/shard_map/pallas_call | solution.py:105
  12.8 8.8 %all-to-all-start.1 = ((bf16[32,32,2048]{2,1,0:T(8,128)(2,1)}), bf16[32,32,2048]{2,1,0:T(8,128)(2,1)}, u32[]{:S(2)}, u32[]{:S(2)}) async-start(bf16[32,32,2048]{2,1,0:T(8,128)(2,1)} %bitcast.103), calls=%async_computation.1 | async-start | bytes 8388608 | tf_op jit(solution)/shard_map/all_to_all | solution.py:376
  21.5 1.7 collective-permute-start
  23.3 3.0 %collective-permute-start.1 = (bf16[88,2048]{1,0:T(8,128)(2,1)S(1)}, bf16[88,2048]{1,0:T(8,128)(2,1)S(1)}, u32[]{:S(2)}, u32[]{:S(2)}) collective-permute-start(bf16[88,2048]{1,0:T(8,128)(2,1)S(1)} %get-tuple-element.91), channel_id=1, source_target_pairs={{0,16},{8,24},{16,32},{24,40},{32,48},{40,56},{48,0},{56,8},{1,17}... | collective-permute-start | bytes 1081352 | tf_op jit(solution)/shard_map/ppermute | solution.py:371
  26.3 3.8 %collective-permute-start.2 = (bf16[88,2048]{1,0:T(8,128)(2,1)}, bf16[88,2048]{1,0:T(8,128)(2,1)S(1)}, u32[]{:S(2)}, u32[]{:S(2)}) collective-permute-start(bf16[88,2048]{1,0:T(8,128)(2,1)} %get-tuple-element.99), channel_id=1, source_target_pairs={{0,24},{8,32},{16,40},{24,48},{32,56},{40,0},{48,8},{56,16},{1,25}... | collective-permute-start | bytes 1081352 | tf_op jit(solution)/shard_map/ppermute | solution.py:371
  30.0 0.5 collective-permute-start.3
  30.5 4.5 %collective-permute-start.4 = (bf16[88,2048]{1,0:T(8,128)(2,1)}, bf16[88,2048]{1,0:T(8,128)(2,1)S(1)}, u32[]{:S(2)}, u32[]{:S(2)}) collective-permute-start(bf16[88,2048]{1,0:T(8,128)(2,1)} %get-tuple-element.101), channel_id=1, source_target_pairs={{0,40},{8,48},{16,56},{24,0},{32,8},{40,16},{48,24},{56,32},{1,41}... | collective-permute-start | bytes 1081352 | tf_op jit(solution)/shard_map/ppermute | solution.py:371
  35.4 0.5 add_sqrt_fusion
  35.9 0.7 and_reduce_fusion
  36.6 0.5 iota_compare_fusion.6
  38.4 1.0 multiply_reduce_fusion.1
  39.5 0.7 pad_maximum_fusion
  40.1 2.4 %collective-permute-start.5 = (bf16[88,2048]{1,0:T(8,128)(2,1)}, bf16[88,2048]{1,0:T(8,128)(2,1)S(1)}, u32[]{:S(2)}, u32[]{:S(2)}) collective-permute-start(bf16[88,2048]{1,0:T(8,128)(2,1)} %get-tuple-element.102), channel_id=1, source_target_pairs={{0,48},{8,56},{16,0},{24,8},{32,16},{40,24},{48,32},{56,40},{1,49}... | collective-permute-start | bytes 1081352 | tf_op jit(solution)/shard_map/ppermute | solution.py:371
  42.5 2.7 %collective-permute-done.1.refs_2_ = bf16[88,2048]{1,0:T(8,128)(2,1)S(1)} collective-permute-done((bf16[88,2048]{1,0:T(8,128)(2,1)S(1)}, bf16[88,2048]{1,0:T(8,128)(2,1)S(1)}, u32[]{:S(2)}, u32[]{:S(2)}) %collective-permute-start.1) | collective-permute-done | bytes 360480 | tf_op jit(solution)/shard_map/ppermute | solution.py:371
  45.2 8.7 %collective-permute-start.6 = (bf16[88,2048]{1,0:T(8,128)(2,1)}, bf16[88,2048]{1,0:T(8,128)(2,1)S(1)}, u32[]{:S(2)}, u32[]{:S(2)}) collective-permute-start(bf16[88,2048]{1,0:T(8,128)(2,1)} %get-tuple-element.103), channel_id=1, source_target_pairs={{0,56},{8,0},{16,8},{24,16},{32,24},{40,32},{48,40},{56,48},{1,57}... | collective-permute-start | bytes 1081352 | tf_op jit(solution)/shard_map/ppermute | solution.py:371
  53.9 20.0 %all-to-all-done.1.rows_ref = bf16[32,32,2048]{2,1,0:T(8,128)(2,1)} async-done(((bf16[32,32,2048]{2,1,0:T(8,128)(2,1)}), bf16[32,32,2048]{2,1,0:T(8,128)(2,1)}, u32[]{:S(2)}, u32[]{:S(2)}) %all-to-all-start.1) | async-done | bytes 4194336 | tf_op jit(solution)/shard_map/all_to_all | solution.py:376
  73.9 6.5 %shard_map.105 = (bf16[88,2048]{1,0:T(8,128)(2,1)}, bf16[88,2048]{1,0:T(8,128)(2,1)}, bf16[88,2048]{1,0:T(8,128)(2,1)S(1)}, bf16[88,2048]{1,0:T(8,128)(2,1)S(1)}...) custom-call(s32[1]{0:T(128)} %bitcast.16.z_ref, ...), custom_call_target="tpu_custom_call" | custom-call | flops 738197504 | bytes 7077888 | tf_op jit(solution)/shard_map/pallas_call | solution.py:201
  80.5 0.7 copy-done
  81.2 0.7 copy-done.2
  81.9 0.7 copy-done.4
  82.7 0.7 copy-done.6
  83.4 0.5 slice.52
  83.9 1.6 collective-permute-start.7
  85.6 4.0 %collective-permute-start.8 = (bf16[88,2048]{1,0:T(8,128)(2,1)}, bf16[88,2048]{1,0:T(8,128)(2,1)}, u32[]{:S(2)}, u32[]{:S(2)}) collective-permute-start(bf16[88,2048]{1,0:T(8,128)(2,1)} %get-tuple-element.105), channel_id=1, source_target_pairs={{0,56},{8,0},{16,8},{24,16},{32,24},{40,32},{48,40},{56,48},{1,57}... | collective-permute-start | bytes 1081352 | tf_op jit(solution)/shard_map/ppermute | solution.py:371
  89.6 0.8 maximum_select_fusion
  90.4 0.8 copy.99
  91.2 14.3 %all-to-all-start.2 = ((f32[256,1,128]{2,1,0:T(1,128)}), f32[256,1,128]{2,1,0:T(1,128)S(1)}, u32[]{:S(2)}, u32[]{:S(2)}) async-start(f32[256,1,128]{2,1,0:T(1,128)} %copy.99), calls=%async_computation.2 | async-start | bytes 262144 | tf_op jit(solution)/shard_map/all_to_all | solution.py:470
  105.5 4.1 %shard_map.106 = bf16[32,32,2048]{2,1,0:T(8,128)(2,1)} custom-call(s32[1]{0:T(128)} %bitcast.16.z_ref, bf16[88,2048]{1,0:T(8,128)(2,1)S(1)} %get-tuple-element.96.refs_0_, bf16[88,2048]{1,0:T(8,128)(2,1)S(1)} %collective-permute-done.refs_1_, bf16[88,2048]{1,0:T(8,128)(2,1)S(1)} %collective-permute-done.1.refs_2_, ...), custom_call_target="tpu_custom_call" | custom-call | flops 1073741824 | bytes 7077888 | tf_op jit(solution)/shard_map/pallas_call | solution.py:249
  109.7 8.6 %all-to-all-done.2 = f32[256,1,128]{2,1,0:T(1,128)S(1)} async-done(((f32[256,1,128]{2,1,0:T(1,128)}), f32[256,1,128]{2,1,0:T(1,128)S(1)}, u32[]{:S(2)}, u32[]{:S(2)}) %all-to-all-start.2) | async-done | bytes 131104 | tf_op jit(solution)/shard_map/all_to_all | solution.py:470
  118.3 4.9 %all-to-all-start.3 = ((bf16[32,32,2048]{2,1,0:T(8,128)(2,1)}), bf16[32,32,2048]{2,1,0:T(8,128)(2,1)}, u32[]{:S(2)}, u32[]{:S(2)}) async-start(bf16[32,32,2048]{2,1,0:T(8,128)(2,1)} %shard_map.106), calls=%async_computation.3 | async-start | bytes 8388608 | tf_op jit(solution)/shard_map/all_to_all | solution.py:376
  123.2 0.8 dynamic_slice.3
  124.0 1.2 collective-permute-start.10
  125.2 2.3 %collective-permute-start.11 = (bf16[88,2048]{1,0:T(8,128)(2,1)S(1)}, bf16[88,2048]{1,0:T(8,128)(2,1)}, u32[]{:S(2)}, u32[]{:S(2)}) collective-permute-start(bf16[88,2048]{1,0:T(8,128)(2,1)S(1)} %copy-done.5), channel_id=1, source_target_pairs={{0,32},{8,40},{16,48},{24,56},{32,0},{40,8},{48,16},{56,24},{1,33}... | collective-permute-start | bytes 1081352 | tf_op jit(solution)/shard_map/ppermute | solution.py:371
  127.5 2.5 %collective-permute-start.12 = (bf16[88,2048]{1,0:T(8,128)(2,1)S(1)}, bf16[88,2048]{1,0:T(8,128)(2,1)}, u32[]{:S(2)}, u32[]{:S(2)}) collective-permute-start(bf16[88,2048]{1,0:T(8,128)(2,1)S(1)} %copy-done.3), channel_id=1, source_target_pairs={{0,40},{8,48},{16,56},{24,0},{32,8},{40,16},{48,24},{56,32},{1,41}... | collective-permute-start | bytes 1081352 | tf_op jit(solution)/shard_map/ppermute | solution.py:371
  130.0 3.1 %collective-permute-start.13 = (bf16[88,2048]{1,0:T(8,128)(2,1)S(1)}, bf16[88,2048]{1,0:T(8,128)(2,1)}, u32[]{:S(2)}, u32[]{:S(2)}) collective-permute-start(bf16[88,2048]{1,0:T(8,128)(2,1)S(1)} %copy-done.1), channel_id=1, source_target_pairs={{0,48},{8,56},{16,0},{24,8},{32,16},{40,24},{48,32},{56,40},{1,49}... | collective-permute-start | bytes 1081352 | tf_op jit(solution)/shard_map/ppermute | solution.py:371
  133.8 2.3 %gather_fusion = f32[512]{0:T(512)S(1)} fusion(f32[1024]{0:T(1024)S(1)} %reshape_reshape.6, s32[1024]{0:T(1024)S(1)} %pad_clamp_fusion.1), kind=kCustom, calls=%fused_computation | custom fusion | bytes 6144 | tf_op jit(solution)/shard_map/gather | solution.py:480
  136.1 2.3 %gather_fusion.1 = f32[512]{0:T(512)S(1)} fusion(f32[1024]{0:T(1024)S(1)} %reshape_reshape.6, s32[1024]{0:T(1024)S(1)} %pad_clamp_fusion), kind=kCustom, calls=%fused_computation.1 | custom fusion | bytes 6144 | tf_op jit(solution)/shard_map/gather | solution.py:480
  138.5 0.6 multiply_reduce_fusion
  140.2 0.7 slice_reduce_fusion.4
  142.2 0.5 add_add_fusion.1
  142.7 32.7 %all-to-all-done.3 = bf16[32,32,2048]{2,1,0:T(8,128)(2,1)} async-done(((bf16[32,32,2048]{2,1,0:T(8,128)(2,1)}), bf16[32,32,2048]{2,1,0:T(8,128)(2,1)}, u32[]{:S(2)}, u32[]{:S(2)}) %all-to-all-start.3) | async-done | bytes 4194336 | tf_op jit(solution)/shard_map/all_to_all | solution.py:376
  175.5 6.4 %shard_map.107 = bf16[501,4096]{1,0:T(8,128)(2,1)} custom-call(s32[1,1024]{1,0:T(1,128)S(1)} %reshape.421.target_ref, f32[1024,1]{1,0:T(8,128)S(1)} %reshape.450.scale_ref, bf16[1024,2048]{1,0:T(8,128)(2,1)} %bitcast.39.rows_ref), custom_call_target="tpu_custom_call" | custom-call | flops 2101346304 | bytes 6246400 | tf_op jit(solution)/shard_map/pallas_call | solution.py:280
  181.9 4.1 %collective-permute-done.13 = bf16[88,2048]{1,0:T(8,128)(2,1)} collective-permute-done((bf16[88,2048]{1,0:T(8,128)(2,1)S(1)}, bf16[88,2048]{1,0:T(8,128)(2,1)}, u32[]{:S(2)}, u32[]{:S(2)}) %collective-permute-start.13) | collective-permute-done | bytes 360480 | tf_op jit(solution)/shard_map/ppermute | solution.py:371
  186.0 7.2 %conditional.1 = (bf16[501,4096]{1,0:T(8,128)(2,1)}) conditional(s32[]{:T(128)} %convert_element_type.47, (s32[256,4]{1,0:T(8,128)S(1)}, f32[256,4]{1,0:T(8,128)S(1)}, s32[1]{0:T(128)}, bf16[88,2048]{1,0:T(8,128)(2,1)S(1)}, bf16[88,2048]{1,0:T(8,128)(2,1)}, /*index=5*/bf16[88,2048]{1,0:T(8,128)(2,1)}, bf16[88,2048]{1,0:T(8,128)(2,1)}, ...), branch_computations={%region_9.10_spmd, %region_10.11_spmd} | conditional | flops 8497661952 | bytes 83836984 | solution.py:527
  186.7 6.6 %branch_0_fun.1 = bf16[501,4096]{1,0:T(8,128)(2,1)} custom-call(s32[1]{0:T(128)} %get-tuple-element.45.z_ref, s32[8,128]{1,0:T(8,128)S(1)} %copy.92.target_ref, f32[8,128]{1,0:T(8,128)S(1)} %copy.93.scale_ref, bf16[88,2048]{1,0:T(8,128)(2,1)S(1)} %get-tuple-element.48.refs_0_, ...), custom_call_target="tpu_custom_call", output_to_operand_aliasing={{}: (11, {})} | custom-call | flops 2101346304 | bytes 4935680 | tf_op jit(solution)/shard_map/cond/branch_0_fun/pallas_call | solution.py:348
  (79 shorter events, 4.9 us)
Async XLA Ops:
  12.7 22.2 %copy-start.9 = (bf16[4,4096]{1,0:T(4,128)(2,1)S(1)}, bf16[4,4096]{1,0:T(4,128)(2,1)}, u32[]{:S(2)}) copy-start(bf16[4,4096]{1,0:T(4,128)(2,1)} %param.13) | copy-start | bytes 98308
  12.7 23.1 %copy-start.10 = (s32[4]{0:T(128)S(1)}, s32[4]{0:T(128)}, u32[]{:S(2)}) copy-start(s32[4]{0:T(128)} %param.14) | copy-start | bytes 52
  12.8 61.2 %all-to-all-start.1 = ((bf16[32,32,2048]{2,1,0:T(8,128)(2,1)}), bf16[32,32,2048]{2,1,0:T(8,128)(2,1)}, u32[]{:S(2)}, u32[]{:S(2)}) async-start(bf16[32,32,2048]{2,1,0:T(8,128)(2,1)} %bitcast.103), calls=%async_computation.1 | async-start | bytes 8388608 | tf_op jit(solution)/shard_map/all_to_all | solution.py:376
  21.5 18.6 %collective-permute-start = (bf16[88,2048]{1,0:T(8,128)(2,1)S(1)}, bf16[88,2048]{1,0:T(8,128)(2,1)S(1)}, u32[]{:S(2)}, u32[]{:S(2)}) collective-permute-start(bf16[88,2048]{1,0:T(8,128)(2,1)S(1)} %get-tuple-element.90), channel_id=1, source_target_pairs={{0,8},{8,16},{16,24},{24,32},{32,40},{40,48},{48,56},{56,0},{1,9},... | collective-permute-start | bytes 1081352 | tf_op jit(solution)/shard_map/ppermute | solution.py:371
  23.3 21.9 %collective-permute-start.1 = (bf16[88,2048]{1,0:T(8,128)(2,1)S(1)}, bf16[88,2048]{1,0:T(8,128)(2,1)S(1)}, u32[]{:S(2)}, u32[]{:S(2)}) collective-permute-start(bf16[88,2048]{1,0:T(8,128)(2,1)S(1)} %get-tuple-element.91), channel_id=1, source_target_pairs={{0,16},{8,24},{16,32},{24,40},{32,48},{40,56},{48,0},{56,8},{1,17}... | collective-permute-start | bytes 1081352 | tf_op jit(solution)/shard_map/ppermute | solution.py:371
  26.3 57.7 %collective-permute-start.2 = (bf16[88,2048]{1,0:T(8,128)(2,1)}, bf16[88,2048]{1,0:T(8,128)(2,1)S(1)}, u32[]{:S(2)}, u32[]{:S(2)}) collective-permute-start(bf16[88,2048]{1,0:T(8,128)(2,1)} %get-tuple-element.99), channel_id=1, source_target_pairs={{0,24},{8,32},{16,40},{24,48},{32,56},{40,0},{48,8},{56,16},{1,25}... | collective-permute-start | bytes 1081352 | tf_op jit(solution)/shard_map/ppermute | solution.py:371
  30.0 55.6 %collective-permute-start.3 = (bf16[88,2048]{1,0:T(8,128)(2,1)}, bf16[88,2048]{1,0:T(8,128)(2,1)S(1)}, u32[]{:S(2)}, u32[]{:S(2)}) collective-permute-start(bf16[88,2048]{1,0:T(8,128)(2,1)} %get-tuple-element.100), channel_id=1, source_target_pairs={{0,32},{8,40},{16,48},{24,56},{32,0},{40,8},{48,16},{56,24},{1,33}... | collective-permute-start | bytes 1081352 | tf_op jit(solution)/shard_map/ppermute | solution.py:371
  30.5 75.0 %collective-permute-start.4 = (bf16[88,2048]{1,0:T(8,128)(2,1)}, bf16[88,2048]{1,0:T(8,128)(2,1)S(1)}, u32[]{:S(2)}, u32[]{:S(2)}) collective-permute-start(bf16[88,2048]{1,0:T(8,128)(2,1)} %get-tuple-element.101), channel_id=1, source_target_pairs={{0,40},{8,48},{16,56},{24,0},{32,8},{40,16},{48,24},{56,32},{1,41}... | collective-permute-start | bytes 1081352 | tf_op jit(solution)/shard_map/ppermute | solution.py:371
  40.1 65.4 %collective-permute-start.5 = (bf16[88,2048]{1,0:T(8,128)(2,1)}, bf16[88,2048]{1,0:T(8,128)(2,1)S(1)}, u32[]{:S(2)}, u32[]{:S(2)}) collective-permute-start(bf16[88,2048]{1,0:T(8,128)(2,1)} %get-tuple-element.102), channel_id=1, source_target_pairs={{0,48},{8,56},{16,0},{24,8},{32,16},{40,24},{48,32},{56,40},{1,49}... | collective-permute-start | bytes 1081352 | tf_op jit(solution)/shard_map/ppermute | solution.py:371
  45.2 60.3 %collective-permute-start.6 = (bf16[88,2048]{1,0:T(8,128)(2,1)}, bf16[88,2048]{1,0:T(8,128)(2,1)S(1)}, u32[]{:S(2)}, u32[]{:S(2)}) collective-permute-start(bf16[88,2048]{1,0:T(8,128)(2,1)} %get-tuple-element.103), channel_id=1, source_target_pairs={{0,56},{8,0},{16,8},{24,16},{32,24},{40,32},{48,40},{56,48},{1,57}... | collective-permute-start | bytes 1081352 | tf_op jit(solution)/shard_map/ppermute | solution.py:371
  73.9 15.7 %copy-start.13 = (pred[128]{0:T(512)(128)(4,1)S(1)}, pred[128]{0:T(512)(128)(4,1)}, u32[]{:S(2)}) copy-start(pred[128]{0:T(512)(128)(4,1)} %iota_compare_fusion.6) | copy-start | bytes 388
  80.5 0.7 copy-start
  81.2 0.7 copy-start.2
  81.9 0.7 copy-start.4
  82.7 0.7 copy-start.6
  83.9 25.7 %collective-permute-start.7 = (bf16[88,2048]{1,0:T(8,128)(2,1)}, bf16[88,2048]{1,0:T(8,128)(2,1)}, u32[]{:S(2)}, u32[]{:S(2)}) collective-permute-start(bf16[88,2048]{1,0:T(8,128)(2,1)} %get-tuple-element.104), channel_id=1, source_target_pairs={{0,8},{8,16},{16,24},{24,32},{32,40},{40,48},{48,56},{56,0},{1,9},... | collective-permute-start | bytes 1081352 | tf_op jit(solution)/shard_map/ppermute | solution.py:371
  85.6 24.1 %collective-permute-start.8 = (bf16[88,2048]{1,0:T(8,128)(2,1)}, bf16[88,2048]{1,0:T(8,128)(2,1)}, u32[]{:S(2)}, u32[]{:S(2)}) collective-permute-start(bf16[88,2048]{1,0:T(8,128)(2,1)} %get-tuple-element.105), channel_id=1, source_target_pairs={{0,56},{8,0},{16,8},{24,16},{32,24},{40,32},{48,40},{56,48},{1,57}... | collective-permute-start | bytes 1081352 | tf_op jit(solution)/shard_map/ppermute | solution.py:371
  91.2 27.1 %all-to-all-start.2 = ((f32[256,1,128]{2,1,0:T(1,128)}), f32[256,1,128]{2,1,0:T(1,128)S(1)}, u32[]{:S(2)}, u32[]{:S(2)}) async-start(f32[256,1,128]{2,1,0:T(1,128)} %copy.99), calls=%async_computation.2 | async-start | bytes 262144 | tf_op jit(solution)/shard_map/all_to_all | solution.py:470
  109.6 14.3 %copy-start.11 = (s32[512]{0:T(512)S(1)}, s32[512]{0:T(512)}, u32[]{:S(2)}) copy-start(s32[512]{0:T(512)} %param.17) | copy-start | bytes 6148
  109.6 14.3 %copy-start.12 = (s32[512]{0:T(512)S(1)}, s32[512]{0:T(512)}, u32[]{:S(2)}) copy-start(s32[512]{0:T(512)} %param.18) | copy-start | bytes 6148
  109.6 14.4 %copy-start.7 = (bf16[88,2048]{1,0:T(8,128)(2,1)S(1)}, bf16[88,2048]{1,0:T(8,128)(2,1)}, u32[]{:S(2)}) copy-start(bf16[88,2048]{1,0:T(8,128)(2,1)} %copy-done.6) | copy-start | bytes 1081348
  109.6 15.6 %copy-start.5 = (bf16[88,2048]{1,0:T(8,128)(2,1)S(1)}, bf16[88,2048]{1,0:T(8,128)(2,1)}, u32[]{:S(2)}) copy-start(bf16[88,2048]{1,0:T(8,128)(2,1)} %copy-done.4) | copy-start | bytes 1081348
  109.6 17.9 %copy-start.3 = (bf16[88,2048]{1,0:T(8,128)(2,1)S(1)}, bf16[88,2048]{1,0:T(8,128)(2,1)}, u32[]{:S(2)}) copy-start(bf16[88,2048]{1,0:T(8,128)(2,1)} %copy-done.2) | copy-start | bytes 1081348
  109.6 20.3 %copy-start.1 = (bf16[88,2048]{1,0:T(8,128)(2,1)S(1)}, bf16[88,2048]{1,0:T(8,128)(2,1)}, u32[]{:S(2)}) copy-start(bf16[88,2048]{1,0:T(8,128)(2,1)} %copy-done) | copy-start | bytes 1081348
  118.3 57.2 %all-to-all-start.3 = ((bf16[32,32,2048]{2,1,0:T(8,128)(2,1)}), bf16[32,32,2048]{2,1,0:T(8,128)(2,1)}, u32[]{:S(2)}, u32[]{:S(2)}) async-start(bf16[32,32,2048]{2,1,0:T(8,128)(2,1)} %shard_map.106), calls=%async_computation.3 | async-start | bytes 8388608 | tf_op jit(solution)/shard_map/all_to_all | solution.py:376
  124.0 57.8 %collective-permute-start.10 = (bf16[88,2048]{1,0:T(8,128)(2,1)S(1)}, bf16[88,2048]{1,0:T(8,128)(2,1)}, u32[]{:S(2)}, u32[]{:S(2)}) collective-permute-start(bf16[88,2048]{1,0:T(8,128)(2,1)S(1)} %copy-done.7), channel_id=1, source_target_pairs={{0,24},{8,32},{16,40},{24,48},{32,56},{40,0},{48,8},{56,16},{1,25}... | collective-permute-start | bytes 1081352 | tf_op jit(solution)/shard_map/ppermute | solution.py:371
  125.2 56.7 %collective-permute-start.11 = (bf16[88,2048]{1,0:T(8,128)(2,1)S(1)}, bf16[88,2048]{1,0:T(8,128)(2,1)}, u32[]{:S(2)}, u32[]{:S(2)}) collective-permute-start(bf16[88,2048]{1,0:T(8,128)(2,1)S(1)} %copy-done.5), channel_id=1, source_target_pairs={{0,32},{8,40},{16,48},{24,56},{32,0},{40,8},{48,16},{56,24},{1,33}... | collective-permute-start | bytes 1081352 | tf_op jit(solution)/shard_map/ppermute | solution.py:371
  127.5 54.3 %collective-permute-start.12 = (bf16[88,2048]{1,0:T(8,128)(2,1)S(1)}, bf16[88,2048]{1,0:T(8,128)(2,1)}, u32[]{:S(2)}, u32[]{:S(2)}) collective-permute-start(bf16[88,2048]{1,0:T(8,128)(2,1)S(1)} %copy-done.3), channel_id=1, source_target_pairs={{0,40},{8,48},{16,56},{24,0},{32,8},{40,16},{48,24},{56,32},{1,41}... | collective-permute-start | bytes 1081352 | tf_op jit(solution)/shard_map/ppermute | solution.py:371
  130.0 56.0 %collective-permute-start.13 = (bf16[88,2048]{1,0:T(8,128)(2,1)S(1)}, bf16[88,2048]{1,0:T(8,128)(2,1)}, u32[]{:S(2)}, u32[]{:S(2)}) collective-permute-start(bf16[88,2048]{1,0:T(8,128)(2,1)S(1)} %copy-done.1), channel_id=1, source_target_pairs={{0,48},{8,56},{16,0},{24,8},{32,16},{40,24},{48,32},{56,40},{1,49}... | collective-permute-start | bytes 1081352 | tf_op jit(solution)/shard_map/ppermute | solution.py:371
  133.1 52.9 %collective-permute-start.9 = (bf16[88,2048]{1,0:T(8,128)(2,1)S(1)}, bf16[88,2048]{1,0:T(8,128)(2,1)}, u32[]{:S(2)}, u32[]{:S(2)}) collective-permute-start(bf16[88,2048]{1,0:T(8,128)(2,1)S(1)} %get-tuple-element.107), channel_id=1, source_target_pairs={{0,16},{8,24},{16,32},{24,40},{32,48},{40,56},{48,0},{56,8},{1,17}... | collective-permute-start | bytes 1081352 | tf_op jit(solution)/shard_map/ppermute | solution.py:371
  175.4 10.6 %copy-start.8 = (bf16[88,2048]{1,0:T(8,128)(2,1)S(1)}, bf16[88,2048]{1,0:T(8,128)(2,1)}, u32[]{:S(2)}) copy-start(bf16[88,2048]{1,0:T(8,128)(2,1)} %get-tuple-element.95) | copy-start | bytes 1081348

commit v7 on v5

--- a/solution.py
+++ b/solution.py
@@ -15,7 +15,8 @@
 RING = 8
 COLUMNS = 32
 ROWS = 88
-BLOCK = 512
+BLOCK = 256
+FIRST = 2304
 VMEM = pltpu.CompilerParams(vmem_limit_bytes=48 << 20)
 NT = (((1,), (1,)), ((), ()))
 
@@ -113,8 +114,8 @@
 
 
 def ring_repack_kernel(z_ref, rows_ref, *refs):
-    outs, flag_ref = refs[:RING], refs[RING]
-    hot_ref, note_ref, place_ref, held_ref = refs[RING + 1 :]
+    outs = refs[:RING]
+    hot_ref, note_ref, place_ref, held_ref, sent_ref = refs[RING:]
     width = rows_ref.shape[2]
     step = pl.program_id(0)
 
@@ -124,7 +125,6 @@
         before = rows_of((256, 256))
         slot = lax.broadcasted_iota(jnp.int32, (256, 256), 1)
         ahead = ((before < slot) & (((before ^ slot) & 4) == 0)).astype(jnp.bfloat16)
-        over = jnp.zeros((8, 256), jnp.float32)
         for q in range(RING // 2):
             total = jnp.zeros((COLUMNS, 8, 128), jnp.float32)
             for c in range(0, width, 128):
@@ -139,18 +139,16 @@
             place = jnp.dot(
                 used.astype(jnp.bfloat16), ahead, preferred_element_type=jnp.float32
             )
-            over = jnp.maximum(over, jnp.where(used & (place >= ROWS - 1), 1.0, 0.0))
             place_ref[8 * q : 8 * q + 8, :] = jnp.where(
                 used & (place < ROWS - 1), place, -1.0
             ).astype(jnp.int32)
-        flag_ref[...] = jnp.broadcast_to(jnp.max(over, axis=1, keepdims=True), (8, 128))
         codes = (((lane >> 3) << 2) + (lane & 3) + 1).astype(jnp.float32).astype(jnp.bfloat16)
         for k in range(RING):
             plane = (z_ref[0] + k) & 7
             start = pl.multiple_of((plane >> 1) * 8, 8)
             mine = ((lane >> 2) & 1) == (plane & 1)
             place = jnp.where(mine, place_ref[pl.ds(start, 8), :], -1)[0:1, :]
-            hot_ref[k] = (rows_of((ROWS, 256)) == place).astype(jnp.bfloat16)
+            hot_ref[plane] = (rows_of((ROWS, 256)) == place).astype(jnp.bfloat16)
             note_ref[8 * k : 8 * k + 8, :] = lax.dot_general(
                 codes,
                 (rows_of((128, 256)) == place).astype(jnp.bfloat16),
@@ -162,40 +160,43 @@
     for q in range(RING // 2):
         rows = rows_ref[:, 8 * q : 8 * q + 8, pl.ds(first, BLOCK)].astype(jnp.float32)
         held_ref[256 * q : 256 * q + 256, :] = rows.reshape(256, BLOCK).astype(jnp.bfloat16)
+    for q in range(RING // 2):
+        hot = jnp.concatenate([hot_ref[2 * q], hot_ref[2 * q + 1]], axis=0)
+        picked = jnp.dot(
+            hot, held_ref[256 * q : 256 * q + 256, :], preferred_element_type=jnp.float32
+        )
+        for half in (0, 1):
+            k = (2 * q + half - z_ref[0]) & 7
+            sent_ref[k] = picked[half * ROWS : (half + 1) * ROWS].astype(jnp.bfloat16)
     for k in range(RING):
-        start = pl.multiple_of((((z_ref[0] + k) & 7) >> 1) * 256, 256)
-        picked = jnp.dot(
-            hot_ref[k], held_ref[pl.ds(start, 256), :], preferred_element_type=jnp.float32
-        )
-        outs[k][...] = picked.astype(jnp.bfloat16)
-
-        @pl.when(step == 0)
-        def _():
+        outs[k][...] = sent_ref[k]
+
+    @pl.when(step == 0)
+    def _():
+        for k in range(RING):
+            tail = sent_ref[k, ROWS - 8 : ROWS, 0:128].astype(jnp.float32)
             note = jnp.where(rows_of((8, 128)) == 7, note_ref[8 * k : 8 * k + 8, :], 0.0)
-            outs[k][ROWS - 8 : ROWS, 0:128] = (picked[ROWS - 8 :, :128] + note).astype(
-                jnp.bfloat16
-            )
+            outs[k][ROWS - 8 : ROWS, 0:128] = (tail + note).astype(jnp.bfloat16)
 
 
 def ring_repacked(z, rows):
     width = rows.shape[2]
-    out = pl.pallas_call(
+    return pl.pallas_call(
         ring_repack_kernel,
-        out_shape=[jax.ShapeDtypeStruct((ROWS, width), jnp.bfloat16)] * RING
-        + [jax.ShapeDtypeStruct((8, 128), jnp.float32)],
+        out_shape=[jax.ShapeDtypeStruct((ROWS, width), jnp.bfloat16)] * RING,
         grid=(width // BLOCK,),
         in_specs=[pl.BlockSpec(memory_space=pltpu.SMEM), whole(rows.shape)],
-        out_specs=[pl.BlockSpec((ROWS, BLOCK), lambda j: (0, j))] * RING + [whole((8, 128))],
+        out_specs=[pl.BlockSpec((ROWS, BLOCK), lambda j: (0, j))] * RING,
         scratch_shapes=[
             pltpu.VMEM((RING, ROWS, 256), jnp.bfloat16),
             pltpu.VMEM((8 * RING, 128), jnp.float32),
             pltpu.VMEM((4 * RING, 256), jnp.int32),
             pltpu.VMEM((128 * RING, BLOCK), jnp.bfloat16),
+            pltpu.VMEM((RING, ROWS, BLOCK), jnp.bfloat16),
         ],
         compiler_params=VMEM,
         cost_estimate=cost(RING * ROWS * 256 * width, (RING * ROWS + 1024) * width),
     )(z, rows)
-    return out[:RING], out[RING]
 
 
 def ring_spread_kernel(z_ref, *refs):
@@ -385,7 +386,7 @@
 ):
     resp_local, block_len = token_ids.shape
     width = sensitivity.shape[2]
-    half = width // 2
+    second_width = width - FIRST
     tok_local = resp_local * block_len
     devices = shard_owner.shape[0]
     slots = devices * CAP
@@ -416,47 +417,54 @@
         place[None, :],
         (column * CAP + rank + 1).astype(jnp.float32)[None, :],
         rows,
-        half,
+        FIRST,
+    )
+    first, code, hidden = lax.optimization_barrier(
+        (
+            first,
+            jnp.where(live, (offset + 1) * resp_local + token_pos // block_len, 0),
+            last_hidden,
+        )
     )
     first = ring_shifted(first)
-    second_slot = jnp.where(live, (column << 5) + (plane << 2) + rank, -1)
-    second = packed_rows(second_slot[None, :], rows, slots, half, half)
-    second = in_plane(second.reshape(COLUMNS, CAP * RING, half))
-    first[1], first[2], second = lax.optimization_barrier((first[1], first[2], second))
-    second, over_there = ring_repacked(z, second)
-    second = ring_shifted(second)
-
-    code = jnp.where(live, (offset + 1) * resp_local + token_pos // block_len, 0)
-    note_slot = (plane * COLUMNS + column) * CAP + rank
-    hidden = last_hidden.astype(jnp.float32)
+
+    hidden = hidden.astype(jnp.float32)
     norm = jnp.sqrt(jnp.mean(hidden * hidden, axis=-1, keepdims=True) + 1e-05)
     own_reward = jnp.sum(hidden / norm * norm_gain * reward_head, axis=-1)
-    slot_match = note_slot[None, :] == jnp.arange(slots, dtype=jnp.int32)[:, None]
+    slot_match = (owner * CAP + rank)[None, :] == jnp.arange(slots, dtype=jnp.int32)[:, None]
     codes = jnp.sum(jnp.where(slot_match, code[None, :], 0), axis=1).reshape(devices, CAP)
-    hidden_cols = hidden.reshape(resp_local, 4, RING, 8, cols).transpose(2, 1, 3, 0, 4)
-    own_facts = jnp.concatenate([own_reward, norm[:, 0], over_here[None]])
-    ready = jnp.concatenate(
+    owner_match = (owner[:, None] == jnp.arange(devices, dtype=jnp.int32)[None, :]) & live[:, None]
+    counts = jnp.sum(owner_match.astype(jnp.float32), axis=0)
+    own_facts = jnp.concatenate(
+        [own_reward, norm[:, 0], over_here[None], jnp.zeros((51,), jnp.float32)]
+    )
+    message = jnp.concatenate(
         [
             codes.astype(jnp.float32),
-            jnp.broadcast_to(own_facts[None, :], (devices, 9)),
-            jnp.zeros((devices, 51), jnp.float32),
-            hidden_cols.reshape(devices, resp_local * cols),
+            jnp.broadcast_to(own_facts[None, :], (devices, 60)),
+            hidden.reshape(resp_local, devices, cols).swapaxes(0, 1).reshape(devices, -1),
+            jnp.broadcast_to((counts[:128] * 8 + counts[128:])[None, :], (devices, 128)),
         ],
         axis=1,
     )
-    lane = jnp.arange(128, dtype=jnp.int32)
-    message = jnp.where(lane[None, :] == 13, over_there[0, 0], ready)
-    message = message.reshape(RING, COLUMNS, 128)
-    message = lax.all_to_all(message, "dev_0", split_axis=0, concat_axis=0, tiled=True)
-    heard = in_plane(message.swapaxes(0, 1)).reshape(devices, 128)
-
-    first = ring_spread(z, first)
-    first, second[1], second[7] = lax.optimization_barrier((first, second[1], second[7]))
-    first = in_plane(first)
+    message, first[1], first[7] = lax.optimization_barrier((message, first[1], first[7]))
+    heard = lax.all_to_all(message, GRP_DEV, split_axis=0, concat_axis=0, tiled=True)
+
+    second_slot = jnp.where(live, (column << 5) + (plane << 2) + rank, -1)
+    second_slot, message, first[2], first[6] = lax.optimization_barrier(
+        (second_slot, message, first[2], first[6])
+    )
+    second = packed_rows(second_slot[None, :], rows, slots, FIRST, second_width)
+    second, heard = lax.optimization_barrier((second, heard))
+    second = in_plane(second.reshape(COLUMNS, CAP * RING, second_width))
+    heard = by_column(heard)
 
     arrived_code = heard[:, :CAP].astype(jnp.int32)
     reward = by_device(heard[:, 4:8]).reshape(responses)
-    any_over = jnp.max(heard[:, 12:14]) > 0
+    coded = heard[:, 128:]
+    upper = jnp.floor(coded * 0.125)
+    plane_counts = jnp.stack([upper, coded - 8 * upper]).reshape(2, COLUMNS, RING, 128).sum(axis=1)
+    any_over = (jnp.max(heard[:, 12]) > 0) | (jnp.max(plane_counts) > ROWS - 1)
     margin = reward[chosen_index] - reward[rejected_index]
     push = -jax.nn.sigmoid(-margin)
     every = jnp.arange(responses, dtype=jnp.int32)
@@ -477,10 +485,16 @@
         scale = jnp.where(response_in == r, reward_grad[:, r : r + 1], scale)
     target = arrived_code // resp_local - 1
     scale = jnp.where(target >= 0, scale, 0.0)
+    target, scale, head_grad, first = lax.optimization_barrier((target, scale, head_grad, first))
+    first = ring_spread(z, first)
+    first, second = lax.optimization_barrier((first, second))
+    first = in_plane(first)
+    second = ring_shifted(ring_repacked(z, second))
+
     half_done = placed_rows(
         target.reshape(1, slots),
         scale.reshape(slots, 1),
-        first.reshape(slots, half),
+        first.reshape(slots, FIRST),
         shard_rows,
         width,
     )

time: 203 us -> 219 us (1.079)
  the two profiles are of different devices: /device:TPU:1 before, /device:TPU:40 now
where the time goes in v7:
time: 219 us; the launch traced here: 218 us
  waiting for transfers between devices  73.7 us (34%)
  starting transfers between devices  58.7 us (27%)
  Pallas kernels  43.5 us (20%)
  local copies, waits for them, and re-layouts  26.8 us (12%)
  other arithmetic  11.9 us (5%)
  between operations  2.94 us (1%)
    ppermute x14, waiting for transfers between devices, ring_shifted(): lax.ppermute(parts[k], 'dev_0', [(i, (i + k) % RING) for i in range(RING)])  50.8 us
    ppermute x14, starting transfers between devices, ring_shifted(): lax.ppermute(parts[k], 'dev_0', [(i, (i + k) % RING) for i in range(RING)])  24.3 us
    all_to_all x1, starting transfers between devices, local(): lax.all_to_all(message, GRP_DEV, split_axis=0, concat_axis=0, tiled=True)  20.9 us
    all_to_all x2, waiting for transfers between devices, in_plane(): return lax.all_to_all(parts, PLANE, split_axis=0, concat_axis=0, tiled=True)  17 us
    all_to_all x2, starting transfers between devices, in_plane(): return lax.all_to_all(parts, PLANE, split_axis=0, concat_axis=0, tiled=True)  13.5 us
    pallas_call x1, Pallas kernels, placed_rows(): pl.pallas_call(place_kernel, out_shape=jax.ShapeDtypeStruct((shard_rows,...  9.39 us
    unnamed x33, local copies, waits for them, and re-layouts  8.66 us
    pallas_call x1, Pallas kernels, ring_packed(): pl.pallas_call(ring_pack_kernel, out_shape=[jax.ShapeDtypeStruct((ROWS, w...  8.24 us
  transfers between devices with their start and end apart: 17, of which 7 were waited for; matrix products, arithmetic and copies ran while one was open for 14% of the time, Pallas kernels for 13%

profile of v7, /device:TPU:40, one launch (start us, length us, event | category | flops | bytes accessed | tf_op | source)
XLA Modules:
  0.0 217.7 jit_solution(3855063434488407495)
XLA Ops:
  1.4 0.8 fusion.11
  2.4 0.9 select_reduce_fusion.1
  4.4 8.2 %shard_map.104 = (bf16[88,2304]{1,0:T(8,128)(2,1)S(1)}, bf16[88,2304]{1,0:T(8,128)(2,1)}, bf16[88,2304]{1,0:T(8,128)(2,1)S(1)}, bf16[88,2304]{1,0:T(8,128)(2,1)}...) custom-call(s32[1,512]{1,0:T(1,128)S(1)} %fusion.9.ring_ref, ...), custom_call_target="tpu_custom_call" | custom-call | flops 1660944384 | bytes 5603328 | tf_op jit(solution)/shard_map/pallas_call | solution.py:101
  13.3 1.9 collective-permute-start
  15.4 4.4 %collective-permute-start.2 = (bf16[88,2304]{1,0:T(8,128)(2,1)S(1)}, bf16[88,2304]{1,0:T(8,128)(2,1)S(1)}, u32[]{:S(2)}, u32[]{:S(2)}) collective-permute-start(bf16[88,2304]{1,0:T(8,128)(2,1)S(1)} %get-tuple-element.119), channel_id=1, source_target_pairs={{0,16},{8,24},{16,32},{24,40},{32,48},{40,56},{48,0},{56,8},{1,17}... | collective-permute-start | bytes 1216520 | tf_op jit(solution)/shard_map/ppermute | solution.py:352
  19.7 1.0 collective-permute-start.3
  20.9 1.0 reshape.287
  24.6 1.2 copy.93
  27.5 2.1 collective-permute-done.refs_1_
  29.6 0.9 all_to_all.17
  30.4 20.9 %all-to-all-start.1 = ((f32[256,1,256]{2,1,0:T(1,128)}), f32[256,1,256]{2,1,0:T(1,128)S(1)}, u32[]{:S(2)}, u32[]{:S(2)}) async-start(f32[256,1,256]{2,1,0:T(1,128)} %all_to_all.17), calls=%async_computation.1 | async-start | bytes 524288 | tf_op jit(solution)/shard_map/all_to_all | solution.py:451
  51.4 5.9 %shard_map.105 = bf16[1024,1792]{1,0:T(8,128)(2,1)S(1)} custom-call(s32[1,512]{1,0:T(1,128)S(1)} %bitcast.101, bf16[512,4096]{1,0:T(8,128)(2,1)} %bitcast.111), custom_call_target="tpu_custom_call" | custom-call | flops 1879048192 | bytes 5505024 | tf_op jit(solution)/shard_map/pallas_call | solution.py:49
  57.3 1.8 copy-done
  59.1 5.9 %all-to-all-done.1 = f32[256,1,256]{2,1,0:T(1,128)S(1)} async-done(((f32[256,1,256]{2,1,0:T(1,128)}), f32[256,1,256]{2,1,0:T(1,128)S(1)}, u32[]{:S(2)}, u32[]{:S(2)}) %all-to-all-start.1) | async-done | bytes 262176 | tf_op jit(solution)/shard_map/all_to_all | solution.py:451
  65.7 5.9 %all-to-all-start.2 = ((bf16[32,32,1792]{2,1,0:T(8,128)(2,1)}), bf16[32,32,1792]{2,1,0:T(8,128)(2,1)}, u32[]{:S(2)}, u32[]{:S(2)}) async-start(bf16[32,32,1792]{2,1,0:T(8,128)(2,1)} %bitcast.98), calls=%async_computation.2 | async-start | bytes 7340032 | tf_op jit(solution)/shard_map/all_to_all | solution.py:357
  71.6 1.6 collective-permute-start.4
  73.2 3.7 %collective-permute-start.5 = (bf16[88,2304]{1,0:T(8,128)(2,1)}, bf16[88,2304]{1,0:T(8,128)(2,1)S(1)}, u32[]{:S(2)}, u32[]{:S(2)}) collective-permute-start(bf16[88,2304]{1,0:T(8,128)(2,1)} %get-tuple-element.127), channel_id=1, source_target_pairs={{0,32},{8,40},{16,48},{24,56},{32,0},{40,8},{48,16},{56,24},{1,33}... | collective-permute-start | bytes 1216520 | tf_op jit(solution)/shard_map/ppermute | solution.py:352
  76.9 1.3 collective-permute-start.6
  78.2 1.3 dynamic_slice.3
  79.5 1.0 copy.95
  81.3 1.0 reshape_reshape.6
  82.4 2.3 %gather_fusion = f32[512]{0:T(512)S(1)} fusion(f32[1024]{0:T(1024)S(1)} %reshape_reshape.6, s32[1024]{0:T(1024)S(1)} %pad_clamp_fusion.1), kind=kCustom, calls=%fused_computation | custom fusion | bytes 6144 | tf_op jit(solution)/shard_map/gather | solution.py:468
  84.7 2.3 %gather_fusion.1 = f32[512]{0:T(512)S(1)} fusion(f32[1024]{0:T(1024)S(1)} %reshape_reshape.6, s32[1024]{0:T(1024)S(1)} %pad_clamp_fusion), kind=kCustom, calls=%fused_computation.1 | custom fusion | bytes 6144 | tf_op jit(solution)/shard_map/gather | solution.py:468
  87.5 0.8 reshape_reshape.7
  88.3 1.8 copy.97
  90.2 0.9 reshape.292
  91.1 1.0 fusion.23
  92.1 1.0 copy.116
  93.1 1.0 copy.117
  94.0 1.6 copy.118
  95.6 1.6 copy.119
  97.2 1.0 slice_reduce_fusion.2
  98.2 1.0 multiply_reduce_fusion.5
  99.2 0.9 select_select_fusion
  101.3 3.7 %collective-permute-done.4.refs_3_ = bf16[88,2304]{1,0:T(8,128)(2,1)S(1)} collective-permute-done((bf16[88,2304]{1,0:T(8,128)(2,1)}, bf16[88,2304]{1,0:T(8,128)(2,1)S(1)}, u32[]{:S(2)}, u32[]{:S(2)}) %collective-permute-start.4) | collective-permute-done | bytes 405536 | tf_op jit(solution)/shard_map/ppermute | solution.py:352
  105.0 18.2 %collective-permute-done.6.refs_5_ = bf16[88,2304]{1,0:T(8,128)(2,1)S(1)} collective-permute-done((bf16[88,2304]{1,0:T(8,128)(2,1)}, bf16[88,2304]{1,0:T(8,128)(2,1)S(1)}, u32[]{:S(2)}, u32[]{:S(2)}) %collective-permute-start.6) | collective-permute-done | bytes 405536 | tf_op jit(solution)/shard_map/ppermute | solution.py:352
  123.3 6.5 %shard_map.106 = bf16[32,32,2304]{2,1,0:T(8,128)(2,1)} custom-call(s32[1]{0:T(128)} %bitcast.37.z_ref, bf16[88,2304]{1,0:T(8,128)(2,1)S(1)} %get-tuple-element.133.refs_0_, bf16[88,2304]{1,0:T(8,128)(2,1)S(1)} %collective-permute-done.refs_1_, bf16[88,2304]{1,0:T(8,128)(2,1)S(1)} %collective-permute-done.2.refs_2_, ...), custom_call_target="tpu_custom_call" | custom-call | flops 1207959552 | bytes 7962624 | tf_op jit(solution)/shard_map/pallas_call | solution.py:230
  129.7 7.5 %all-to-all-start.3 = ((bf16[32,32,2304]{2,1,0:T(8,128)(2,1)}), bf16[32,32,2304]{2,1,0:T(8,128)(2,1)}, u32[]{:S(2)}, u32[]{:S(2)}) async-start(bf16[32,32,2304]{2,1,0:T(8,128)(2,1)} %shard_map.106), calls=%async_computation.3 | async-start | bytes 9437184 | tf_op jit(solution)/shard_map/all_to_all | solution.py:357
  137.3 6.1 %shard_map.107 = (bf16[88,1792]{1,0:T(8,128)(2,1)S(1)}, bf16[88,1792]{1,0:T(8,128)(2,1)S(1)}, bf16[88,1792]{1,0:T(8,128)(2,1)S(1)}, bf16[88,1792]{1,0:T(8,128)(2...) custom-call(s32[1]{0:T(128)} %bitcast.37.z_ref, ...), custom_call_target="tpu_custom_call" | custom-call | flops 645922816 | bytes 6193152 | tf_op jit(solution)/shard_map/pallas_call | solution.py:184
  143.4 2.5 %collective-permute-start.10 = (bf16[88,1792]{1,0:T(8,128)(2,1)S(1)}, bf16[88,1792]{1,0:T(8,128)(2,1)S(1)}, u32[]{:S(2)}, u32[]{:S(2)}) collective-permute-start(bf16[88,1792]{1,0:T(8,128)(2,1)S(1)} %get-tuple-element.147), channel_id=1, source_target_pairs={{0,32},{8,40},{16,48},{24,56},{32,0},{40,8},{48,16},{56,24},{1,33}... | collective-permute-start | bytes 946184 | tf_op jit(solution)/shard_map/ppermute | solution.py:352
  145.9 2.4 %collective-permute-start.11 = (bf16[88,1792]{1,0:T(8,128)(2,1)S(1)}, bf16[88,1792]{1,0:T(8,128)(2,1)S(1)}, u32[]{:S(2)}, u32[]{:S(2)}) collective-permute-start(bf16[88,1792]{1,0:T(8,128)(2,1)S(1)} %get-tuple-element.148), channel_id=1, source_target_pairs={{0,40},{8,48},{16,56},{24,0},{32,8},{40,16},{48,24},{56,32},{1,41}... | collective-permute-start | bytes 946184 | tf_op jit(solution)/shard_map/ppermute | solution.py:352
  148.7 4.2 %collective-permute-start.13 = (bf16[88,1792]{1,0:T(8,128)(2,1)S(1)}, bf16[88,1792]{1,0:T(8,128)(2,1)}, u32[]{:S(2)}, u32[]{:S(2)}) collective-permute-start(bf16[88,1792]{1,0:T(8,128)(2,1)S(1)} %get-tuple-element.150), channel_id=1, source_target_pairs={{0,56},{8,0},{16,8},{24,16},{32,24},{40,32},{48,40},{56,48},{1,57}... | collective-permute-start | bytes 946184 | tf_op jit(solution)/shard_map/ppermute | solution.py:352
  153.0 13.5 %collective-permute-done.10 = bf16[88,1792]{1,0:T(8,128)(2,1)S(1)} collective-permute-done((bf16[88,1792]{1,0:T(8,128)(2,1)S(1)}, bf16[88,1792]{1,0:T(8,128)(2,1)S(1)}, u32[]{:S(2)}, u32[]{:S(2)}) %collective-permute-start.10) | collective-permute-done | bytes 315424 | tf_op jit(solution)/shard_map/ppermute | solution.py:352
  166.7 13.3 %collective-permute-done.11 = bf16[88,1792]{1,0:T(8,128)(2,1)S(1)} collective-permute-done((bf16[88,1792]{1,0:T(8,128)(2,1)S(1)}, bf16[88,1792]{1,0:T(8,128)(2,1)S(1)}, u32[]{:S(2)}, u32[]{:S(2)}) %collective-permute-start.11) | collective-permute-done | bytes 315424 | tf_op jit(solution)/shard_map/ppermute | solution.py:352
  183.0 17.0 %all-to-all-done.3 = bf16[32,32,2304]{2,1,0:T(8,128)(2,1)} async-done(((bf16[32,32,2304]{2,1,0:T(8,128)(2,1)}), bf16[32,32,2304]{2,1,0:T(8,128)(2,1)}, u32[]{:S(2)}, u32[]{:S(2)}) %all-to-all-start.3) | async-done | bytes 4718624 | tf_op jit(solution)/shard_map/all_to_all | solution.py:357
  200.0 9.4 %shard_map.108 = bf16[501,4096]{1,0:T(8,128)(2,1)} custom-call(s32[1,1024]{1,0:T(1,128)S(1)} %reshape.294.target_ref, f32[1024,1]{1,0:T(8,128)S(1)} %reshape.321.scale_ref, bf16[1024,2304]{1,0:T(8,128)(2,1)} %bitcast.39.rows_ref), custom_call_target="tpu_custom_call" | custom-call | flops 2364014592 | bytes 7027200 | tf_op jit(solution)/shard_map/pallas_call | solution.py:261
  209.4 8.3 %conditional.1 = (bf16[501,4096]{1,0:T(8,128)(2,1)}) conditional(s32[]{:T(128)} %convert_element_type.48, (s32[256,4]{1,0:T(8,128)S(1)}, f32[256,4]{1,0:T(8,128)S(1)}, s32[1]{0:T(128)}, bf16[88,1792]{1,0:T(8,128)(2,1)S(1)}, bf16[88,1792]{1,0:T(8,128)(2,1)}, /*index=5*/bf16[88,1792]{1,0:T(8,128)(2,1)}, bf16[88,1792]{1,0:T(8,128)(2,1)}, ...), branch_computations={%region_16.17_spmd, %region_17.18_spmd} | conditional | flops 8497661440 | bytes 83835432 | solution.py:521
  210.3 7.5 %branch_0_fun.1 = bf16[501,4096]{1,0:T(8,128)(2,1)} custom-call(s32[1]{0:T(128)} %get-tuple-element.29.z_ref, s32[8,128]{1,0:T(8,128)S(1)} %copy.88.target_ref, f32[8,128]{1,0:T(8,128)S(1)} %copy.89.scale_ref, bf16[88,1792]{1,0:T(8,128)(2,1)S(1)} %get-tuple-element.42.refs_0_, ...), custom_call_target="tpu_custom_call", output_to_operand_aliasing={{}: (11, {})} | custom-call | flops 1838678016 | bytes 4318720 | tf_op jit(solution)/shard_map/cond/branch_0_fun/pallas_call | solution.py:329
  (82 shorter events, 13.0 us)
Async XLA Ops:
  4.3 16.5 %copy-start.7 = (bf16[4,4096]{1,0:T(4,128)(2,1)S(1)}, bf16[4,4096]{1,0:T(4,128)(2,1)}, u32[]{:S(2)}) copy-start(bf16[4,4096]{1,0:T(4,128)(2,1)} %param.13) | copy-start | bytes 98308
  4.3 18.6 %copy-start.8 = (f32[4096]{0:T(1024)S(1)}, f32[4096]{0:T(1024)}, u32[]{:S(2)}) copy-start(f32[4096]{0:T(1024)} %param.16) | copy-start | bytes 49156
  4.3 18.6 %copy-start.9 = (f32[4096]{0:T(1024)S(1)}, f32[4096]{0:T(1024)}, u32[]{:S(2)}) copy-start(f32[4096]{0:T(1024)} %param.15) | copy-start | bytes 49156
  4.3 18.9 %copy-start.10 = (s32[4]{0:T(128)S(1)}, s32[4]{0:T(128)}, u32[]{:S(2)}) copy-start(s32[4]{0:T(128)} %param.14) | copy-start | bytes 52
  12.6 0.7 copy-start.1
  13.3 16.2 %collective-permute-start = (bf16[88,2304]{1,0:T(8,128)(2,1)}, bf16[88,2304]{1,0:T(8,128)(2,1)S(1)}, u32[]{:S(2)}, u32[]{:S(2)}) collective-permute-start(bf16[88,2304]{1,0:T(8,128)(2,1)} %get-tuple-element.116), channel_id=1, source_target_pairs={{0,8},{8,16},{16,24},{24,32},{32,40},{40,48},{48,56},{56,0},{1,9},... | collective-permute-start | bytes 1216520 | tf_op jit(solution)/shard_map/ppermute | solution.py:352
  15.3 14.3 %collective-permute-start.1 = (bf16[88,2304]{1,0:T(8,128)(2,1)S(1)}, bf16[88,2304]{1,0:T(8,128)(2,1)S(1)}, u32[]{:S(2)}, u32[]{:S(2)}) collective-permute-start(bf16[88,2304]{1,0:T(8,128)(2,1)S(1)} %get-tuple-element.117), channel_id=1, source_target_pairs={{0,56},{8,0},{16,8},{24,16},{32,24},{40,32},{48,40},{56,48},{1,57}... | collective-permute-start | bytes 1216520 | tf_op jit(solution)/shard_map/ppermute | solution.py:352
  15.4 36.0 %collective-permute-start.2 = (bf16[88,2304]{1,0:T(8,128)(2,1)S(1)}, bf16[88,2304]{1,0:T(8,128)(2,1)S(1)}, u32[]{:S(2)}, u32[]{:S(2)}) collective-permute-start(bf16[88,2304]{1,0:T(8,128)(2,1)S(1)} %get-tuple-element.119), channel_id=1, source_target_pairs={{0,16},{8,24},{16,32},{24,40},{32,48},{40,56},{48,0},{56,8},{1,17}... | collective-permute-start | bytes 1216520 | tf_op jit(solution)/shard_map/ppermute | solution.py:352
  19.7 31.6 %collective-permute-start.3 = (bf16[88,2304]{1,0:T(8,128)(2,1)S(1)}, bf16[88,2304]{1,0:T(8,128)(2,1)S(1)}, u32[]{:S(2)}, u32[]{:S(2)}) collective-permute-start(bf16[88,2304]{1,0:T(8,128)(2,1)S(1)} %get-tuple-element.120), channel_id=1, source_target_pairs={{0,48},{8,56},{16,0},{24,8},{32,16},{40,24},{48,32},{56,40},{1,49}... | collective-permute-start | bytes 1216520 | tf_op jit(solution)/shard_map/ppermute | solution.py:352
  22.1 3.6 %copy-start.11 = (f32[4]{0:T(128)}, f32[4]{0:T(128)S(1)}, u32[]{:S(2)}) copy-start(f32[4]{0:T(128)S(1)} %add_sqrt_fusion) | copy-start | bytes 52
  30.4 34.5 %all-to-all-start.1 = ((f32[256,1,256]{2,1,0:T(1,128)}), f32[256,1,256]{2,1,0:T(1,128)S(1)}, u32[]{:S(2)}, u32[]{:S(2)}) async-start(f32[256,1,256]{2,1,0:T(1,128)} %all_to_all.17), calls=%async_computation.1 | async-start | bytes 524288 | tf_op jit(solution)/shard_map/all_to_all | solution.py:451
  57.3 1.8 copy-start
  65.7 13.8 %copy-start.12 = (s32[512]{0:T(512)S(1)}, s32[512]{0:T(512)}, u32[]{:S(2)}) copy-start(s32[512]{0:T(512)} %param.17) | copy-start | bytes 6148
  65.7 13.8 %copy-start.13 = (s32[512]{0:T(512)S(1)}, s32[512]{0:T(512)}, u32[]{:S(2)}) copy-start(s32[512]{0:T(512)} %param.18) | copy-start | bytes 6148
  65.7 64.0 %all-to-all-start.2 = ((bf16[32,32,1792]{2,1,0:T(8,128)(2,1)}), bf16[32,32,1792]{2,1,0:T(8,128)(2,1)}, u32[]{:S(2)}, u32[]{:S(2)}) async-start(bf16[32,32,1792]{2,1,0:T(8,128)(2,1)} %bitcast.98), calls=%async_computation.2 | async-start | bytes 7340032 | tf_op jit(solution)/shard_map/all_to_all | solution.py:357
  71.6 33.4 %collective-permute-start.4 = (bf16[88,2304]{1,0:T(8,128)(2,1)}, bf16[88,2304]{1,0:T(8,128)(2,1)S(1)}, u32[]{:S(2)}, u32[]{:S(2)}) collective-permute-start(bf16[88,2304]{1,0:T(8,128)(2,1)} %get-tuple-element.126), channel_id=1, source_target_pairs={{0,24},{8,32},{16,40},{24,48},{32,56},{40,0},{48,8},{56,16},{1,25}... | collective-permute-start | bytes 1216520 | tf_op jit(solution)/shard_map/ppermute | solution.py:352
  73.2 31.8 %collective-permute-start.5 = (bf16[88,2304]{1,0:T(8,128)(2,1)}, bf16[88,2304]{1,0:T(8,128)(2,1)S(1)}, u32[]{:S(2)}, u32[]{:S(2)}) collective-permute-start(bf16[88,2304]{1,0:T(8,128)(2,1)} %get-tuple-element.127), channel_id=1, source_target_pairs={{0,32},{8,40},{16,48},{24,56},{32,0},{40,8},{48,16},{56,24},{1,33}... | collective-permute-start | bytes 1216520 | tf_op jit(solution)/shard_map/ppermute | solution.py:352
  76.9 46.3 %collective-permute-start.6 = (bf16[88,2304]{1,0:T(8,128)(2,1)}, bf16[88,2304]{1,0:T(8,128)(2,1)S(1)}, u32[]{:S(2)}, u32[]{:S(2)}) collective-permute-start(bf16[88,2304]{1,0:T(8,128)(2,1)} %copy-done.1), channel_id=1, source_target_pairs={{0,40},{8,48},{16,56},{24,0},{32,8},{40,16},{48,24},{56,32},{1,41}... | collective-permute-start | bytes 1216520 | tf_op jit(solution)/shard_map/ppermute | solution.py:352
  129.7 70.2 %all-to-all-start.3 = ((bf16[32,32,2304]{2,1,0:T(8,128)(2,1)}), bf16[32,32,2304]{2,1,0:T(8,128)(2,1)}, u32[]{:S(2)}, u32[]{:S(2)}) async-start(bf16[32,32,2304]{2,1,0:T(8,128)(2,1)} %shard_map.106), calls=%async_computation.3 | async-start | bytes 9437184 | tf_op jit(solution)/shard_map/all_to_all | solution.py:357
  137.3 43.4 %copy-start.2 = (f32[256,4]{1,0:T(8,128)S(1)}, f32[256,4]{1,0:T(8,128)}, u32[]{:S(2)}) copy-start(f32[256,4]{1,0:T(8,128)} %get-tuple-element.132) | copy-start | bytes 12292
  137.3 43.6 %copy-start.3 = (s32[256,4]{1,0:T(8,128)S(1)}, s32[256,4]{1,0:T(8,128)}, u32[]{:S(2)}) copy-start(s32[256,4]{1,0:T(8,128)} %fusion.4) | copy-start | bytes 12292
  143.4 23.0 %collective-permute-start.10 = (bf16[88,1792]{1,0:T(8,128)(2,1)S(1)}, bf16[88,1792]{1,0:T(8,128)(2,1)S(1)}, u32[]{:S(2)}, u32[]{:S(2)}) collective-permute-start(bf16[88,1792]{1,0:T(8,128)(2,1)S(1)} %get-tuple-element.147), channel_id=1, source_target_pairs={{0,32},{8,40},{16,48},{24,56},{32,0},{40,8},{48,16},{56,24},{1,33}... | collective-permute-start | bytes 946184 | tf_op jit(solution)/shard_map/ppermute | solution.py:352
  145.9 34.0 %collective-permute-start.11 = (bf16[88,1792]{1,0:T(8,128)(2,1)S(1)}, bf16[88,1792]{1,0:T(8,128)(2,1)S(1)}, u32[]{:S(2)}, u32[]{:S(2)}) collective-permute-start(bf16[88,1792]{1,0:T(8,128)(2,1)S(1)} %get-tuple-element.148), channel_id=1, source_target_pairs={{0,40},{8,48},{16,56},{24,0},{32,8},{40,16},{48,24},{56,32},{1,41}... | collective-permute-start | bytes 946184 | tf_op jit(solution)/shard_map/ppermute | solution.py:352
  148.3 61.0 %collective-permute-start.12 = (bf16[88,1792]{1,0:T(8,128)(2,1)S(1)}, bf16[88,1792]{1,0:T(8,128)(2,1)}, u32[]{:S(2)}, u32[]{:S(2)}) collective-permute-start(bf16[88,1792]{1,0:T(8,128)(2,1)S(1)} %get-tuple-element.149), channel_id=1, source_target_pairs={{0,48},{8,56},{16,0},{24,8},{32,16},{40,24},{48,32},{56,40},{1,49}... | collective-permute-start | bytes 946184 | tf_op jit(solution)/shard_map/ppermute | solution.py:352
  148.7 60.6 %collective-permute-start.13 = (bf16[88,1792]{1,0:T(8,128)(2,1)S(1)}, bf16[88,1792]{1,0:T(8,128)(2,1)}, u32[]{:S(2)}, u32[]{:S(2)}) collective-permute-start(bf16[88,1792]{1,0:T(8,128)(2,1)S(1)} %get-tuple-element.150), channel_id=1, source_target_pairs={{0,56},{8,0},{16,8},{24,16},{32,24},{40,32},{48,40},{56,48},{1,57}... | collective-permute-start | bytes 946184 | tf_op jit(solution)/shard_map/ppermute | solution.py:352
  153.0 56.4 %collective-permute-start.7 = (bf16[88,1792]{1,0:T(8,128)(2,1)S(1)}, bf16[88,1792]{1,0:T(8,128)(2,1)}, u32[]{:S(2)}, u32[]{:S(2)}) collective-permute-start(bf16[88,1792]{1,0:T(8,128)(2,1)S(1)} %get-tuple-element.144), channel_id=1, source_target_pairs={{0,8},{8,16},{16,24},{24,32},{32,40},{40,48},{48,56},{56,0},{1,9},... | collective-permute-start | bytes 946184 | tf_op jit(solution)/shard_map/ppermute | solution.py:352
  166.5 14.0 %copy-start.4 = (bf16[88,1792]{1,0:T(8,128)(2,1)}, bf16[88,1792]{1,0:T(8,128)(2,1)S(1)}, u32[]{:S(2)}) copy-start(bf16[88,1792]{1,0:T(8,128)(2,1)S(1)} %collective-permute-done.10) | copy-start | bytes 946180
  166.5 42.9 %collective-permute-start.8 = (bf16[88,1792]{1,0:T(8,128)(2,1)S(1)}, bf16[88,1792]{1,0:T(8,128)(2,1)}, u32[]{:S(2)}, u32[]{:S(2)}) collective-permute-start(bf16[88,1792]{1,0:T(8,128)(2,1)S(1)} %get-tuple-element.145), channel_id=1, source_target_pairs={{0,16},{8,24},{16,32},{24,40},{32,48},{40,56},{48,0},{56,8},{1,17}... | collective-permute-start | bytes 946184 | tf_op jit(solution)/shard_map/ppermute | solution.py:352
  179.9 0.7 copy-start.6
  179.9 29.4 %collective-permute-start.9 = (bf16[88,1792]{1,0:T(8,128)(2,1)S(1)}, bf16[88,1792]{1,0:T(8,128)(2,1)}, u32[]{:S(2)}, u32[]{:S(2)}) collective-permute-start(bf16[88,1792]{1,0:T(8,128)(2,1)S(1)} %get-tuple-element.146), channel_id=1, source_target_pairs={{0,24},{8,32},{16,40},{24,48},{32,56},{40,0},{48,8},{56,16},{1,25}... | collective-permute-start | bytes 946184 | tf_op jit(solution)/shard_map/ppermute | solution.py:352
  200.0 9.4 %copy-start.5 = (bf16[88,1792]{1,0:T(8,128)(2,1)S(1)}, bf16[88,1792]{1,0:T(8,128)(2,1)}, u32[]{:S(2)}) copy-start(bf16[88,1792]{1,0:T(8,128)(2,1)} %copy-done.4) | copy-start | bytes 946180

commit v8 on v5

--- a/solution.py
+++ b/solution.py
@@ -16,7 +16,7 @@
 COLUMNS = 32
 ROWS = 88
 BLOCK = 512
-VMEM = pltpu.CompilerParams(vmem_limit_bytes=48 << 20)
+VMEM = pltpu.CompilerParams(vmem_limit_bytes=62 << 20)
 NT = (((1,), (1,)), ((), ()))
 
 
@@ -114,7 +114,7 @@
 
 def ring_repack_kernel(z_ref, rows_ref, *refs):
     outs, flag_ref = refs[:RING], refs[RING]
-    hot_ref, note_ref, place_ref, held_ref = refs[RING + 1 :]
+    hot_ref, note_ref, place_ref, held_ref, sent_ref = refs[RING + 1 :]
     width = rows_ref.shape[2]
     step = pl.program_id(0)
 
@@ -150,7 +150,7 @@
             start = pl.multiple_of((plane >> 1) * 8, 8)
             mine = ((lane >> 2) & 1) == (plane & 1)
             place = jnp.where(mine, place_ref[pl.ds(start, 8), :], -1)[0:1, :]
-            hot_ref[k] = (rows_of((ROWS, 256)) == place).astype(jnp.bfloat16)
+            hot_ref[plane] = (rows_of((ROWS, 256)) == place).astype(jnp.bfloat16)
             note_ref[8 * k : 8 * k + 8, :] = lax.dot_general(
                 codes,
                 (rows_of((128, 256)) == place).astype(jnp.bfloat16),
@@ -162,19 +162,23 @@
     for q in range(RING // 2):
         rows = rows_ref[:, 8 * q : 8 * q + 8, pl.ds(first, BLOCK)].astype(jnp.float32)
         held_ref[256 * q : 256 * q + 256, :] = rows.reshape(256, BLOCK).astype(jnp.bfloat16)
+    for q in range(RING // 2):
+        hot = jnp.concatenate([hot_ref[2 * q], hot_ref[2 * q + 1]], axis=0)
+        picked = jnp.dot(
+            hot, held_ref[256 * q : 256 * q + 256, :], preferred_element_type=jnp.float32
+        )
+        for half in (0, 1):
+            k = (2 * q + half - z_ref[0]) & 7
+            sent_ref[k] = picked[half * ROWS : (half + 1) * ROWS].astype(jnp.bfloat16)
     for k in range(RING):
-        start = pl.multiple_of((((z_ref[0] + k) & 7) >> 1) * 256, 256)
-        picked = jnp.dot(
-            hot_ref[k], held_ref[pl.ds(start, 256), :], preferred_element_type=jnp.float32
-        )
-        outs[k][...] = picked.astype(jnp.bfloat16)
-
-        @pl.when(step == 0)
-        def _():
+        outs[k][...] = sent_ref[k]
+
+    @pl.when(step == 0)
+    def _():
+        for k in range(RING):
+            tail = sent_ref[k, ROWS - 8 : ROWS, 0:128].astype(jnp.float32)
             note = jnp.where(rows_of((8, 128)) == 7, note_ref[8 * k : 8 * k + 8, :], 0.0)
-            outs[k][ROWS - 8 : ROWS, 0:128] = (picked[ROWS - 8 :, :128] + note).astype(
-                jnp.bfloat16
-            )
+            outs[k][ROWS - 8 : ROWS, 0:128] = (tail + note).astype(jnp.bfloat16)
 
 
 def ring_repacked(z, rows):
@@ -191,9 +195,10 @@
             pltpu.VMEM((8 * RING, 128), jnp.float32),
             pltpu.VMEM((4 * RING, 256), jnp.int32),
             pltpu.VMEM((128 * RING, BLOCK), jnp.bfloat16),
+            pltpu.VMEM((RING, ROWS, BLOCK), jnp.bfloat16),
         ],
         compiler_params=VMEM,
-        cost_estimate=cost(RING * ROWS * 256 * width, (RING * ROWS + 1024) * width),
+        cost_estimate=cost(RING * ROWS * 1024 * width, (RING * ROWS + 1024) * width),
     )(z, rows)
     return out[:RING], out[RING]
 
@@ -238,7 +243,7 @@
             pltpu.VMEM((128 * RING, BLOCK), jnp.bfloat16),
         ],
         compiler_params=VMEM,
-        cost_estimate=cost(1024 * 256 * width, (1024 + ROWS * RING) * width),
+        cost_estimate=cost(1024 * 1024 * width, (1024 + ROWS * RING) * width),
     )(z, *parts)
 
 
@@ -427,13 +432,13 @@
     second = ring_shifted(second)
 
     code = jnp.where(live, (offset + 1) * resp_local + token_pos // block_len, 0)
-    note_slot = (plane * COLUMNS + column) * CAP + rank
+    note_slot = owner * CAP + rank
     hidden = last_hidden.astype(jnp.float32)
     norm = jnp.sqrt(jnp.mean(hidden * hidden, axis=-1, keepdims=True) + 1e-05)
     own_reward = jnp.sum(hidden / norm * norm_gain * reward_head, axis=-1)
     slot_match = note_slot[None, :] == jnp.arange(slots, dtype=jnp.int32)[:, None]
     codes = jnp.sum(jnp.where(slot_match, code[None, :], 0), axis=1).reshape(devices, CAP)
-    hidden_cols = hidden.reshape(resp_local, 4, RING, 8, cols).transpose(2, 1, 3, 0, 4)
+    hidden_cols = hidden.reshape(resp_local, devices, cols).swapaxes(0, 1)
     own_facts = jnp.concatenate([own_reward, norm[:, 0], over_here[None]])
     ready = jnp.concatenate(
         [
@@ -446,9 +451,8 @@
     )
     lane = jnp.arange(128, dtype=jnp.int32)
     message = jnp.where(lane[None, :] == 13, over_there[0, 0], ready)
-    message = message.reshape(RING, COLUMNS, 128)
-    message = lax.all_to_all(message, "dev_0", split_axis=0, concat_axis=0, tiled=True)
-    heard = in_plane(message.swapaxes(0, 1)).reshape(devices, 128)
+    heard = lax.all_to_all(message, GRP_DEV, split_axis=0, concat_axis=0, tiled=True)
+    heard = by_column(heard)
 
     first = ring_spread(z, first)
     first, second[1], second[7] = lax.optimization_barrier((first, second[1], second[7]))

time: 203 us -> 191 us (0.941)
  blocking collectives: 18.3 us -> 0 us
  starting transfers between devices: 61 us -> 70.5 us
  local copies, waits for them, and re-layouts: 18.3 us -> 14 us
    all_to_all x1 -> x0, blocking collectives: 18.3 us -> none  [local(): lax.all_to_all(message, 'dev_0', split_axis=0, concat_axis=0, tiled=True)]
    all_to_all x0 -> x1, starting transfers between devices: none -> 14 us  [local(): lax.all_to_all(message, GRP_DEV, split_axis=0, concat_axis=0, tiled=True)]
    ppermute x14, waiting for transfers between devices: 6.03 us -> 12.9 us  [ring_shifted(): lax.ppermute(parts[k], 'dev_0', [(i, (i + k) % RING) for i in range(RING)])]
    all_to_all x3 -> x2, waiting for transfers between devices: 50.5 us -> 44.4 us  [in_plane(): return lax.all_to_all(parts, PLANE, split_axis=0, concat_axis=0, tiled=True)]
    all_to_all x3 -> x2, starting transfers between devices: 21.3 us -> 16.6 us  [in_plane(): return lax.all_to_all(parts, PLANE, split_axis=0, concat_axis=0, tiled=True)]
    pallas_call x1, Pallas kernels: 10.8 us -> 6.71 us  [ring_repacked(): pl.pallas_call(ring_repack_kernel, out_shape=[jax.ShapeDtypeStruct((ROWS,...]
    unnamed x42 -> x28, local copies, waits for them, and re-layouts: 5.28 us -> 1.79 us
    reshape x2 -> x1, local copies, waits for them, and re-layouts: 2.36 us -> 0.17 us  [local(): hidden_cols = hidden.reshape(resp_local, devices, cols).swapaxes(0, 1)]
  transfers between devices with their start and end apart: 17 -> 17, of which waited for: 5 -> 5; matrix products, arithmetic and copies ran while one was open for 9% -> 8% of each run, Pallas kernels for 13% -> 13%
where the time goes in v8:
time: 191 us; the launch traced here: 190 us
  starting transfers between devices  70.5 us (37%)
  waiting for transfers between devices  57.3 us (30%)
  Pallas kernels  37 us (19%)
  local copies, waits for them, and re-layouts  14 us (7%)
  other arithmetic  8.69 us (5%)
  between operations  2.27 us (1%)
    all_to_all x2, waiting for transfers between devices, in_plane(): return lax.all_to_all(parts, PLANE, split_axis=0, concat_axis=0, tiled=True)  44.4 us
    ppermute x14, starting transfers between devices, ring_shifted(): lax.ppermute(parts[k], 'dev_0', [(i, (i + k) % RING) for i in range(RING)])  39.8 us
    all_to_all x2, starting transfers between devices, in_plane(): return lax.all_to_all(parts, PLANE, split_axis=0, concat_axis=0, tiled=True)  16.6 us
    all_to_all x1, starting transfers between devices, local(): lax.all_to_all(message, GRP_DEV, split_axis=0, concat_axis=0, tiled=True)  14 us
    ppermute x14, waiting for transfers between devices, ring_shifted(): lax.ppermute(parts[k], 'dev_0', [(i, (i + k) % RING) for i in range(RING)])  12.9 us
    pallas_call x1, Pallas kernels, ring_repacked(): pl.pallas_call(ring_repack_kernel, out_shape=[jax.ShapeDtypeStruct((ROWS,...  6.71 us
    pallas_call x1, Pallas kernels, placed_rows(): pl.pallas_call(place_kernel, out_shape=jax.ShapeDtypeStruct((shard_rows,...  6.49 us
    pallas_call x1, Pallas kernels, ring_placed(): pl.pallas_call(ring_place_kernel, out_shape=jax.ShapeDtypeStruct(half_don...  6.36 us
  transfers between devices with their start and end apart: 17, of which 5 were waited for; matrix products, arithmetic and copies ran while one was open for 8% of the time, Pallas kernels for 13%

profile of v8, /device:TPU:1, one launch (start us, length us, event | category | flops | bytes accessed | tf_op | source)
XLA Modules:
  0.0 189.7 jit_solution(7103933122341982156)
XLA Ops:
  0.6 0.7 fusion.17
  1.4 0.8 add_select_fusion.4
  2.4 0.9 select_reduce_fusion.1
  3.3 0.6 add_add_fusion
  4.2 0.6 bitcast_select_fusion
  4.8 5.9 %shard_map.105 = bf16[1024,2048]{1,0:T(8,128)(2,1)} custom-call(s32[1,512]{1,0:T(1,128)} %get-tuple-element.232.slot_ref, bf16[512,4096]{1,0:T(8,128)(2,1)} %bitcast.100), custom_call_target="tpu_custom_call" | custom-call | flops 2147483648 | bytes 6291456 | tf_op jit(solution)/shard_map/pallas_call | solution.py:48
  10.6 8.6 %all-to-all-start.1 = ((bf16[32,32,2048]{2,1,0:T(8,128)(2,1)}), bf16[32,32,2048]{2,1,0:T(8,128)(2,1)}, u32[]{:S(2)}, u32[]{:S(2)}) async-start(bf16[32,32,2048]{2,1,0:T(8,128)(2,1)} %bitcast.99), calls=%async_computation.1 | async-start | bytes 8388608 | tf_op jit(solution)/shard_map/all_to_all | solution.py:361
  19.4 5.7 %shard_map.104 = (bf16[88,2048]{1,0:T(8,128)(2,1)}, bf16[88,2048]{1,0:T(8,128)(2,1)}, bf16[88,2048]{1,0:T(8,128)(2,1)}, bf16[88,2048]{1,0:T(8,128)(2,1)}, bf16[8...) custom-call(s32[1,512]{1,0:T(1,128)} %get-tuple-element.233.ring_ref, ...), custom_call_target="tpu_custom_call" | custom-call | flops 1476395008 | bytes 4980736 | tf_op jit(solution)/shard_map/pallas_call | solution.py:100
  25.0 1.7 collective-permute-start
  26.7 3.0 %collective-permute-start.1 = (bf16[88,2048]{1,0:T(8,128)(2,1)}, bf16[88,2048]{1,0:T(8,128)(2,1)S(1)}, u32[]{:S(2)}, u32[]{:S(2)}) collective-permute-start(bf16[88,2048]{1,0:T(8,128)(2,1)} %get-tuple-element.90), channel_id=1, source_target_pairs={{0,16},{8,24},{16,32},{24,40},{32,48},{40,56},{48,0},{56,8},{1,17}... | collective-permute-start | bytes 1081352 | tf_op jit(solution)/shard_map/ppermute | solution.py:356
  29.7 3.8 %collective-permute-start.2 = (bf16[88,2048]{1,0:T(8,128)(2,1)}, bf16[88,2048]{1,0:T(8,128)(2,1)S(1)}, u32[]{:S(2)}, u32[]{:S(2)}) collective-permute-start(bf16[88,2048]{1,0:T(8,128)(2,1)} %get-tuple-element.97), channel_id=1, source_target_pairs={{0,24},{8,32},{16,40},{24,48},{32,56},{40,0},{48,8},{56,16},{1,25}... | collective-permute-start | bytes 1081352 | tf_op jit(solution)/shard_map/ppermute | solution.py:356
  33.5 0.4 collective-permute-start.3
  33.9 4.5 %collective-permute-start.4 = (bf16[88,2048]{1,0:T(8,128)(2,1)}, bf16[88,2048]{1,0:T(8,128)(2,1)}, u32[]{:S(2)}, u32[]{:S(2)}) collective-permute-start(bf16[88,2048]{1,0:T(8,128)(2,1)} %get-tuple-element.99), channel_id=1, source_target_pairs={{0,40},{8,48},{16,56},{24,0},{32,8},{40,16},{48,24},{56,32},{1,41}... | collective-permute-start | bytes 1081352 | tf_op jit(solution)/shard_map/ppermute | solution.py:356
  38.9 0.7 and_reduce_fusion
  41.2 2.4 %collective-permute-start.5 = (bf16[88,2048]{1,0:T(8,128)(2,1)}, bf16[88,2048]{1,0:T(8,128)(2,1)}, u32[]{:S(2)}, u32[]{:S(2)}) collective-permute-start(bf16[88,2048]{1,0:T(8,128)(2,1)} %get-tuple-element.100), channel_id=1, source_target_pairs={{0,48},{8,56},{16,0},{24,8},{32,16},{40,24},{48,32},{56,40},{1,49}... | collective-permute-start | bytes 1081352 | tf_op jit(solution)/shard_map/ppermute | solution.py:356
  43.7 5.2 %collective-permute-done.1.refs_2_ = bf16[88,2048]{1,0:T(8,128)(2,1)S(1)} collective-permute-done((bf16[88,2048]{1,0:T(8,128)(2,1)}, bf16[88,2048]{1,0:T(8,128)(2,1)S(1)}, u32[]{:S(2)}, u32[]{:S(2)}) %collective-permute-start.1) | collective-permute-done | bytes 360480 | tf_op jit(solution)/shard_map/ppermute | solution.py:356
  48.9 8.8 %collective-permute-start.6 = (bf16[88,2048]{1,0:T(8,128)(2,1)}, bf16[88,2048]{1,0:T(8,128)(2,1)}, u32[]{:S(2)}, u32[]{:S(2)}) collective-permute-start(bf16[88,2048]{1,0:T(8,128)(2,1)} %get-tuple-element.101), channel_id=1, source_target_pairs={{0,56},{8,0},{16,8},{24,16},{32,24},{40,32},{48,40},{56,48},{1,57}... | collective-permute-start | bytes 1081352 | tf_op jit(solution)/shard_map/ppermute | solution.py:356
  57.6 14.1 %all-to-all-done.1.rows_ref = bf16[32,32,2048]{2,1,0:T(8,128)(2,1)} async-done(((bf16[32,32,2048]{2,1,0:T(8,128)(2,1)}), bf16[32,32,2048]{2,1,0:T(8,128)(2,1)}, u32[]{:S(2)}, u32[]{:S(2)}) %all-to-all-start.1) | async-done | bytes 4194336 | tf_op jit(solution)/shard_map/all_to_all | solution.py:361
  71.7 6.7 %shard_map.106 = (bf16[88,2048]{1,0:T(8,128)(2,1)S(1)}, bf16[88,2048]{1,0:T(8,128)(2,1)}, bf16[88,2048]{1,0:T(8,128)(2,1)}, bf16[88,2048]{1,0:T(8,128)(2,1)}, bf...) custom-call(s32[1]{0:T(128)} %bitcast.16.z_ref, ...), custom_call_target="tpu_custom_call" | custom-call | flops 2952790016 | bytes 7077888 | tf_op jit(solution)/shard_map/pallas_call | solution.py:186
  78.4 1.2 slice.52
  79.6 0.8 maximum_select_fusion
  80.4 0.8 copy.99
  81.1 14.0 %all-to-all-start.2 = ((f32[256,1,128]{2,1,0:T(1,128)}), f32[256,1,128]{2,1,0:T(1,128)S(1)}, u32[]{:S(2)}, u32[]{:S(2)}) async-start(f32[256,1,128]{2,1,0:T(1,128)} %copy.99), calls=%async_computation.2 | async-start | bytes 262144 | tf_op jit(solution)/shard_map/all_to_all | solution.py:454
  95.2 0.7 copy-done.10
  95.9 1.5 collective-permute-start.7
  97.4 0.7 copy-done.11
  98.1 2.8 %collective-permute-start.8 = (bf16[88,2048]{1,0:T(8,128)(2,1)}, bf16[88,2048]{1,0:T(8,128)(2,1)S(1)}, u32[]{:S(2)}, u32[]{:S(2)}) collective-permute-start(bf16[88,2048]{1,0:T(8,128)(2,1)} %get-tuple-element.103), channel_id=1, source_target_pairs={{0,56},{8,0},{16,8},{24,16},{32,24},{40,32},{48,40},{56,48},{1,57}... | collective-permute-start | bytes 1081352 | tf_op jit(solution)/shard_map/ppermute | solution.py:356
  101.0 5.9 %shard_map.107 = bf16[32,32,2048]{2,1,0:T(8,128)(2,1)} custom-call(s32[1]{0:T(128)} %bitcast.16.z_ref, bf16[88,2048]{1,0:T(8,128)(2,1)} %get-tuple-element.94.refs_0_, bf16[88,2048]{1,0:T(8,128)(2,1)} %copy-done.8, bf16[88,2048]{1,0:T(8,128)(2,1)} %copy-done.9, bf16[88,2048]{1,0:T(8,128)(2,1)} %copy-done.10, bf16[88,2048]{1,0:T(8,128)(2,1)} %copy-done.11, ...), custom_call_target="tpu_custom_call" | custom-call | flops 4294967296 | bytes 7077888 | tf_op jit(solution)/shard_map/pallas_call | solution.py:234
  106.9 2.6 %collective-permute-done.7 = bf16[88,2048]{1,0:T(8,128)(2,1)S(1)} collective-permute-done((bf16[88,2048]{1,0:T(8,128)(2,1)}, bf16[88,2048]{1,0:T(8,128)(2,1)S(1)}, u32[]{:S(2)}, u32[]{:S(2)}) %collective-permute-start.7) | collective-permute-done | bytes 360480 | tf_op jit(solution)/shard_map/ppermute | solution.py:356
  109.5 8.0 %all-to-all-start.3 = ((bf16[32,32,2048]{2,1,0:T(8,128)(2,1)}), bf16[32,32,2048]{2,1,0:T(8,128)(2,1)}, u32[]{:S(2)}, u32[]{:S(2)}) async-start(bf16[32,32,2048]{2,1,0:T(8,128)(2,1)} %shard_map.107), calls=%async_computation.3 | async-start | bytes 8388608 | tf_op jit(solution)/shard_map/all_to_all | solution.py:361
  117.7 5.0 %collective-permute-start.10 = (bf16[88,2048]{1,0:T(8,128)(2,1)}, bf16[88,2048]{1,0:T(8,128)(2,1)S(1)}, u32[]{:S(2)}, u32[]{:S(2)}) collective-permute-start(bf16[88,2048]{1,0:T(8,128)(2,1)} %get-tuple-element.106), channel_id=1, source_target_pairs={{0,24},{8,32},{16,40},{24,48},{32,56},{40,0},{48,8},{56,16},{1,25}... | collective-permute-start | bytes 1081352 | tf_op jit(solution)/shard_map/ppermute | solution.py:356
  122.6 1.3 collective-permute-start.11
  123.9 2.3 %collective-permute-start.12 = (bf16[88,2048]{1,0:T(8,128)(2,1)}, bf16[88,2048]{1,0:T(8,128)(2,1)}, u32[]{:S(2)}, u32[]{:S(2)}) collective-permute-start(bf16[88,2048]{1,0:T(8,128)(2,1)} %get-tuple-element.108), channel_id=1, source_target_pairs={{0,40},{8,48},{16,56},{24,0},{32,8},{40,16},{48,24},{56,32},{1,41}... | collective-permute-start | bytes 1081352 | tf_op jit(solution)/shard_map/ppermute | solution.py:356
  126.2 2.1 %collective-permute-start.13 = (bf16[88,2048]{1,0:T(8,128)(2,1)}, bf16[88,2048]{1,0:T(8,128)(2,1)}, u32[]{:S(2)}, u32[]{:S(2)}) collective-permute-start(bf16[88,2048]{1,0:T(8,128)(2,1)} %get-tuple-element.109), channel_id=1, source_target_pairs={{0,48},{8,56},{16,0},{24,8},{32,16},{40,24},{48,32},{56,40},{1,49}... | collective-permute-start | bytes 1081352 | tf_op jit(solution)/shard_map/ppermute | solution.py:356
  129.3 2.3 %gather_fusion = f32[512]{0:T(512)S(1)} fusion(f32[1024]{0:T(1024)S(1)} %reshape_reshape.6, s32[1024]{0:T(1024)S(1)} %pad_clamp_fusion.1), kind=kCustom, calls=%fused_computation | custom fusion | bytes 6144 | tf_op jit(solution)/shard_map/gather | solution.py:464
  131.6 2.3 %gather_fusion.1 = f32[512]{0:T(512)S(1)} fusion(f32[1024]{0:T(1024)S(1)} %reshape_reshape.6, s32[1024]{0:T(1024)S(1)} %pad_clamp_fusion), kind=kCustom, calls=%fused_computation.1 | custom fusion | bytes 6144 | tf_op jit(solution)/shard_map/gather | solution.py:464
  134.0 0.6 multiply_reduce_fusion
  135.3 1.0 reshape.450.scale_ref
  136.4 0.7 reshape.421.target_ref
  137.1 0.7 slice_reduce_fusion.4
  139.1 0.5 add_add_fusion.1
  139.6 30.4 %all-to-all-done.3 = bf16[32,32,2048]{2,1,0:T(8,128)(2,1)} async-done(((bf16[32,32,2048]{2,1,0:T(8,128)(2,1)}), bf16[32,32,2048]{2,1,0:T(8,128)(2,1)}, u32[]{:S(2)}, u32[]{:S(2)}) %all-to-all-start.3) | async-done | bytes 4194336 | tf_op jit(solution)/shard_map/all_to_all | solution.py:361
  170.0 6.5 %shard_map.108 = bf16[501,4096]{1,0:T(8,128)(2,1)} custom-call(s32[1,1024]{1,0:T(1,128)} %reshape.421.target_ref, f32[1024,1]{1,0:T(8,128)} %reshape.450.scale_ref, bf16[1024,2048]{1,0:T(8,128)(2,1)} %bitcast.39.rows_ref), custom_call_target="tpu_custom_call" | custom-call | flops 2101346304 | bytes 6246400 | tf_op jit(solution)/shard_map/pallas_call | solution.py:265
  176.5 5.0 %collective-permute-done.13 = bf16[88,2048]{1,0:T(8,128)(2,1)} collective-permute-done((bf16[88,2048]{1,0:T(8,128)(2,1)}, bf16[88,2048]{1,0:T(8,128)(2,1)}, u32[]{:S(2)}, u32[]{:S(2)}) %collective-permute-start.13) | collective-permute-done | bytes 360480 | tf_op jit(solution)/shard_map/ppermute | solution.py:356
  181.5 8.2 %conditional.1 = (bf16[501,4096]{1,0:T(8,128)(2,1)}) conditional(s32[]{:T(128)} %convert_element_type.47, (s32[256,4]{1,0:T(8,128)S(1)}, f32[256,4]{1,0:T(8,128)S(1)}, s32[1]{0:T(128)}, bf16[88,2048]{1,0:T(8,128)(2,1)S(1)}, bf16[88,2048]{1,0:T(8,128)(2,1)S(1)}, /*index=5*/bf16[88,2048]{1,0:T(8,128)(2,1)}, bf16[88,2048]{1,0:T(8,128)(2,1)S(1)}, ...), branch_computations={%region_9.10_spmd, %region_10.11_spmd} | conditional | flops 8497661952 | bytes 83836984 | solution.py:511
  181.8 0.7 copy.92.target_ref
  182.7 0.7 copy.93.scale_ref
  183.4 6.4 %branch_0_fun.1 = bf16[501,4096]{1,0:T(8,128)(2,1)} custom-call(s32[1]{0:T(128)} %get-tuple-element.45.z_ref, s32[8,128]{1,0:T(8,128)} %copy.92.target_ref, f32[8,128]{1,0:T(8,128)} %copy.93.scale_ref, bf16[88,2048]{1,0:T(8,128)(2,1)S(1)} %get-tuple-element.48.refs_0_, ...), custom_call_target="tpu_custom_call", output_to_operand_aliasing={{}: (11, {})} | custom-call | flops 2101346304 | bytes 4935680 | tf_op jit(solution)/shard_map/cond/branch_0_fun/pallas_call | solution.py:333
  (76 shorter events, 5.1 us)
Async XLA Ops:
  4.2 6.5 %copy-start.1 = (s32[512]{0:T(512)}, s32[512]{0:T(512)S(1)}, u32[]{:S(2)}) copy-start(s32[512]{0:T(512)S(1)} %convert_reduce_fusion.1) | copy-start | bytes 6148
  10.6 61.0 %all-to-all-start.1 = ((bf16[32,32,2048]{2,1,0:T(8,128)(2,1)}), bf16[32,32,2048]{2,1,0:T(8,128)(2,1)}, u32[]{:S(2)}, u32[]{:S(2)}) async-start(bf16[32,32,2048]{2,1,0:T(8,128)(2,1)} %bitcast.99), calls=%async_computation.1 | async-start | bytes 8388608 | tf_op jit(solution)/shard_map/all_to_all | solution.py:361
  19.3 19.1 %copy-start = (bf16[4,4096]{1,0:T(4,128)(2,1)S(1)}, bf16[4,4096]{1,0:T(4,128)(2,1)}, u32[]{:S(2)}) copy-start(bf16[4,4096]{1,0:T(4,128)(2,1)} %param.13) | copy-start | bytes 98308
  19.3 19.6 %copy-start.2 = (s32[512]{0:T(512)S(1)}, s32[512]{0:T(512)}, u32[]{:S(2)}) copy-start(s32[512]{0:T(512)} %copy-done.1) | copy-start | bytes 6148
  19.3 19.6 %copy-start.5 = (s32[4]{0:T(128)S(1)}, s32[4]{0:T(128)}, u32[]{:S(2)}) copy-start(s32[4]{0:T(128)} %param.14) | copy-start | bytes 52
  19.3 21.6 %copy-start.3 = (f32[4096]{0:T(1024)S(1)}, f32[4096]{0:T(1024)}, u32[]{:S(2)}) copy-start(f32[4096]{0:T(1024)} %param.16) | copy-start | bytes 49156
  19.3 21.6 %copy-start.4 = (f32[4096]{0:T(1024)S(1)}, f32[4096]{0:T(1024)}, u32[]{:S(2)}) copy-start(f32[4096]{0:T(1024)} %param.15) | copy-start | bytes 49156
  25.0 16.2 %collective-permute-start = (bf16[88,2048]{1,0:T(8,128)(2,1)}, bf16[88,2048]{1,0:T(8,128)(2,1)S(1)}, u32[]{:S(2)}, u32[]{:S(2)}) collective-permute-start(bf16[88,2048]{1,0:T(8,128)(2,1)} %get-tuple-element.89), channel_id=1, source_target_pairs={{0,8},{8,16},{16,24},{24,32},{32,40},{40,48},{48,56},{56,0},{1,9},... | collective-permute-start | bytes 1081352 | tf_op jit(solution)/shard_map/ppermute | solution.py:356
  26.7 22.1 %collective-permute-start.1 = (bf16[88,2048]{1,0:T(8,128)(2,1)}, bf16[88,2048]{1,0:T(8,128)(2,1)S(1)}, u32[]{:S(2)}, u32[]{:S(2)}) collective-permute-start(bf16[88,2048]{1,0:T(8,128)(2,1)} %get-tuple-element.90), channel_id=1, source_target_pairs={{0,16},{8,24},{16,32},{24,40},{32,48},{40,56},{48,0},{56,8},{1,17}... | collective-permute-start | bytes 1081352 | tf_op jit(solution)/shard_map/ppermute | solution.py:356
  29.7 65.4 %collective-permute-start.2 = (bf16[88,2048]{1,0:T(8,128)(2,1)}, bf16[88,2048]{1,0:T(8,128)(2,1)S(1)}, u32[]{:S(2)}, u32[]{:S(2)}) collective-permute-start(bf16[88,2048]{1,0:T(8,128)(2,1)} %get-tuple-element.97), channel_id=1, source_target_pairs={{0,24},{8,32},{16,40},{24,48},{32,56},{40,0},{48,8},{56,16},{1,25}... | collective-permute-start | bytes 1081352 | tf_op jit(solution)/shard_map/ppermute | solution.py:356
  33.5 63.9 %collective-permute-start.3 = (bf16[88,2048]{1,0:T(8,128)(2,1)}, bf16[88,2048]{1,0:T(8,128)(2,1)S(1)}, u32[]{:S(2)}, u32[]{:S(2)}) collective-permute-start(bf16[88,2048]{1,0:T(8,128)(2,1)} %get-tuple-element.98), channel_id=1, source_target_pairs={{0,32},{8,40},{16,48},{24,56},{32,0},{40,8},{48,16},{56,24},{1,33}... | collective-permute-start | bytes 1081352 | tf_op jit(solution)/shard_map/ppermute | solution.py:356
  33.9 67.0 %collective-permute-start.4 = (bf16[88,2048]{1,0:T(8,128)(2,1)}, bf16[88,2048]{1,0:T(8,128)(2,1)}, u32[]{:S(2)}, u32[]{:S(2)}) collective-permute-start(bf16[88,2048]{1,0:T(8,128)(2,1)} %get-tuple-element.99), channel_id=1, source_target_pairs={{0,40},{8,48},{16,56},{24,0},{32,8},{40,16},{48,24},{56,32},{1,41}... | collective-permute-start | bytes 1081352 | tf_op jit(solution)/shard_map/ppermute | solution.py:356
  41.2 37.2 %copy-start.8 = (bf16[88,2048]{1,0:T(8,128)(2,1)}, bf16[88,2048]{1,0:T(8,128)(2,1)S(1)}, u32[]{:S(2)}) copy-start(bf16[88,2048]{1,0:T(8,128)(2,1)S(1)} %collective-permute-done.refs_1_) | copy-start | bytes 1081348
  41.2 59.7 %collective-permute-start.5 = (bf16[88,2048]{1,0:T(8,128)(2,1)}, bf16[88,2048]{1,0:T(8,128)(2,1)}, u32[]{:S(2)}, u32[]{:S(2)}) collective-permute-start(bf16[88,2048]{1,0:T(8,128)(2,1)} %get-tuple-element.100), channel_id=1, source_target_pairs={{0,48},{8,56},{16,0},{24,8},{32,16},{40,24},{48,32},{56,40},{1,49}... | collective-permute-start | bytes 1081352 | tf_op jit(solution)/shard_map/ppermute | solution.py:356
  48.9 22.8 %copy-start.9 = (bf16[88,2048]{1,0:T(8,128)(2,1)}, bf16[88,2048]{1,0:T(8,128)(2,1)S(1)}, u32[]{:S(2)}) copy-start(bf16[88,2048]{1,0:T(8,128)(2,1)S(1)} %collective-permute-done.1.refs_2_) | copy-start | bytes 1081348
  48.9 52.1 %collective-permute-start.6 = (bf16[88,2048]{1,0:T(8,128)(2,1)}, bf16[88,2048]{1,0:T(8,128)(2,1)}, u32[]{:S(2)}, u32[]{:S(2)}) collective-permute-start(bf16[88,2048]{1,0:T(8,128)(2,1)} %get-tuple-element.101), channel_id=1, source_target_pairs={{0,56},{8,0},{16,8},{24,16},{32,24},{40,32},{48,40},{56,48},{1,57}... | collective-permute-start | bytes 1081352 | tf_op jit(solution)/shard_map/ppermute | solution.py:356
  81.1 28.4 %all-to-all-start.2 = ((f32[256,1,128]{2,1,0:T(1,128)}), f32[256,1,128]{2,1,0:T(1,128)S(1)}, u32[]{:S(2)}, u32[]{:S(2)}) async-start(f32[256,1,128]{2,1,0:T(1,128)} %copy.99), calls=%async_computation.2 | async-start | bytes 262144 | tf_op jit(solution)/shard_map/all_to_all | solution.py:454
  95.2 0.7 copy-start.10
  95.9 13.6 %collective-permute-start.7 = (bf16[88,2048]{1,0:T(8,128)(2,1)}, bf16[88,2048]{1,0:T(8,128)(2,1)S(1)}, u32[]{:S(2)}, u32[]{:S(2)}) collective-permute-start(bf16[88,2048]{1,0:T(8,128)(2,1)} %get-tuple-element.102), channel_id=1, source_target_pairs={{0,8},{8,16},{16,24},{24,32},{32,40},{40,48},{48,56},{56,0},{1,9},... | collective-permute-start | bytes 1081352 | tf_op jit(solution)/shard_map/ppermute | solution.py:356
  97.4 0.7 copy-start.11
  98.1 11.4 %collective-permute-start.8 = (bf16[88,2048]{1,0:T(8,128)(2,1)}, bf16[88,2048]{1,0:T(8,128)(2,1)S(1)}, u32[]{:S(2)}, u32[]{:S(2)}) collective-permute-start(bf16[88,2048]{1,0:T(8,128)(2,1)} %get-tuple-element.103), channel_id=1, source_target_pairs={{0,56},{8,0},{16,8},{24,16},{32,24},{40,32},{48,40},{56,48},{1,57}... | collective-permute-start | bytes 1081352 | tf_op jit(solution)/shard_map/ppermute | solution.py:356
  106.9 10.7 %copy-start.6 = (s32[512]{0:T(512)S(1)}, s32[512]{0:T(512)}, u32[]{:S(2)}) copy-start(s32[512]{0:T(512)} %param.17) | copy-start | bytes 6148
  106.9 10.7 %copy-start.7 = (s32[512]{0:T(512)S(1)}, s32[512]{0:T(512)}, u32[]{:S(2)}) copy-start(s32[512]{0:T(512)} %param.18) | copy-start | bytes 6148
  109.5 60.5 %all-to-all-start.3 = ((bf16[32,32,2048]{2,1,0:T(8,128)(2,1)}), bf16[32,32,2048]{2,1,0:T(8,128)(2,1)}, u32[]{:S(2)}, u32[]{:S(2)}) async-start(bf16[32,32,2048]{2,1,0:T(8,128)(2,1)} %shard_map.107), calls=%async_computation.3 | async-start | bytes 8388608 | tf_op jit(solution)/shard_map/all_to_all | solution.py:361
  117.7 58.8 %collective-permute-start.10 = (bf16[88,2048]{1,0:T(8,128)(2,1)}, bf16[88,2048]{1,0:T(8,128)(2,1)S(1)}, u32[]{:S(2)}, u32[]{:S(2)}) collective-permute-start(bf16[88,2048]{1,0:T(8,128)(2,1)} %get-tuple-element.106), channel_id=1, source_target_pairs={{0,24},{8,32},{16,40},{24,48},{32,56},{40,0},{48,8},{56,16},{1,25}... | collective-permute-start | bytes 1081352 | tf_op jit(solution)/shard_map/ppermute | solution.py:356
  122.6 53.9 %collective-permute-start.11 = (bf16[88,2048]{1,0:T(8,128)(2,1)}, bf16[88,2048]{1,0:T(8,128)(2,1)}, u32[]{:S(2)}, u32[]{:S(2)}) collective-permute-start(bf16[88,2048]{1,0:T(8,128)(2,1)} %get-tuple-element.107), channel_id=1, source_target_pairs={{0,32},{8,40},{16,48},{24,56},{32,0},{40,8},{48,16},{56,24},{1,33}... | collective-permute-start | bytes 1081352 | tf_op jit(solution)/shard_map/ppermute | solution.py:356
  123.9 52.6 %collective-permute-start.12 = (bf16[88,2048]{1,0:T(8,128)(2,1)}, bf16[88,2048]{1,0:T(8,128)(2,1)}, u32[]{:S(2)}, u32[]{:S(2)}) collective-permute-start(bf16[88,2048]{1,0:T(8,128)(2,1)} %get-tuple-element.108), channel_id=1, source_target_pairs={{0,40},{8,48},{16,56},{24,0},{32,8},{40,16},{48,24},{56,32},{1,41}... | collective-permute-start | bytes 1081352 | tf_op jit(solution)/shard_map/ppermute | solution.py:356
  126.2 55.3 %collective-permute-start.13 = (bf16[88,2048]{1,0:T(8,128)(2,1)}, bf16[88,2048]{1,0:T(8,128)(2,1)}, u32[]{:S(2)}, u32[]{:S(2)}) collective-permute-start(bf16[88,2048]{1,0:T(8,128)(2,1)} %get-tuple-element.109), channel_id=1, source_target_pairs={{0,48},{8,56},{16,0},{24,8},{32,16},{40,24},{48,32},{56,40},{1,49}... | collective-permute-start | bytes 1081352 | tf_op jit(solution)/shard_map/ppermute | solution.py:356
  128.3 53.2 %collective-permute-start.9 = (bf16[88,2048]{1,0:T(8,128)(2,1)}, bf16[88,2048]{1,0:T(8,128)(2,1)}, u32[]{:S(2)}, u32[]{:S(2)}) collective-permute-start(bf16[88,2048]{1,0:T(8,128)(2,1)} %get-tuple-element.105), channel_id=1, source_target_pairs={{0,16},{8,24},{16,32},{24,40},{32,48},{40,56},{48,0},{56,8},{1,17}... | collective-permute-start | bytes 1081352 | tf_op jit(solution)/shard_map/ppermute | solution.py:356

commit v9 on v8

--- a/solution.py
+++ b/solution.py
@@ -16,7 +16,7 @@
 COLUMNS = 32
 ROWS = 88
 BLOCK = 512
-VMEM = pltpu.CompilerParams(vmem_limit_bytes=62 << 20)
+VMEM = pltpu.CompilerParams(vmem_limit_bytes=48 << 20)
 NT = (((1,), (1,)), ((), ()))
 
 
@@ -285,7 +285,7 @@
     return x.astype(jnp.bfloat16).astype(jnp.float32)
 
 
-def ring_place_kernel(z_ref, target_ref, scale_ref, *refs):
+def ring_place_kernel(z_ref, table_ref, *refs):
     ins, (_, out_ref, hot_ref, held_ref, scaled_ref) = refs[:RING], refs[RING:]
 
     @pl.when(pl.program_id(0) == 0)
@@ -296,8 +296,8 @@
             code = ins[k][ROWS - 8 : ROWS, 0:128].astype(jnp.float32)[7:8, :].astype(jnp.int32)
             plane = (z_ref[0] - k) & 7
             listed = (rows_of((128, 128)) == code - 1).astype(jnp.bfloat16)
-            target = target_ref[pl.ds(plane, 1), :] + 1
-            scale = scale_ref[pl.ds(plane, 1), :]
+            target = table_ref[pl.ds(plane, 1), :].astype(jnp.int32) + 1
+            scale = table_ref[pl.ds(plane + RING, 1), :]
             high = rounded(scale)
             middle = rounded(scale - high)
             low = scale - high - middle
@@ -326,7 +326,7 @@
     ).astype(jnp.bfloat16)
 
 
-def ring_placed(z, target, scale, parts, half_done):
+def ring_placed(z, tables, parts, half_done):
     shard_rows, out_width = half_done.shape
     width = parts[0].shape[1]
     skip = (out_width - width) // BLOCK
@@ -335,7 +335,7 @@
         out_shape=jax.ShapeDtypeStruct(half_done.shape, jnp.bfloat16),
         grid=(width // BLOCK,),
         in_specs=[pl.BlockSpec(memory_space=pltpu.SMEM)]
-        + [whole((RING, 128))] * 2
+        + [whole((2 * RING, 128))]
         + [pl.BlockSpec((ROWS, BLOCK), lambda j: (0, j))] * RING
         + [pl.BlockSpec(memory_space=pl.ANY)],
         out_specs=pl.BlockSpec((shard_rows, BLOCK), lambda j: (0, skip + j)),
@@ -344,10 +344,10 @@
             pltpu.VMEM((128 * RING, 128), jnp.float32),
             pltpu.VMEM((128 * RING, BLOCK), jnp.bfloat16),
         ],
-        input_output_aliases={3 + RING: 0},
+        input_output_aliases={2 + RING: 0},
         compiler_params=VMEM,
         cost_estimate=cost(shard_rows * 1024 * width, (shard_rows + 704) * width),
-    )(z, target, scale, *parts, half_done)
+    )(z, tables, *parts, half_done)
 
 
 def ring_shifted(parts):
@@ -427,7 +427,7 @@
     second_slot = jnp.where(live, (column << 5) + (plane << 2) + rank, -1)
     second = packed_rows(second_slot[None, :], rows, slots, half, half)
     second = in_plane(second.reshape(COLUMNS, CAP * RING, half))
-    first[1], first[2], second = lax.optimization_barrier((first[1], first[2], second))
+    first[1], first[7], second = lax.optimization_barrier((first[1], first[7], second))
     second, over_there = ring_repacked(z, second)
     second = ring_shifted(second)
 
@@ -450,7 +450,7 @@
         axis=1,
     )
     lane = jnp.arange(128, dtype=jnp.int32)
-    message = jnp.where(lane[None, :] == 13, over_there[0, 0], ready)
+    message = jnp.where(lane[None, :] == 13, over_there[0:1, :], ready)
     heard = lax.all_to_all(message, GRP_DEV, split_axis=0, concat_axis=0, tiled=True)
     heard = by_column(heard)
 
@@ -492,8 +492,10 @@
     def by_plane(table):
         return table.reshape(COLUMNS, RING, CAP).swapaxes(0, 1).reshape(RING, -1)
 
+    tail_table = jnp.concatenate([by_plane(target).astype(jnp.float32), by_plane(scale)])
+
     def by_ring():
-        return ring_placed(z, by_plane(target), by_plane(scale), second, half_done)
+        return ring_placed(z, tail_table, second, half_done)
 
     def direct():
         sent = packed_rows(

time: 191 us -> 186 us (0.974)
  starting transfers between devices: 70.5 us -> 58 us
  waiting for transfers between devices: 57.3 us -> 69.7 us
  Pallas kernels: 37 us -> 34.8 us
    ppermute x14, starting transfers between devices: 39.8 us -> 27.8 us  [ring_shifted(): lax.ppermute(parts[k], 'dev_0', [(i, (i + k) % RING) for i in range(RING)])]
    ppermute x14, waiting for transfers between devices: 12.9 us -> 24.1 us  [ring_shifted(): lax.ppermute(parts[k], 'dev_0', [(i, (i + k) % RING) for i in range(RING)])]
    unnamed x28 -> x32, local copies, waits for them, and re-layouts: 1.79 us -> 5.49 us
  transfers between devices with their start and end apart: 17 -> 17, of which waited for: 5 -> 6; matrix products, arithmetic and copies ran while one was open for 8% -> 7% of each run, Pallas kernels for 13% -> 13%
where the time goes in v9:
time: 186 us
  waiting for transfers between devices  69.7 us (37%)
  starting transfers between devices  58 us (31%)
  Pallas kernels  34.8 us (19%)
  local copies, waits for them, and re-layouts  13.9 us (7%)
  other arithmetic  6.89 us (4%)
  between operations  2.31 us (1%)
    all_to_all x2, waiting for transfers between devices, in_plane(): return lax.all_to_all(parts, PLANE, split_axis=0, concat_axis=0, tiled=True)  45.6 us
    ppermute x14, starting transfers between devices, ring_shifted(): lax.ppermute(parts[k], 'dev_0', [(i, (i + k) % RING) for i in range(RING)])  27.8 us
    ppermute x14, waiting for transfers between devices, ring_shifted(): lax.ppermute(parts[k], 'dev_0', [(i, (i + k) % RING) for i in range(RING)])  24.1 us
    all_to_all x2, starting transfers between devices, in_plane(): return lax.all_to_all(parts, PLANE, split_axis=0, concat_axis=0, tiled=True)  16.3 us
    all_to_all x1, starting transfers between devices, local(): lax.all_to_all(message, GRP_DEV, split_axis=0, concat_axis=0, tiled=True)  13.9 us
    pallas_call x1, Pallas kernels, ring_placed(): pl.pallas_call(ring_place_kernel, out_shape=jax.ShapeDtypeStruct(half_don...  6.5 us
    pallas_call x1, Pallas kernels, placed_rows(): pl.pallas_call(place_kernel, out_shape=jax.ShapeDtypeStruct((shard_rows,...  6.41 us
    pallas_call x1, Pallas kernels, ring_repacked(): pl.pallas_call(ring_repack_kernel, out_shape=[jax.ShapeDtypeStruct((ROWS,...  6.33 us
  transfers between devices with their start and end apart: 17, of which 6 were waited for; matrix products, arithmetic and copies ran while one was open for 7% of the time, Pallas kernels for 13%

profile of v9, /device:TPU:1, one launch (start us, length us, event | category | flops | bytes accessed | tf_op | source)
XLA Modules:
  0.0 185.6 jit_solution(1878252137907864453)
XLA Ops:
  0.6 0.7 fusion.17
  1.4 0.8 add_select_fusion.4
  2.4 0.9 select_reduce_fusion.1
  3.3 0.3 convert_reduce_fusion.1
  3.6 4.7 %shard_map.105 = bf16[1024,2048]{1,0:T(8,128)(2,1)S(1)} custom-call(s32[1,512]{1,0:T(1,128)S(1)} %get-tuple-element.192.slot_ref, bf16[512,4096]{1,0:T(8,128)(2,1)} %bitcast.106), custom_call_target="tpu_custom_call" | custom-call | flops 2147483648 | bytes 6291456 | tf_op jit(solution)/shard_map/pallas_call | solution.py:48
  8.3 2.0 %copy-done = bf16[1024,2048]{1,0:T(8,128)(2,1)} copy-done((bf16[1024,2048]{1,0:T(8,128)(2,1)}, bf16[1024,2048]{1,0:T(8,128)(2,1)S(1)}, u32[]{:S(2)}) %copy-start) | copy-done | bytes 4194328
  10.3 8.6 %all-to-all-start.1 = ((bf16[32,32,2048]{2,1,0:T(8,128)(2,1)}), bf16[32,32,2048]{2,1,0:T(8,128)(2,1)}, u32[]{:S(2)}, u32[]{:S(2)}) async-start(bf16[32,32,2048]{2,1,0:T(8,128)(2,1)} %bitcast.95), calls=%async_computation.1 | async-start | bytes 8388608 | tf_op jit(solution)/shard_map/all_to_all | solution.py:361
  19.0 5.4 %shard_map.104 = (bf16[88,2048]{1,0:T(8,128)(2,1)S(1)}, bf16[88,2048]{1,0:T(8,128)(2,1)S(1)}, bf16[88,2048]{1,0:T(8,128)(2,1)}, bf16[88,2048]{1,0:T(8,128)(2,1)}...) custom-call(s32[1,512]{1,0:T(1,128)S(1)} %get-tuple-element.193.ring, ...), custom_call_target="tpu_custom_call" | custom-call | flops 1476395008 | bytes 4980736 | tf_op jit(solution)/shard_map/pallas_call | solution.py:100
  24.4 1.6 collective-permute-start
  26.0 4.0 %collective-permute-start.1 = (bf16[88,2048]{1,0:T(8,128)(2,1)S(1)}, bf16[88,2048]{1,0:T(8,128)(2,1)S(1)}, u32[]{:S(2)}, u32[]{:S(2)}) collective-permute-start(bf16[88,2048]{1,0:T(8,128)(2,1)S(1)} %get-tuple-element.87), channel_id=1, source_target_pairs={{0,56},{8,0},{16,8},{24,16},{32,24},{40,32},{48,40},{56,48},{1,57}... | collective-permute-start | bytes 1081352 | tf_op jit(solution)/shard_map/ppermute | solution.py:356
  30.1 3.5 %collective-permute-start.3 = (bf16[88,2048]{1,0:T(8,128)(2,1)}, bf16[88,2048]{1,0:T(8,128)(2,1)}, u32[]{:S(2)}, u32[]{:S(2)}) collective-permute-start(bf16[88,2048]{1,0:T(8,128)(2,1)} %get-tuple-element.94), channel_id=1, source_target_pairs={{0,24},{8,32},{16,40},{24,48},{32,56},{40,0},{48,8},{56,16},{1,25}... | collective-permute-start | bytes 1081352 | tf_op jit(solution)/shard_map/ppermute | solution.py:356
  33.5 0.9 collective-permute-start.4
  34.6 0.3 select_reduce_fusion
  34.9 0.7 and_reduce_fusion
  37.2 1.4 collective-permute-done.refs_1_
  38.6 2.7 %collective-permute-start.5 = (bf16[88,2048]{1,0:T(8,128)(2,1)S(1)}, bf16[88,2048]{1,0:T(8,128)(2,1)}, u32[]{:S(2)}, u32[]{:S(2)}) collective-permute-start(bf16[88,2048]{1,0:T(8,128)(2,1)S(1)} %get-tuple-element.96), channel_id=1, source_target_pairs={{0,40},{8,48},{16,56},{24,0},{32,8},{40,16},{48,24},{56,32},{1,41}... | collective-permute-start | bytes 1081352 | tf_op jit(solution)/shard_map/ppermute | solution.py:356
  41.3 15.8 %collective-permute-done.1.refs_7_ = bf16[88,2048]{1,0:T(8,128)(2,1)S(1)} collective-permute-done((bf16[88,2048]{1,0:T(8,128)(2,1)S(1)}, bf16[88,2048]{1,0:T(8,128)(2,1)S(1)}, u32[]{:S(2)}, u32[]{:S(2)}) %collective-permute-start.1) | collective-permute-done | bytes 360480 | tf_op jit(solution)/shard_map/ppermute | solution.py:356
  57.1 14.3 %all-to-all-done.1.rows_ref = bf16[32,32,2048]{2,1,0:T(8,128)(2,1)} async-done(((bf16[32,32,2048]{2,1,0:T(8,128)(2,1)}), bf16[32,32,2048]{2,1,0:T(8,128)(2,1)}, u32[]{:S(2)}, u32[]{:S(2)}) %all-to-all-start.1) | async-done | bytes 4194336 | tf_op jit(solution)/shard_map/all_to_all | solution.py:361
  71.4 6.3 %shard_map.106 = (bf16[88,2048]{1,0:T(8,128)(2,1)}, bf16[88,2048]{1,0:T(8,128)(2,1)S(1)}, bf16[88,2048]{1,0:T(8,128)(2,1)S(1)}, bf16[88,2048]{1,0:T(8,128)(2,1)S...) custom-call(s32[1]{0:T(128)} %bitcast.6.z_ref, ...), custom_call_target="tpu_custom_call" | custom-call | flops 2952790016 | bytes 7077888 | tf_op jit(solution)/shard_map/pallas_call | solution.py:186
  77.7 0.7 copy-done.1
  78.5 0.7 copy-done.2
  79.4 0.7 copy.93
  80.1 13.9 %all-to-all-start.2 = ((f32[256,1,128]{2,1,0:T(1,128)}), f32[256,1,128]{2,1,0:T(1,128)S(1)}, u32[]{:S(2)}, u32[]{:S(2)}) async-start(f32[256,1,128]{2,1,0:T(1,128)} %copy.93), calls=%async_computation.2 | async-start | bytes 262144 | tf_op jit(solution)/shard_map/all_to_all | solution.py:454
  94.0 1.8 collective-permute-start.7
  95.8 2.9 %collective-permute-start.8 = (bf16[88,2048]{1,0:T(8,128)(2,1)}, bf16[88,2048]{1,0:T(8,128)(2,1)}, u32[]{:S(2)}, u32[]{:S(2)}) collective-permute-start(bf16[88,2048]{1,0:T(8,128)(2,1)} %copy-done.1), channel_id=1, source_target_pairs={{0,56},{8,0},{16,8},{24,16},{32,24},{40,32},{48,40},{56,48},{1,57}... | collective-permute-start | bytes 1081352 | tf_op jit(solution)/shard_map/ppermute | solution.py:356
  98.7 1.0 copy-done.4
  99.7 5.5 %shard_map.107 = bf16[32,32,2048]{2,1,0:T(8,128)(2,1)} custom-call(s32[1]{0:T(128)} %bitcast.6.z_ref, bf16[88,2048]{1,0:T(8,128)(2,1)S(1)} %copy-done.4, bf16[88,2048]{1,0:T(8,128)(2,1)S(1)} %collective-permute-done.refs_1_, bf16[88,2048]{1,0:T(8,128)(2,1)} %collective-permute-done.2.refs_2_, bf16[88,2048]{1,0:T(8,128)(2,1)} %collective-permute-done.3.refs_3_, ...), custom_call_target="tpu_custom_call" | custom-call | flops 4294967296 | bytes 7077888 | tf_op jit(solution)/shard_map/pallas_call | solution.py:234
  105.2 3.5 %collective-permute-done.7 = bf16[88,2048]{1,0:T(8,128)(2,1)S(1)} collective-permute-done((bf16[88,2048]{1,0:T(8,128)(2,1)}, bf16[88,2048]{1,0:T(8,128)(2,1)S(1)}, u32[]{:S(2)}, u32[]{:S(2)}) %collective-permute-start.7) | collective-permute-done | bytes 360480 | tf_op jit(solution)/shard_map/ppermute | solution.py:356
  108.7 0.8 copy-done.6
  109.4 7.6 %all-to-all-start.3 = ((bf16[32,32,2048]{2,1,0:T(8,128)(2,1)}), bf16[32,32,2048]{2,1,0:T(8,128)(2,1)}, u32[]{:S(2)}, u32[]{:S(2)}) async-start(bf16[32,32,2048]{2,1,0:T(8,128)(2,1)} %shard_map.107), calls=%async_computation.3 | async-start | bytes 8388608 | tf_op jit(solution)/shard_map/all_to_all | solution.py:361
  117.2 3.2 %collective-permute-start.10 = (bf16[88,2048]{1,0:T(8,128)(2,1)S(1)}, bf16[88,2048]{1,0:T(8,128)(2,1)}, u32[]{:S(2)}, u32[]{:S(2)}) collective-permute-start(bf16[88,2048]{1,0:T(8,128)(2,1)S(1)} %get-tuple-element.103), channel_id=1, source_target_pairs={{0,24},{8,32},{16,40},{24,48},{32,56},{40,0},{48,8},{56,16},{1,25}... | collective-permute-start | bytes 1081352 | tf_op jit(solution)/shard_map/ppermute | solution.py:356
  120.4 0.9 collective-permute-start.11
  121.3 3.9 %collective-permute-start.12 = (bf16[88,2048]{1,0:T(8,128)(2,1)S(1)}, bf16[88,2048]{1,0:T(8,128)(2,1)}, u32[]{:S(2)}, u32[]{:S(2)}) collective-permute-start(bf16[88,2048]{1,0:T(8,128)(2,1)S(1)} %get-tuple-element.105), channel_id=1, source_target_pairs={{0,40},{8,48},{16,56},{24,0},{32,8},{40,16},{48,24},{56,32},{1,41}... | collective-permute-start | bytes 1081352 | tf_op jit(solution)/shard_map/ppermute | solution.py:356
  125.3 0.8 collective-permute-start.13
  126.1 1.6 collective-permute-start.9
  127.9 2.3 %gather_fusion = f32[512]{0:T(512)S(1)} fusion(f32[1024]{0:T(1024)S(1)} %reshape_reshape.6, s32[1024]{0:T(1024)S(1)} %pad_clamp_fusion.1), kind=kCustom, calls=%fused_computation | custom fusion | bytes 6144 | tf_op jit(solution)/shard_map/gather | solution.py:464
  130.2 2.3 %gather_fusion.1 = f32[512]{0:T(512)S(1)} fusion(f32[1024]{0:T(1024)S(1)} %reshape_reshape.6, s32[1024]{0:T(1024)S(1)} %pad_clamp_fusion), kind=kCustom, calls=%fused_computation.1 | custom fusion | bytes 6144 | tf_op jit(solution)/shard_map/gather | solution.py:464
  132.5 0.6 multiply_reduce_fusion
  133.2 0.3 copy.98
  134.1 0.4 slice_reduce_fusion.2
  134.7 0.5 add_add_fusion.1
  135.6 0.7 slice_reduce_fusion.4
  136.9 0.3 copy.96
  137.9 31.3 %all-to-all-done.3 = bf16[32,32,2048]{2,1,0:T(8,128)(2,1)} async-done(((bf16[32,32,2048]{2,1,0:T(8,128)(2,1)}), bf16[32,32,2048]{2,1,0:T(8,128)(2,1)}, u32[]{:S(2)}, u32[]{:S(2)}) %all-to-all-start.3) | async-done | bytes 4194336 | tf_op jit(solution)/shard_map/all_to_all | solution.py:361
  169.3 6.4 %shard_map.108 = bf16[501,4096]{1,0:T(8,128)(2,1)} custom-call(s32[1,1024]{1,0:T(1,128)S(1)} %reshape.445.target_ref, f32[1024,1]{1,0:T(8,128)S(1)} %reshape.474.scale_ref, bf16[1024,2048]{1,0:T(8,128)(2,1)} %bitcast.37.rows_ref), custom_call_target="tpu_custom_call" | custom-call | flops 2101346304 | bytes 6246400 | tf_op jit(solution)/shard_map/pallas_call | solution.py:265
  175.7 3.4 %collective-permute-done.13 = bf16[88,2048]{1,0:T(8,128)(2,1)} collective-permute-done((bf16[88,2048]{1,0:T(8,128)(2,1)S(1)}, bf16[88,2048]{1,0:T(8,128)(2,1)}, u32[]{:S(2)}, u32[]{:S(2)}) %collective-permute-start.13) | collective-permute-done | bytes 360480 | tf_op jit(solution)/shard_map/ppermute | solution.py:356
  179.1 6.5 %conditional.1 = (bf16[501,4096]{1,0:T(8,128)(2,1)}) conditional(s32[]{:T(128)} %convert_element_type.59, (s32[1]{0:T(128)}, f32[16,128]{1,0:T(8,128)S(1)}, bf16[88,2048]{1,0:T(8,128)(2,1)S(1)}, bf16[88,2048]{1,0:T(8,128)(2,1)S(1)}, bf16[88,2048]{1,0:T(8,128)(2,1)}, /*index=5*/bf16[88,2048]{1,0:T(8,128)(2,1)}, bf16[88,2048]{1,0:T(8,128)(2,1)}, ...), branch_computations={%region_9.10_spmd, %region_10.11_spmd} | conditional | flops 8497661952 | bytes 83836984 | solution.py:513
  179.1 6.5 %branch_0_fun.1 = bf16[501,4096]{1,0:T(8,128)(2,1)} custom-call(s32[1]{0:T(128)} %get-tuple-element.43.z_ref, f32[16,128]{1,0:T(8,128)S(1)} %get-tuple-element.44.table_ref, bf16[88,2048]{1,0:T(8,128)(2,1)S(1)} %get-tuple-element.45.refs_0_, bf16[88,2048]{1,0:T(8,128)(2,1)S(1)} %get-tuple-element.46.refs_1_, ...), custom_call_target="tpu_custom_call", output_to_operand_aliasing={{}: (10, {})} | custom-call | flops 2101346304 | bytes 4935680 | tf_op jit(solution)/shard_map/cond/branch_0_fun/pallas_call | solution.py:333
  (81 shorter events, 3.9 us)
Async XLA Ops:
  8.3 2.0 %copy-start = (bf16[1024,2048]{1,0:T(8,128)(2,1)}, bf16[1024,2048]{1,0:T(8,128)(2,1)S(1)}, u32[]{:S(2)}) copy-start(bf16[1024,2048]{1,0:T(8,128)(2,1)S(1)} %shard_map.105) | copy-start | bytes 12582916
  10.3 61.1 %all-to-all-start.1 = ((bf16[32,32,2048]{2,1,0:T(8,128)(2,1)}), bf16[32,32,2048]{2,1,0:T(8,128)(2,1)}, u32[]{:S(2)}, u32[]{:S(2)}) async-start(bf16[32,32,2048]{2,1,0:T(8,128)(2,1)} %bitcast.95), calls=%async_computation.1 | async-start | bytes 8388608 | tf_op jit(solution)/shard_map/all_to_all | solution.py:361
  18.9 15.5 %copy-start.8 = (bf16[4,4096]{1,0:T(4,128)(2,1)S(1)}, bf16[4,4096]{1,0:T(4,128)(2,1)}, u32[]{:S(2)}) copy-start(bf16[4,4096]{1,0:T(4,128)(2,1)} %param.13) | copy-start | bytes 98308
  18.9 16.0 %copy-start.11 = (s32[4]{0:T(128)S(1)}, s32[4]{0:T(128)}, u32[]{:S(2)}) copy-start(s32[4]{0:T(128)} %param.14) | copy-start | bytes 52
  18.9 18.0 %copy-start.9 = (f32[4096]{0:T(1024)S(1)}, f32[4096]{0:T(1024)}, u32[]{:S(2)}) copy-start(f32[4096]{0:T(1024)} %param.16) | copy-start | bytes 49156
  18.9 18.0 %copy-start.10 = (f32[4096]{0:T(1024)S(1)}, f32[4096]{0:T(1024)}, u32[]{:S(2)}) copy-start(f32[4096]{0:T(1024)} %param.15) | copy-start | bytes 49156
  24.4 47.0 %copy-start.3 = (bf16[88,2048]{1,0:T(8,128)(2,1)}, bf16[88,2048]{1,0:T(8,128)(2,1)S(1)}, u32[]{:S(2)}) copy-start(bf16[88,2048]{1,0:T(8,128)(2,1)S(1)} %get-tuple-element.91.refs_0_) | copy-start | bytes 1081348
  24.4 14.2 %collective-permute-start = (bf16[88,2048]{1,0:T(8,128)(2,1)S(1)}, bf16[88,2048]{1,0:T(8,128)(2,1)S(1)}, u32[]{:S(2)}, u32[]{:S(2)}) collective-permute-start(bf16[88,2048]{1,0:T(8,128)(2,1)S(1)} %get-tuple-element.86), channel_id=1, source_target_pairs={{0,8},{8,16},{16,24},{24,32},{32,40},{40,48},{48,56},{56,0},{1,9},... | collective-permute-start | bytes 1081352 | tf_op jit(solution)/shard_map/ppermute | solution.py:356
  26.0 31.1 %collective-permute-start.1 = (bf16[88,2048]{1,0:T(8,128)(2,1)S(1)}, bf16[88,2048]{1,0:T(8,128)(2,1)S(1)}, u32[]{:S(2)}, u32[]{:S(2)}) collective-permute-start(bf16[88,2048]{1,0:T(8,128)(2,1)S(1)} %get-tuple-element.87), channel_id=1, source_target_pairs={{0,56},{8,0},{16,8},{24,16},{32,24},{40,32},{48,40},{56,48},{1,57}... | collective-permute-start | bytes 1081352 | tf_op jit(solution)/shard_map/ppermute | solution.py:356
  30.0 64.0 %collective-permute-start.2 = (bf16[88,2048]{1,0:T(8,128)(2,1)}, bf16[88,2048]{1,0:T(8,128)(2,1)}, u32[]{:S(2)}, u32[]{:S(2)}) collective-permute-start(bf16[88,2048]{1,0:T(8,128)(2,1)} %get-tuple-element.93), channel_id=1, source_target_pairs={{0,16},{8,24},{16,32},{24,40},{32,48},{40,56},{48,0},{56,8},{1,17}... | collective-permute-start | bytes 1081352 | tf_op jit(solution)/shard_map/ppermute | solution.py:356
  30.1 65.7 %collective-permute-start.3 = (bf16[88,2048]{1,0:T(8,128)(2,1)}, bf16[88,2048]{1,0:T(8,128)(2,1)}, u32[]{:S(2)}, u32[]{:S(2)}) collective-permute-start(bf16[88,2048]{1,0:T(8,128)(2,1)} %get-tuple-element.94), channel_id=1, source_target_pairs={{0,24},{8,32},{16,40},{24,48},{32,56},{40,0},{48,8},{56,16},{1,25}... | collective-permute-start | bytes 1081352 | tf_op jit(solution)/shard_map/ppermute | solution.py:356
  33.5 65.2 %collective-permute-start.4 = (bf16[88,2048]{1,0:T(8,128)(2,1)}, bf16[88,2048]{1,0:T(8,128)(2,1)}, u32[]{:S(2)}, u32[]{:S(2)}) collective-permute-start(bf16[88,2048]{1,0:T(8,128)(2,1)} %get-tuple-element.95), channel_id=1, source_target_pairs={{0,32},{8,40},{16,48},{24,56},{32,0},{40,8},{48,16},{56,24},{1,33}... | collective-permute-start | bytes 1081352 | tf_op jit(solution)/shard_map/ppermute | solution.py:356
  38.6 60.1 %collective-permute-start.5 = (bf16[88,2048]{1,0:T(8,128)(2,1)S(1)}, bf16[88,2048]{1,0:T(8,128)(2,1)}, u32[]{:S(2)}, u32[]{:S(2)}) collective-permute-start(bf16[88,2048]{1,0:T(8,128)(2,1)S(1)} %get-tuple-element.96), channel_id=1, source_target_pairs={{0,40},{8,48},{16,56},{24,0},{32,8},{40,16},{48,24},{56,32},{1,41}... | collective-permute-start | bytes 1081352 | tf_op jit(solution)/shard_map/ppermute | solution.py:356
  57.1 41.6 %collective-permute-start.6 = (bf16[88,2048]{1,0:T(8,128)(2,1)S(1)}, bf16[88,2048]{1,0:T(8,128)(2,1)}, u32[]{:S(2)}, u32[]{:S(2)}) collective-permute-start(bf16[88,2048]{1,0:T(8,128)(2,1)S(1)} %get-tuple-element.97), channel_id=1, source_target_pairs={{0,48},{8,56},{16,0},{24,8},{32,16},{40,24},{48,32},{56,40},{1,49}... | collective-permute-start | bytes 1081352 | tf_op jit(solution)/shard_map/ppermute | solution.py:356
  77.7 0.7 copy-start.1
  78.5 0.7 copy-start.2
  80.1 29.3 %all-to-all-start.2 = ((f32[256,1,128]{2,1,0:T(1,128)}), f32[256,1,128]{2,1,0:T(1,128)S(1)}, u32[]{:S(2)}, u32[]{:S(2)}) async-start(f32[256,1,128]{2,1,0:T(1,128)} %copy.93), calls=%async_computation.2 | async-start | bytes 262144 | tf_op jit(solution)/shard_map/all_to_all | solution.py:454
  94.0 14.6 %collective-permute-start.7 = (bf16[88,2048]{1,0:T(8,128)(2,1)}, bf16[88,2048]{1,0:T(8,128)(2,1)S(1)}, u32[]{:S(2)}, u32[]{:S(2)}) collective-permute-start(bf16[88,2048]{1,0:T(8,128)(2,1)} %copy-done.2), channel_id=1, source_target_pairs={{0,8},{8,16},{16,24},{24,32},{32,40},{40,48},{48,56},{56,0},{1,9},... | collective-permute-start | bytes 1081352 | tf_op jit(solution)/shard_map/ppermute | solution.py:356
  95.8 13.6 %collective-permute-start.8 = (bf16[88,2048]{1,0:T(8,128)(2,1)}, bf16[88,2048]{1,0:T(8,128)(2,1)}, u32[]{:S(2)}, u32[]{:S(2)}) collective-permute-start(bf16[88,2048]{1,0:T(8,128)(2,1)} %copy-done.1), channel_id=1, source_target_pairs={{0,56},{8,0},{16,8},{24,16},{32,24},{40,32},{48,40},{56,48},{1,57}... | collective-permute-start | bytes 1081352 | tf_op jit(solution)/shard_map/ppermute | solution.py:356
  98.7 1.0 copy-start.4
  105.2 12.0 %copy-start.12 = (s32[512]{0:T(512)S(1)}, s32[512]{0:T(512)}, u32[]{:S(2)}) copy-start(s32[512]{0:T(512)} %param.17) | copy-start | bytes 6148
  105.2 12.0 %copy-start.13 = (s32[512]{0:T(512)S(1)}, s32[512]{0:T(512)}, u32[]{:S(2)}) copy-start(s32[512]{0:T(512)} %param.18) | copy-start | bytes 6148
  108.7 0.8 copy-start.6
  109.4 59.9 %all-to-all-start.3 = ((bf16[32,32,2048]{2,1,0:T(8,128)(2,1)}), bf16[32,32,2048]{2,1,0:T(8,128)(2,1)}, u32[]{:S(2)}, u32[]{:S(2)}) async-start(bf16[32,32,2048]{2,1,0:T(8,128)(2,1)} %shard_map.107), calls=%async_computation.3 | async-start | bytes 8388608 | tf_op jit(solution)/shard_map/all_to_all | solution.py:361
  117.2 58.5 %collective-permute-start.10 = (bf16[88,2048]{1,0:T(8,128)(2,1)S(1)}, bf16[88,2048]{1,0:T(8,128)(2,1)}, u32[]{:S(2)}, u32[]{:S(2)}) collective-permute-start(bf16[88,2048]{1,0:T(8,128)(2,1)S(1)} %get-tuple-element.103), channel_id=1, source_target_pairs={{0,24},{8,32},{16,40},{24,48},{32,56},{40,0},{48,8},{56,16},{1,25}... | collective-permute-start | bytes 1081352 | tf_op jit(solution)/shard_map/ppermute | solution.py:356
  120.4 55.3 %collective-permute-start.11 = (bf16[88,2048]{1,0:T(8,128)(2,1)S(1)}, bf16[88,2048]{1,0:T(8,128)(2,1)}, u32[]{:S(2)}, u32[]{:S(2)}) collective-permute-start(bf16[88,2048]{1,0:T(8,128)(2,1)S(1)} %get-tuple-element.104), channel_id=1, source_target_pairs={{0,32},{8,40},{16,48},{24,56},{32,0},{40,8},{48,16},{56,24},{1,33}... | collective-permute-start | bytes 1081352 | tf_op jit(solution)/shard_map/ppermute | solution.py:356
  121.3 54.4 %collective-permute-start.12 = (bf16[88,2048]{1,0:T(8,128)(2,1)S(1)}, bf16[88,2048]{1,0:T(8,128)(2,1)}, u32[]{:S(2)}, u32[]{:S(2)}) collective-permute-start(bf16[88,2048]{1,0:T(8,128)(2,1)S(1)} %get-tuple-element.105), channel_id=1, source_target_pairs={{0,40},{8,48},{16,56},{24,0},{32,8},{40,16},{48,24},{56,32},{1,41}... | collective-permute-start | bytes 1081352 | tf_op jit(solution)/shard_map/ppermute | solution.py:356
  125.3 53.8 %collective-permute-start.13 = (bf16[88,2048]{1,0:T(8,128)(2,1)S(1)}, bf16[88,2048]{1,0:T(8,128)(2,1)}, u32[]{:S(2)}, u32[]{:S(2)}) collective-permute-start(bf16[88,2048]{1,0:T(8,128)(2,1)S(1)} %get-tuple-element.106), channel_id=1, source_target_pairs={{0,48},{8,56},{16,0},{24,8},{32,16},{40,24},{48,32},{56,40},{1,49}... | collective-permute-start | bytes 1081352 | tf_op jit(solution)/shard_map/ppermute | solution.py:356
  126.1 53.0 %collective-permute-start.9 = (bf16[88,2048]{1,0:T(8,128)(2,1)S(1)}, bf16[88,2048]{1,0:T(8,128)(2,1)}, u32[]{:S(2)}, u32[]{:S(2)}) collective-permute-start(bf16[88,2048]{1,0:T(8,128)(2,1)S(1)} %get-tuple-element.102), channel_id=1, source_target_pairs={{0,16},{8,24},{16,32},{24,40},{32,48},{40,56},{48,0},{56,8},{1,17}... | collective-permute-start | bytes 1081352 | tf_op jit(solution)/shard_map/ppermute | solution.py:356
  169.3 9.8 %copy-start.5 = (bf16[88,2048]{1,0:T(8,128)(2,1)S(1)}, bf16[88,2048]{1,0:T(8,128)(2,1)}, u32[]{:S(2)}) copy-start(bf16[88,2048]{1,0:T(8,128)(2,1)} %get-tuple-element.90) | copy-start | bytes 1081348
  169.3 9.8 %copy-start.7 = (bf16[88,2048]{1,0:T(8,128)(2,1)S(1)}, bf16[88,2048]{1,0:T(8,128)(2,1)}, u32[]{:S(2)}) copy-start(bf16[88,2048]{1,0:T(8,128)(2,1)} %copy-done.6) | copy-start | bytes 1081348

commit v10 on v9

--- a/solution.py
+++ b/solution.py
@@ -15,7 +15,7 @@
 RING = 8
 COLUMNS = 32
 ROWS = 88
-BLOCK = 512
+BLOCK = 1024
 VMEM = pltpu.CompilerParams(vmem_limit_bytes=48 << 20)
 NT = (((1,), (1,)), ((), ()))
 

time: 186 us -> 184 us (0.989)
  Pallas kernels: 34.8 us -> 31.2 us
  waiting for transfers between devices: 69.7 us -> 72.1 us
  transfers between devices with their start and end apart: 17 -> 17, of which waited for: 6 -> 6; matrix products, arithmetic and copies ran while one was open for 7% -> 7% of each run, Pallas kernels for 13% -> 11%
where the time goes in v10:
time: 184 us
  waiting for transfers between devices  72.1 us (39%)
  starting transfers between devices  57.6 us (31%)
  Pallas kernels  31.2 us (17%)
  local copies, waits for them, and re-layouts  13.9 us (8%)
  other arithmetic  6.89 us (4%)
  between operations  2.31 us (1%)
    all_to_all x2, waiting for transfers between devices, in_plane(): return lax.all_to_all(parts, PLANE, split_axis=0, concat_axis=0, tiled=True)  46.5 us
    ppermute x14, starting transfers between devices, ring_shifted(): lax.ppermute(parts[k], 'dev_0', [(i, (i + k) % RING) for i in range(RING)])  27.5 us
    ppermute x14, waiting for transfers between devices, ring_shifted(): lax.ppermute(parts[k], 'dev_0', [(i, (i + k) % RING) for i in range(RING)])  25.6 us
    all_to_all x2, starting transfers between devices, in_plane(): return lax.all_to_all(parts, PLANE, split_axis=0, concat_axis=0, tiled=True)  16.2 us
    all_to_all x1, starting transfers between devices, local(): lax.all_to_all(message, GRP_DEV, split_axis=0, concat_axis=0, tiled=True)  13.9 us
    pallas_call x1, Pallas kernels, ring_placed(): pl.pallas_call(ring_place_kernel, out_shape=jax.ShapeDtypeStruct(half_don...  6.05 us
    pallas_call x1, Pallas kernels, placed_rows(): pl.pallas_call(place_kernel, out_shape=jax.ShapeDtypeStruct((shard_rows,...  5.8 us
    pallas_call x1, Pallas kernels, ring_repacked(): pl.pallas_call(ring_repack_kernel, out_shape=[jax.ShapeDtypeStruct((ROWS,...  5.8 us
  transfers between devices with their start and end apart: 17, of which 6 were waited for; matrix products, arithmetic and copies ran while one was open for 7% of the time, Pallas kernels for 11%

profile of v10, /device:TPU:1, one launch (start us, length us, event | category | flops | bytes accessed | tf_op | source)
XLA Modules:
  0.0 184.0 jit_solution(10471205984067169709)
XLA Ops:
  0.6 0.7 fusion.17
  1.4 0.8 add_select_fusion.4
  2.4 0.9 select_reduce_fusion.1
  3.3 0.3 convert_reduce_fusion.1
  3.6 4.2 %shard_map.105 = bf16[1024,2048]{1,0:T(8,128)(2,1)S(1)} custom-call(s32[1,512]{1,0:T(1,128)S(1)} %get-tuple-element.192.slot_ref, bf16[512,4096]{1,0:T(8,128)(2,1)} %bitcast.106), custom_call_target="tpu_custom_call" | custom-call | flops 2147483648 | bytes 6291456 | tf_op jit(solution)/shard_map/pallas_call | solution.py:48
  7.8 2.0 %copy-done = bf16[1024,2048]{1,0:T(8,128)(2,1)} copy-done((bf16[1024,2048]{1,0:T(8,128)(2,1)}, bf16[1024,2048]{1,0:T(8,128)(2,1)S(1)}, u32[]{:S(2)}) %copy-start) | copy-done | bytes 4194328
  9.8 8.6 %all-to-all-start.1 = ((bf16[32,32,2048]{2,1,0:T(8,128)(2,1)}), bf16[32,32,2048]{2,1,0:T(8,128)(2,1)}, u32[]{:S(2)}, u32[]{:S(2)}) async-start(bf16[32,32,2048]{2,1,0:T(8,128)(2,1)} %bitcast.95), calls=%async_computation.1 | async-start | bytes 8388608 | tf_op jit(solution)/shard_map/all_to_all | solution.py:361
  18.5 4.7 %shard_map.104 = (bf16[88,2048]{1,0:T(8,128)(2,1)S(1)}, bf16[88,2048]{1,0:T(8,128)(2,1)S(1)}, bf16[88,2048]{1,0:T(8,128)(2,1)}, bf16[88,2048]{1,0:T(8,128)(2,1)}...) custom-call(s32[1,512]{1,0:T(1,128)S(1)} %get-tuple-element.193.ring, ...), custom_call_target="tpu_custom_call" | custom-call | flops 1476395008 | bytes 4980736 | tf_op jit(solution)/shard_map/pallas_call | solution.py:100
  23.2 1.7 collective-permute-start
  24.9 4.0 %collective-permute-start.1 = (bf16[88,2048]{1,0:T(8,128)(2,1)S(1)}, bf16[88,2048]{1,0:T(8,128)(2,1)S(1)}, u32[]{:S(2)}, u32[]{:S(2)}) collective-permute-start(bf16[88,2048]{1,0:T(8,128)(2,1)S(1)} %get-tuple-element.87), channel_id=1, source_target_pairs={{0,56},{8,0},{16,8},{24,16},{32,24},{40,32},{48,40},{56,48},{1,57}... | collective-permute-start | bytes 1081352 | tf_op jit(solution)/shard_map/ppermute | solution.py:356
  28.9 3.5 %collective-permute-start.3 = (bf16[88,2048]{1,0:T(8,128)(2,1)}, bf16[88,2048]{1,0:T(8,128)(2,1)}, u32[]{:S(2)}, u32[]{:S(2)}) collective-permute-start(bf16[88,2048]{1,0:T(8,128)(2,1)} %get-tuple-element.94), channel_id=1, source_target_pairs={{0,24},{8,32},{16,40},{24,48},{32,56},{40,0},{48,8},{56,16},{1,25}... | collective-permute-start | bytes 1081352 | tf_op jit(solution)/shard_map/ppermute | solution.py:356
  32.3 0.9 collective-permute-start.4
  33.4 0.3 select_reduce_fusion
  33.7 0.7 and_reduce_fusion
  36.1 1.4 collective-permute-done.refs_1_
  37.5 2.7 %collective-permute-start.5 = (bf16[88,2048]{1,0:T(8,128)(2,1)S(1)}, bf16[88,2048]{1,0:T(8,128)(2,1)}, u32[]{:S(2)}, u32[]{:S(2)}) collective-permute-start(bf16[88,2048]{1,0:T(8,128)(2,1)S(1)} %get-tuple-element.96), channel_id=1, source_target_pairs={{0,40},{8,48},{16,56},{24,0},{32,8},{40,16},{48,24},{56,32},{1,41}... | collective-permute-start | bytes 1081352 | tf_op jit(solution)/shard_map/ppermute | solution.py:356
  40.1 15.8 %collective-permute-done.1.refs_7_ = bf16[88,2048]{1,0:T(8,128)(2,1)S(1)} collective-permute-done((bf16[88,2048]{1,0:T(8,128)(2,1)S(1)}, bf16[88,2048]{1,0:T(8,128)(2,1)S(1)}, u32[]{:S(2)}, u32[]{:S(2)}) %collective-permute-start.1) | collective-permute-done | bytes 360480 | tf_op jit(solution)/shard_map/ppermute | solution.py:356
  56.0 15.0 %all-to-all-done.1.rows_ref = bf16[32,32,2048]{2,1,0:T(8,128)(2,1)} async-done(((bf16[32,32,2048]{2,1,0:T(8,128)(2,1)}), bf16[32,32,2048]{2,1,0:T(8,128)(2,1)}, u32[]{:S(2)}, u32[]{:S(2)}) %all-to-all-start.1) | async-done | bytes 4194336 | tf_op jit(solution)/shard_map/all_to_all | solution.py:361
  70.9 5.8 %shard_map.106 = (bf16[88,2048]{1,0:T(8,128)(2,1)}, bf16[88,2048]{1,0:T(8,128)(2,1)S(1)}, bf16[88,2048]{1,0:T(8,128)(2,1)S(1)}, bf16[88,2048]{1,0:T(8,128)(2,1)S...) custom-call(s32[1]{0:T(128)} %bitcast.6.z_ref, ...), custom_call_target="tpu_custom_call" | custom-call | flops 2952790016 | bytes 7077888 | tf_op jit(solution)/shard_map/pallas_call | solution.py:186
  76.7 0.7 copy-done.1
  77.5 0.7 copy-done.2
  78.4 0.7 copy.93
  79.1 13.9 %all-to-all-start.2 = ((f32[256,1,128]{2,1,0:T(1,128)}), f32[256,1,128]{2,1,0:T(1,128)S(1)}, u32[]{:S(2)}, u32[]{:S(2)}) async-start(f32[256,1,128]{2,1,0:T(1,128)} %copy.93), calls=%async_computation.2 | async-start | bytes 262144 | tf_op jit(solution)/shard_map/all_to_all | solution.py:454
  93.0 1.6 collective-permute-start.7
  94.6 2.9 %collective-permute-start.8 = (bf16[88,2048]{1,0:T(8,128)(2,1)}, bf16[88,2048]{1,0:T(8,128)(2,1)}, u32[]{:S(2)}, u32[]{:S(2)}) collective-permute-start(bf16[88,2048]{1,0:T(8,128)(2,1)} %copy-done.1), channel_id=1, source_target_pairs={{0,56},{8,0},{16,8},{24,16},{32,24},{40,32},{48,40},{56,48},{1,57}... | collective-permute-start | bytes 1081352 | tf_op jit(solution)/shard_map/ppermute | solution.py:356
  97.6 1.0 copy-done.4
  98.5 4.6 %shard_map.107 = bf16[32,32,2048]{2,1,0:T(8,128)(2,1)} custom-call(s32[1]{0:T(128)} %bitcast.6.z_ref, bf16[88,2048]{1,0:T(8,128)(2,1)S(1)} %copy-done.4, bf16[88,2048]{1,0:T(8,128)(2,1)S(1)} %collective-permute-done.refs_1_, bf16[88,2048]{1,0:T(8,128)(2,1)} %collective-permute-done.2.refs_2_, bf16[88,2048]{1,0:T(8,128)(2,1)} %collective-permute-done.3.refs_3_, ...), custom_call_target="tpu_custom_call" | custom-call | flops 4294967296 | bytes 7077888 | tf_op jit(solution)/shard_map/pallas_call | solution.py:234
  103.2 4.5 %collective-permute-done.7 = bf16[88,2048]{1,0:T(8,128)(2,1)S(1)} collective-permute-done((bf16[88,2048]{1,0:T(8,128)(2,1)}, bf16[88,2048]{1,0:T(8,128)(2,1)S(1)}, u32[]{:S(2)}, u32[]{:S(2)}) %collective-permute-start.7) | collective-permute-done | bytes 360480 | tf_op jit(solution)/shard_map/ppermute | solution.py:356
  107.7 0.8 copy-done.6
  108.5 7.6 %all-to-all-start.3 = ((bf16[32,32,2048]{2,1,0:T(8,128)(2,1)}), bf16[32,32,2048]{2,1,0:T(8,128)(2,1)}, u32[]{:S(2)}, u32[]{:S(2)}) async-start(bf16[32,32,2048]{2,1,0:T(8,128)(2,1)} %shard_map.107), calls=%async_computation.3 | async-start | bytes 8388608 | tf_op jit(solution)/shard_map/all_to_all | solution.py:361
  116.2 3.0 %collective-permute-start.10 = (bf16[88,2048]{1,0:T(8,128)(2,1)S(1)}, bf16[88,2048]{1,0:T(8,128)(2,1)}, u32[]{:S(2)}, u32[]{:S(2)}) collective-permute-start(bf16[88,2048]{1,0:T(8,128)(2,1)S(1)} %get-tuple-element.103), channel_id=1, source_target_pairs={{0,24},{8,32},{16,40},{24,48},{32,56},{40,0},{48,8},{56,16},{1,25}... | collective-permute-start | bytes 1081352 | tf_op jit(solution)/shard_map/ppermute | solution.py:356
  119.2 0.9 collective-permute-start.11
  120.1 3.9 %collective-permute-start.12 = (bf16[88,2048]{1,0:T(8,128)(2,1)S(1)}, bf16[88,2048]{1,0:T(8,128)(2,1)}, u32[]{:S(2)}, u32[]{:S(2)}) collective-permute-start(bf16[88,2048]{1,0:T(8,128)(2,1)S(1)} %get-tuple-element.105), channel_id=1, source_target_pairs={{0,40},{8,48},{16,56},{24,0},{32,8},{40,16},{48,24},{56,32},{1,41}... | collective-permute-start | bytes 1081352 | tf_op jit(solution)/shard_map/ppermute | solution.py:356
  124.1 0.8 collective-permute-start.13
  124.9 1.5 collective-permute-start.9
  126.7 2.3 %gather_fusion = f32[512]{0:T(512)S(1)} fusion(f32[1024]{0:T(1024)S(1)} %reshape_reshape.6, s32[1024]{0:T(1024)S(1)} %pad_clamp_fusion.1), kind=kCustom, calls=%fused_computation | custom fusion | bytes 6144 | tf_op jit(solution)/shard_map/gather | solution.py:464
  129.0 2.3 %gather_fusion.1 = f32[512]{0:T(512)S(1)} fusion(f32[1024]{0:T(1024)S(1)} %reshape_reshape.6, s32[1024]{0:T(1024)S(1)} %pad_clamp_fusion), kind=kCustom, calls=%fused_computation.1 | custom fusion | bytes 6144 | tf_op jit(solution)/shard_map/gather | solution.py:464
  131.3 0.6 multiply_reduce_fusion
  132.0 0.3 copy.98
  132.9 0.4 slice_reduce_fusion.2
  133.6 0.5 add_add_fusion.1
  134.4 0.7 slice_reduce_fusion.4
  135.7 0.3 copy.96
  136.8 31.5 %all-to-all-done.3 = bf16[32,32,2048]{2,1,0:T(8,128)(2,1)} async-done(((bf16[32,32,2048]{2,1,0:T(8,128)(2,1)}), bf16[32,32,2048]{2,1,0:T(8,128)(2,1)}, u32[]{:S(2)}, u32[]{:S(2)}) %all-to-all-start.3) | async-done | bytes 4194336 | tf_op jit(solution)/shard_map/all_to_all | solution.py:361
  168.3 5.8 %shard_map.108 = bf16[501,4096]{1,0:T(8,128)(2,1)} custom-call(s32[1,1024]{1,0:T(1,128)S(1)} %reshape.445.target_ref, f32[1024,1]{1,0:T(8,128)S(1)} %reshape.474.scale_ref, bf16[1024,2048]{1,0:T(8,128)(2,1)} %bitcast.37.rows_ref), custom_call_target="tpu_custom_call" | custom-call | flops 2101346304 | bytes 6246400 | tf_op jit(solution)/shard_map/pallas_call | solution.py:265
  174.1 3.8 %collective-permute-done.13 = bf16[88,2048]{1,0:T(8,128)(2,1)} collective-permute-done((bf16[88,2048]{1,0:T(8,128)(2,1)S(1)}, bf16[88,2048]{1,0:T(8,128)(2,1)}, u32[]{:S(2)}, u32[]{:S(2)}) %collective-permute-start.13) | collective-permute-done | bytes 360480 | tf_op jit(solution)/shard_map/ppermute | solution.py:356
  177.9 6.1 %conditional.1 = (bf16[501,4096]{1,0:T(8,128)(2,1)}) conditional(s32[]{:T(128)} %convert_element_type.59, (s32[1]{0:T(128)}, f32[16,128]{1,0:T(8,128)S(1)}, bf16[88,2048]{1,0:T(8,128)(2,1)S(1)}, bf16[88,2048]{1,0:T(8,128)(2,1)S(1)}, bf16[88,2048]{1,0:T(8,128)(2,1)}, /*index=5*/bf16[88,2048]{1,0:T(8,128)(2,1)}, bf16[88,2048]{1,0:T(8,128)(2,1)}, ...), branch_computations={%region_9.10_spmd, %region_10.11_spmd} | conditional | flops 8497661952 | bytes 83836984 | solution.py:513
  178.0 6.1 %branch_0_fun.1 = bf16[501,4096]{1,0:T(8,128)(2,1)} custom-call(s32[1]{0:T(128)} %get-tuple-element.43.z_ref, f32[16,128]{1,0:T(8,128)S(1)} %get-tuple-element.44.table_ref, bf16[88,2048]{1,0:T(8,128)(2,1)S(1)} %get-tuple-element.45.refs_0_, bf16[88,2048]{1,0:T(8,128)(2,1)S(1)} %get-tuple-element.46.refs_1_, ...), custom_call_target="tpu_custom_call", output_to_operand_aliasing={{}: (10, {})} | custom-call | flops 2101346304 | bytes 4935680 | tf_op jit(solution)/shard_map/cond/branch_0_fun/pallas_call | solution.py:333
  (81 shorter events, 3.9 us)
Async XLA Ops:
  7.8 2.0 %copy-start = (bf16[1024,2048]{1,0:T(8,128)(2,1)}, bf16[1024,2048]{1,0:T(8,128)(2,1)S(1)}, u32[]{:S(2)}) copy-start(bf16[1024,2048]{1,0:T(8,128)(2,1)S(1)} %shard_map.105) | copy-start | bytes 12582916
  9.8 61.1 %all-to-all-start.1 = ((bf16[32,32,2048]{2,1,0:T(8,128)(2,1)}), bf16[32,32,2048]{2,1,0:T(8,128)(2,1)}, u32[]{:S(2)}, u32[]{:S(2)}) async-start(bf16[32,32,2048]{2,1,0:T(8,128)(2,1)} %bitcast.95), calls=%async_computation.1 | async-start | bytes 8388608 | tf_op jit(solution)/shard_map/all_to_all | solution.py:361
  18.4 14.8 %copy-start.8 = (bf16[4,4096]{1,0:T(4,128)(2,1)S(1)}, bf16[4,4096]{1,0:T(4,128)(2,1)}, u32[]{:S(2)}) copy-start(bf16[4,4096]{1,0:T(4,128)(2,1)} %param.13) | copy-start | bytes 98308
  18.5 15.3 %copy-start.11 = (s32[4]{0:T(128)S(1)}, s32[4]{0:T(128)}, u32[]{:S(2)}) copy-start(s32[4]{0:T(128)} %param.14) | copy-start | bytes 52
  18.5 17.3 %copy-start.9 = (f32[4096]{0:T(1024)S(1)}, f32[4096]{0:T(1024)}, u32[]{:S(2)}) copy-start(f32[4096]{0:T(1024)} %param.16) | copy-start | bytes 49156
  18.5 17.3 %copy-start.10 = (f32[4096]{0:T(1024)S(1)}, f32[4096]{0:T(1024)}, u32[]{:S(2)}) copy-start(f32[4096]{0:T(1024)} %param.15) | copy-start | bytes 49156
  23.2 47.7 %copy-start.3 = (bf16[88,2048]{1,0:T(8,128)(2,1)}, bf16[88,2048]{1,0:T(8,128)(2,1)S(1)}, u32[]{:S(2)}) copy-start(bf16[88,2048]{1,0:T(8,128)(2,1)S(1)} %get-tuple-element.91.refs_0_) | copy-start | bytes 1081348
  23.2 14.2 %collective-permute-start = (bf16[88,2048]{1,0:T(8,128)(2,1)S(1)}, bf16[88,2048]{1,0:T(8,128)(2,1)S(1)}, u32[]{:S(2)}, u32[]{:S(2)}) collective-permute-start(bf16[88,2048]{1,0:T(8,128)(2,1)S(1)} %get-tuple-element.86), channel_id=1, source_target_pairs={{0,8},{8,16},{16,24},{24,32},{32,40},{40,48},{48,56},{56,0},{1,9},... | collective-permute-start | bytes 1081352 | tf_op jit(solution)/shard_map/ppermute | solution.py:356
  24.9 31.1 %collective-permute-start.1 = (bf16[88,2048]{1,0:T(8,128)(2,1)S(1)}, bf16[88,2048]{1,0:T(8,128)(2,1)S(1)}, u32[]{:S(2)}, u32[]{:S(2)}) collective-permute-start(bf16[88,2048]{1,0:T(8,128)(2,1)S(1)} %get-tuple-element.87), channel_id=1, source_target_pairs={{0,56},{8,0},{16,8},{24,16},{32,24},{40,32},{48,40},{56,48},{1,57}... | collective-permute-start | bytes 1081352 | tf_op jit(solution)/shard_map/ppermute | solution.py:356
  28.9 64.1 %collective-permute-start.2 = (bf16[88,2048]{1,0:T(8,128)(2,1)}, bf16[88,2048]{1,0:T(8,128)(2,1)}, u32[]{:S(2)}, u32[]{:S(2)}) collective-permute-start(bf16[88,2048]{1,0:T(8,128)(2,1)} %get-tuple-element.93), channel_id=1, source_target_pairs={{0,16},{8,24},{16,32},{24,40},{32,48},{40,56},{48,0},{56,8},{1,17}... | collective-permute-start | bytes 1081352 | tf_op jit(solution)/shard_map/ppermute | solution.py:356
  28.9 65.7 %collective-permute-start.3 = (bf16[88,2048]{1,0:T(8,128)(2,1)}, bf16[88,2048]{1,0:T(8,128)(2,1)}, u32[]{:S(2)}, u32[]{:S(2)}) collective-permute-start(bf16[88,2048]{1,0:T(8,128)(2,1)} %get-tuple-element.94), channel_id=1, source_target_pairs={{0,24},{8,32},{16,40},{24,48},{32,56},{40,0},{48,8},{56,16},{1,25}... | collective-permute-start | bytes 1081352 | tf_op jit(solution)/shard_map/ppermute | solution.py:356
  32.3 65.2 %collective-permute-start.4 = (bf16[88,2048]{1,0:T(8,128)(2,1)}, bf16[88,2048]{1,0:T(8,128)(2,1)}, u32[]{:S(2)}, u32[]{:S(2)}) collective-permute-start(bf16[88,2048]{1,0:T(8,128)(2,1)} %get-tuple-element.95), channel_id=1, source_target_pairs={{0,32},{8,40},{16,48},{24,56},{32,0},{40,8},{48,16},{56,24},{1,33}... | collective-permute-start | bytes 1081352 | tf_op jit(solution)/shard_map/ppermute | solution.py:356
  37.5 60.1 %collective-permute-start.5 = (bf16[88,2048]{1,0:T(8,128)(2,1)S(1)}, bf16[88,2048]{1,0:T(8,128)(2,1)}, u32[]{:S(2)}, u32[]{:S(2)}) collective-permute-start(bf16[88,2048]{1,0:T(8,128)(2,1)S(1)} %get-tuple-element.96), channel_id=1, source_target_pairs={{0,40},{8,48},{16,56},{24,0},{32,8},{40,16},{48,24},{56,32},{1,41}... | collective-permute-start | bytes 1081352 | tf_op jit(solution)/shard_map/ppermute | solution.py:356
  56.0 41.6 %collective-permute-start.6 = (bf16[88,2048]{1,0:T(8,128)(2,1)S(1)}, bf16[88,2048]{1,0:T(8,128)(2,1)}, u32[]{:S(2)}, u32[]{:S(2)}) collective-permute-start(bf16[88,2048]{1,0:T(8,128)(2,1)S(1)} %get-tuple-element.97), channel_id=1, source_target_pairs={{0,48},{8,56},{16,0},{24,8},{32,16},{40,24},{48,32},{56,40},{1,49}... | collective-permute-start | bytes 1081352 | tf_op jit(solution)/shard_map/ppermute | solution.py:356
  76.7 0.7 copy-start.1
  77.5 0.7 copy-start.2
  79.1 29.4 %all-to-all-start.2 = ((f32[256,1,128]{2,1,0:T(1,128)}), f32[256,1,128]{2,1,0:T(1,128)S(1)}, u32[]{:S(2)}, u32[]{:S(2)}) async-start(f32[256,1,128]{2,1,0:T(1,128)} %copy.93), calls=%async_computation.2 | async-start | bytes 262144 | tf_op jit(solution)/shard_map/all_to_all | solution.py:454
  93.0 14.7 %collective-permute-start.7 = (bf16[88,2048]{1,0:T(8,128)(2,1)}, bf16[88,2048]{1,0:T(8,128)(2,1)S(1)}, u32[]{:S(2)}, u32[]{:S(2)}) collective-permute-start(bf16[88,2048]{1,0:T(8,128)(2,1)} %copy-done.2), channel_id=1, source_target_pairs={{0,8},{8,16},{16,24},{24,32},{32,40},{40,48},{48,56},{56,0},{1,9},... | collective-permute-start | bytes 1081352 | tf_op jit(solution)/shard_map/ppermute | solution.py:356
  94.6 13.9 %collective-permute-start.8 = (bf16[88,2048]{1,0:T(8,128)(2,1)}, bf16[88,2048]{1,0:T(8,128)(2,1)}, u32[]{:S(2)}, u32[]{:S(2)}) collective-permute-start(bf16[88,2048]{1,0:T(8,128)(2,1)} %copy-done.1), channel_id=1, source_target_pairs={{0,56},{8,0},{16,8},{24,16},{32,24},{40,32},{48,40},{56,48},{1,57}... | collective-permute-start | bytes 1081352 | tf_op jit(solution)/shard_map/ppermute | solution.py:356
  97.6 1.0 copy-start.4
  103.2 13.0 %copy-start.12 = (s32[512]{0:T(512)S(1)}, s32[512]{0:T(512)}, u32[]{:S(2)}) copy-start(s32[512]{0:T(512)} %param.17) | copy-start | bytes 6148
  103.2 13.0 %copy-start.13 = (s32[512]{0:T(512)S(1)}, s32[512]{0:T(512)}, u32[]{:S(2)}) copy-start(s32[512]{0:T(512)} %param.18) | copy-start | bytes 6148
  107.7 0.8 copy-start.6
  108.5 59.8 %all-to-all-start.3 = ((bf16[32,32,2048]{2,1,0:T(8,128)(2,1)}), bf16[32,32,2048]{2,1,0:T(8,128)(2,1)}, u32[]{:S(2)}, u32[]{:S(2)}) async-start(bf16[32,32,2048]{2,1,0:T(8,128)(2,1)} %shard_map.107), calls=%async_computation.3 | async-start | bytes 8388608 | tf_op jit(solution)/shard_map/all_to_all | solution.py:361
  116.2 57.9 %collective-permute-start.10 = (bf16[88,2048]{1,0:T(8,128)(2,1)S(1)}, bf16[88,2048]{1,0:T(8,128)(2,1)}, u32[]{:S(2)}, u32[]{:S(2)}) collective-permute-start(bf16[88,2048]{1,0:T(8,128)(2,1)S(1)} %get-tuple-element.103), channel_id=1, source_target_pairs={{0,24},{8,32},{16,40},{24,48},{32,56},{40,0},{48,8},{56,16},{1,25}... | collective-permute-start | bytes 1081352 | tf_op jit(solution)/shard_map/ppermute | solution.py:356
  119.2 54.9 %collective-permute-start.11 = (bf16[88,2048]{1,0:T(8,128)(2,1)S(1)}, bf16[88,2048]{1,0:T(8,128)(2,1)}, u32[]{:S(2)}, u32[]{:S(2)}) collective-permute-start(bf16[88,2048]{1,0:T(8,128)(2,1)S(1)} %get-tuple-element.104), channel_id=1, source_target_pairs={{0,32},{8,40},{16,48},{24,56},{32,0},{40,8},{48,16},{56,24},{1,33}... | collective-permute-start | bytes 1081352 | tf_op jit(solution)/shard_map/ppermute | solution.py:356
  120.1 54.0 %collective-permute-start.12 = (bf16[88,2048]{1,0:T(8,128)(2,1)S(1)}, bf16[88,2048]{1,0:T(8,128)(2,1)}, u32[]{:S(2)}, u32[]{:S(2)}) collective-permute-start(bf16[88,2048]{1,0:T(8,128)(2,1)S(1)} %get-tuple-element.105), channel_id=1, source_target_pairs={{0,40},{8,48},{16,56},{24,0},{32,8},{40,16},{48,24},{56,32},{1,41}... | collective-permute-start | bytes 1081352 | tf_op jit(solution)/shard_map/ppermute | solution.py:356
  124.1 53.9 %collective-permute-start.13 = (bf16[88,2048]{1,0:T(8,128)(2,1)S(1)}, bf16[88,2048]{1,0:T(8,128)(2,1)}, u32[]{:S(2)}, u32[]{:S(2)}) collective-permute-start(bf16[88,2048]{1,0:T(8,128)(2,1)S(1)} %get-tuple-element.106), channel_id=1, source_target_pairs={{0,48},{8,56},{16,0},{24,8},{32,16},{40,24},{48,32},{56,40},{1,49}... | collective-permute-start | bytes 1081352 | tf_op jit(solution)/shard_map/ppermute | solution.py:356
  124.9 53.0 %collective-permute-start.9 = (bf16[88,2048]{1,0:T(8,128)(2,1)S(1)}, bf16[88,2048]{1,0:T(8,128)(2,1)}, u32[]{:S(2)}, u32[]{:S(2)}) collective-permute-start(bf16[88,2048]{1,0:T(8,128)(2,1)S(1)} %get-tuple-element.102), channel_id=1, source_target_pairs={{0,16},{8,24},{16,32},{24,40},{32,48},{40,56},{48,0},{56,8},{1,17}... | collective-permute-start | bytes 1081352 | tf_op jit(solution)/shard_map/ppermute | solution.py:356
  168.3 9.7 %copy-start.5 = (bf16[88,2048]{1,0:T(8,128)(2,1)S(1)}, bf16[88,2048]{1,0:T(8,128)(2,1)}, u32[]{:S(2)}) copy-start(bf16[88,2048]{1,0:T(8,128)(2,1)} %get-tuple-element.90) | copy-start | bytes 1081348
  168.3 9.7 %copy-start.7 = (bf16[88,2048]{1,0:T(8,128)(2,1)S(1)}, bf16[88,2048]{1,0:T(8,128)(2,1)}, u32[]{:S(2)}) copy-start(bf16[88,2048]{1,0:T(8,128)(2,1)} %copy-done.6) | copy-start | bytes 1081348
